TPU v7x, 32 devices: a whole 2x2x4 slice. The times are simulated.
32 devices in a mesh: stream: 4 (over y, x), ctx: 4 (over z), head: 2 (over core).
Axes of the slice: x: 2, y: 2, z: 4, core: 2. Of those that a mesh axis runs over, the one named last changes fastest.
Arguments:
- tokens: bfloat16 [4, 1024, 2048], P('stream', 'ctx'), may hold values from -6 to 6
- doc_lengths: int32 [4, 6], P('stream'), may hold values from 1 to 512, 1024 in all within a row
- ln1_gain: bfloat16 [2048], replicated, may hold values from 0.25 to 1.75
- ln1_bias: bfloat16 [2048], replicated, may hold values from -1.5 to 1.5
- qkv_weight: bfloat16 [3, 2048, 2048], P(None, 'ctx', 'head'), may hold values from -0.125 to 0.125
- qkv_bias: bfloat16 [3, 2048], P(None, 'head'), may hold values from -0.5 to 0.5
- out_weight: bfloat16 [2048, 2048], P('head', 'ctx'), may hold values from -1 to 1
- out_bias: bfloat16 [2048], replicated, may hold values from -3 to 3
- ln2_gain: bfloat16 [2048], replicated, may hold values from 0.25 to 1.75
- ln2_bias: bfloat16 [2048], replicated, may hold values from -1.5 to 1.5
- up_weight: bfloat16 [2048, 8192], P('ctx', 'head'), may hold values from -0.125 to 0.125
- up_bias: bfloat16 [8192], P('head'), may hold values from -1.5 to 1.5
- down_weight: bfloat16 [8192, 2048], P('head', 'ctx'), may hold values from -0.0625 to 0.0625
- down_bias: bfloat16 [2048], replicated, may hold values from -3 to 3
- cotangent: bfloat16 [4, 1024, 2048], P('stream', 'ctx'), may hold values from -6 to 6
Outputs:
- output: bfloat16 [4, 1024, 2048], P('stream', 'ctx')
- input_grad: float32 [4, 1024, 2048], P('stream', 'ctx')
- ln1_gain_grad: float32 [2048], replicated
- ln1_bias_grad: float32 [2048], replicated
- qkv_weight_grad: float32 [3, 2048, 2048], P(None, 'ctx', 'head')
- qkv_bias_grad: float32 [3, 2048], P(None, 'head')
- out_weight_grad: float32 [2048, 2048], P('head', 'ctx')
- out_bias_grad: float32 [2048], replicated
- ln2_gain_grad: float32 [2048], replicated
- ln2_bias_grad: float32 [2048], replicated
- up_weight_grad: float32 [2048, 8192], P('ctx', 'head')
- up_bias_grad: float32 [8192], P('head')
- down_weight_grad: float32 [8192, 2048], P('head', 'ctx')
- down_bias_grad: float32 [2048], replicated
Inputs may be any that keep to these rules, and one draw needn't show every extreme that they name: `doc_lengths`: each sequence's 6 document lengths sum to 1024, the documents lie end to end in the given order, and the longest has exactly 512 tokens.
All inputs are finite; a program needn't handle non-finite values.
Results may differ from a plain program's by a relative error of at most 0.025.
Values may be sent and summed in bfloat16 or wider, within the bound.
A program may use at most 256 MiB of HBM per device.

v0:
```python
from functools import partial
import math

import jax
import jax.numpy as jnp
from jax import lax
from jax.sharding import PartitionSpec as P

HEAD = 256
ROT = 64


def layer_norm(values, gain, offset):
    centre = jnp.mean(values, axis=-1, keepdims=True)
    centred = values - centre
    spread = jnp.mean(centred * centred, axis=-1, keepdims=True)
    return centred * lax.rsqrt(spread + 1e-05) * gain + offset


def rotary(values, angles):
    half = angles.shape[-1]
    cosine = jnp.cos(angles)[:, None, :]
    sine = jnp.sin(angles)[:, None, :]
    first = values[..., :half]
    second = values[..., half : 2 * half]
    return jnp.concatenate(
        [first * cosine - second * sine, second * cosine + first * sine, values[..., 2 * half :]],
        axis=-1,
    )


def doc_starts(doc_sizes, positions):
    ends = jnp.cumsum(doc_sizes)
    starts = ends - doc_sizes
    return jnp.max(jnp.where(starts[None, :] <= positions[:, None], starts[None, :], 0), axis=1)


def per_device(
    tokens,
    doc_lengths,
    ln1_gain,
    ln1_bias,
    qkv_weight,
    qkv_bias,
    out_weight,
    out_bias,
    ln2_gain,
    ln2_bias,
    up_weight,
    up_bias,
    down_weight,
    down_bias,
    cotangent,
):
    inputs = tokens[0].astype(jnp.float32)
    count = inputs.shape[0]
    ctx_count = lax.axis_size("ctx")
    length = count * ctx_count
    positions = lax.axis_index("ctx") * count + jnp.arange(count, dtype=jnp.int32)
    starts = doc_starts(doc_lengths[0], positions)
    frequency = 10000.0 ** (-jnp.arange(0, ROT, 2, dtype=jnp.float32) / ROT)
    angles = (positions - starts).astype(jnp.float32)[:, None] * frequency[None, :]
    scale = HEAD ** (-0.5)
    full_qkv, full_out, full_up, full_down = (
        lax.all_gather(qkv_weight, "ctx", axis=1, tiled=True),
        lax.all_gather(out_weight, "ctx", axis=1, tiled=True),
        lax.all_gather(up_weight, "ctx", axis=0, tiled=True),
        lax.all_gather(down_weight, "ctx", axis=1, tiled=True),
    )
    gain_one = ln1_gain.astype(jnp.float32)
    offset_one = ln1_bias.astype(jnp.float32)
    gain_two = ln2_gain.astype(jnp.float32)
    offset_two = ln2_bias.astype(jnp.float32)
    low_one = layer_norm(inputs, gain_one, offset_one).astype(jnp.bfloat16)
    low_two = layer_norm(inputs, gain_two, offset_two).astype(jnp.bfloat16)
    projected = (
        jnp.einsum("nd,cde->cne", low_one, full_qkv, preferred_element_type=jnp.float32)
        + qkv_bias.astype(jnp.float32)[:, None, :]
    )
    width = projected.shape[2]
    local_heads = width // HEAD
    query = rotary(projected[0].reshape(count, local_heads, HEAD), angles).astype(jnp.bfloat16)
    keys_flat = (
        rotary(projected[1].reshape(count, local_heads, HEAD), angles)
        .reshape(count, width)
        .astype(jnp.bfloat16)
    )
    values_flat = projected[2].astype(jnp.bfloat16)
    all_keys, all_values = (
        lax.all_gather(keys_flat, "ctx", axis=0, tiled=True),
        lax.all_gather(values_flat, "ctx", axis=0, tiled=True),
    )
    block = math.gcd(length, 512)
    block_count = length // block
    key_blocks = all_keys.reshape(block_count, block, local_heads, HEAD)
    value_blocks = all_values.reshape(block_count, block, local_heads, HEAD)
    firsts = jnp.arange(block_count, dtype=jnp.int32) * block

    def block_scores(key_block, first):
        key_index = first + jnp.arange(block, dtype=jnp.int32)
        allowed = (key_index[None, :] <= positions[:, None]) & (
            key_index[None, :] >= starts[:, None]
        )
        scores = (
            jnp.einsum("qhe,khe->hqk", query, key_block, preferred_element_type=jnp.float32) * scale
        )
        return (jnp.where(allowed[None], scores, -1e30), allowed[None])

    def statistics(carry, item):
        running, norm_sum = carry
        key_block, first = item
        masked, allowed = block_scores(key_block, first)
        newest = jnp.maximum(running, jnp.max(masked, axis=-1))
        raised = jnp.where(allowed, jnp.exp(masked - newest[..., None]), 0.0)
        norm_sum = norm_sum * jnp.exp(running - newest) + jnp.sum(raised, axis=-1)
        return ((newest, norm_sum), None)

    initial = (
        jnp.full((local_heads, count), -1e30, jnp.float32),
        jnp.zeros((local_heads, count), jnp.float32),
    )
    (running, norm_sum), _ = lax.scan(statistics, initial, (key_blocks, firsts))
    log_norm = running + jnp.log(norm_sum)

    def share_block(key_block, first):
        masked, allowed = block_scores(key_block, first)
        return jnp.where(allowed, jnp.exp(masked - log_norm[..., None]), 0.0)

    def accumulate(mixed, item):
        key_block, value_block, first = item
        shares_low = share_block(key_block, first).astype(jnp.bfloat16)
        return (
            mixed
            + jnp.einsum(
                "hqk,khe->qhe", shares_low, value_block, preferred_element_type=jnp.float32
            ),
            None,
        )

    mixed, _ = lax.scan(
        accumulate,
        jnp.zeros((count, local_heads, HEAD), jnp.float32),
        (key_blocks, value_blocks, firsts),
    )
    mixed_low = mixed.reshape(count, width).astype(jnp.bfloat16)
    attention = jnp.dot(mixed_low, full_out, preferred_element_type=jnp.float32)
    hidden = jnp.dot(low_two, full_up, preferred_element_type=jnp.float32) + up_bias.astype(
        jnp.float32
    )
    activated = jax.nn.gelu(hidden, approximate=False).astype(jnp.bfloat16)
    branches = attention + jnp.dot(activated, full_down, preferred_element_type=jnp.float32)
    joint = lax.psum(branches.astype(jnp.bfloat16), "head").astype(jnp.float32)
    output = inputs + joint + out_bias.astype(jnp.float32) + down_bias.astype(jnp.float32)
    upstream = cotangent[0]
    down_grad = jnp.dot(activated.T, upstream, preferred_element_type=jnp.float32)
    activated_grad = jnp.dot(upstream, full_down.T, preferred_element_type=jnp.float32)
    _, gelu_back = jax.vjp(partial(jax.nn.gelu, approximate=False), hidden)
    hidden_grad = gelu_back(activated_grad)[0].astype(jnp.bfloat16)
    up_grad = jnp.dot(low_two.T, hidden_grad, preferred_element_type=jnp.float32)
    up_bias_grad = jnp.sum(hidden_grad.astype(jnp.float32), axis=0)
    normed_two_grad = jnp.dot(hidden_grad, full_up.T, preferred_element_type=jnp.float32)
    out_grad = jnp.dot(mixed_low.T, upstream, preferred_element_type=jnp.float32)
    mixed_grad = jnp.dot(upstream, full_out.T, preferred_element_type=jnp.float32).astype(
        jnp.bfloat16
    )
    mixed_grad_heads = mixed_grad.reshape(count, local_heads, HEAD)
    delta = jnp.sum(mixed_grad_heads.astype(jnp.float32) * mixed, axis=-1).T

    def backward_block(query_grad, item):
        key_block, value_block, first = item
        shares = share_block(key_block, first)
        share_grad = jnp.einsum(
            "qhe,khe->hqk", mixed_grad_heads, value_block, preferred_element_type=jnp.float32
        )
        score_grad = (shares * (share_grad - delta[..., None])).astype(jnp.bfloat16)
        query_grad = (
            query_grad
            + jnp.einsum("hqk,khe->qhe", score_grad, key_block, preferred_element_type=jnp.float32)
            * scale
        )
        key_grad = (
            jnp.einsum("hqk,qhe->khe", score_grad, query, preferred_element_type=jnp.float32)
            * scale
        )
        value_grad = jnp.einsum(
            "hqk,qhe->khe",
            shares.astype(jnp.bfloat16),
            mixed_grad_heads,
            preferred_element_type=jnp.float32,
        )
        return (
            query_grad,
            jnp.concatenate(
                [key_grad.reshape(block, width), value_grad.reshape(block, width)], axis=1
            ),
        )

    query_grad, key_terms = lax.scan(
        backward_block,
        jnp.zeros((count, local_heads, HEAD), jnp.float32),
        (key_blocks, value_blocks, firsts),
    )
    own_grads = lax.psum_scatter(
        key_terms.reshape(length, 2 * width).astype(jnp.bfloat16),
        "ctx",
        scatter_dimension=0,
        tiled=True,
    ).astype(jnp.float32)
    query_pre = rotary(query_grad, -angles).reshape(count, width)
    key_pre = rotary(own_grads[:, :width].reshape(count, local_heads, HEAD), -angles).reshape(
        count, width
    )
    projected_grad = jnp.stack([query_pre, key_pre, own_grads[:, width:]]).astype(jnp.bfloat16)
    qkv_grad = jnp.einsum(
        "nd,cne->cde", low_one, projected_grad, preferred_element_type=jnp.float32
    )
    qkv_bias_grad = jnp.sum(projected_grad.astype(jnp.float32), axis=1)
    normed_one_grad = jnp.einsum(
        "cne,cde->nd", projected_grad, full_qkv, preferred_element_type=jnp.float32
    )
    normed_one_grad, normed_two_grad = (
        lax.psum(normed_one_grad.astype(jnp.bfloat16), "head").astype(jnp.float32),
        lax.psum(normed_two_grad.astype(jnp.bfloat16), "head").astype(jnp.float32),
    )
    _, norm_back_one = jax.vjp(layer_norm, inputs, gain_one, offset_one)
    input_one, gain_grad_one, offset_grad_one = norm_back_one(normed_one_grad)
    _, norm_back_two = jax.vjp(layer_norm, inputs, gain_two, offset_two)
    input_two, gain_grad_two, offset_grad_two = norm_back_two(normed_two_grad)
    upstream_wide = upstream.astype(jnp.float32)
    input_grad = upstream_wide + input_one + input_two
    bias_grad = jnp.sum(upstream_wide, axis=0)
    small = lax.psum(
        (
            gain_grad_one,
            offset_grad_one,
            qkv_bias_grad,
            bias_grad,
            gain_grad_two,
            offset_grad_two,
            up_bias_grad,
        ),
        ("stream", "ctx"),
    )
    slices = (
        lax.psum_scatter(
            qkv_grad.astype(jnp.bfloat16), "ctx", scatter_dimension=1, tiled=True
        ).astype(jnp.float32),
        lax.psum_scatter(
            out_grad.astype(jnp.bfloat16), "ctx", scatter_dimension=1, tiled=True
        ).astype(jnp.float32),
        lax.psum_scatter(
            up_grad.astype(jnp.bfloat16), "ctx", scatter_dimension=0, tiled=True
        ).astype(jnp.float32),
        lax.psum_scatter(
            down_grad.astype(jnp.bfloat16), "ctx", scatter_dimension=1, tiled=True
        ).astype(jnp.float32),
    )
    shards = (
        lax.psum(slices[0].astype(jnp.bfloat16), "stream").astype(jnp.float32),
        lax.psum(slices[1].astype(jnp.bfloat16), "stream").astype(jnp.float32),
        lax.psum(slices[2].astype(jnp.bfloat16), "stream").astype(jnp.float32),
        lax.psum(slices[3].astype(jnp.bfloat16), "stream").astype(jnp.float32),
    )
    return (
        output.astype(jnp.bfloat16)[None],
        input_grad[None],
        small[0],
        small[1],
        shards[0],
        small[2],
        shards[1],
        small[3],
        small[4],
        small[5],
        shards[2],
        small[6],
        shards[3],
        small[3],
    )


def solution(mesh):
    in_specs = (
        P("stream", "ctx", None),
        P("stream", None),
        P(),
        P(),
        P(None, "ctx", "head"),
        P(None, "head"),
        P("head", "ctx"),
        P(),
        P(),
        P(),
        P("ctx", "head"),
        P("head"),
        P("head", "ctx"),
        P(),
        P("stream", "ctx", None),
    )
    out_specs = (
        P("stream", "ctx", None),
        P("stream", "ctx", None),
        P(),
        P(),
        P(None, "ctx", "head"),
        P(None, "head"),
        P("head", "ctx"),
        P(),
        P(),
        P(),
        P("ctx", "head"),
        P("head"),
        P("head", "ctx"),
        P(),
    )
    return jax.shard_map(
        per_device, mesh=mesh, in_specs=in_specs, out_specs=out_specs, check_vma=False
    )
```

profile of v0, /device:TPU:0, one launch (start us, length us, event | category | flops | bytes accessed | tf_op | source)
XLA Modules:
  0.0 2362.3 jit_solution(6158996267998633471)
XLA Ops:
  10.8 219.8 %all-gather.8.cloned.1.call-done = bf16[3,2048,1024]{2,1,0:T(8,128)(2,1)} async-done(((bf16[3,512,1024]{2,1,0:T(8,128)(2,1)}), bf16[3,2048,1024]{2,1,0:T(8,128)(2,1)}) %all-gather.8.cloned.1.call-update) | async-done | bytes 12582928 | tf_op jit(solution)/shard_map/all_gather | solution.py:65
  230.6 6.5 add_bitcast_fusion
  244.9 2.1 slice.108
  249.2 61.9 %all-gather.12.cloned.1.call-done = bf16[1024,2048]{1,0:T(8,128)(2,1)} async-done(((bf16[1024,512]{1,0:T(8,128)(2,1)}), bf16[1024,2048]{1,0:T(8,128)(2,1)}) %all-gather.12.cloned.1.call-update) | async-done | bytes 4194320 | tf_op jit(solution)/shard_map/all_gather | solution.py:66
  311.1 3.5 convolution_convert_fusion.4
  315.9 41.9 %all-gather.10.cloned.1.call-done = bf16[1024,1024]{1,0:T(8,128)(2,1)} async-done(((bf16[256,1024]{1,0:T(8,128)(2,1)}), bf16[1024,1024]{1,0:T(8,128)(2,1)}) %all-gather.10.cloned.1.call-update) | async-done | bytes 2097168 | tf_op jit(solution)/shard_map/all_gather | solution.py:90
  357.8 3.3 reshape.405
  362.7 41.8 %all-gather.18.cloned.1.call-done = bf16[1,1024,1024]{2,1,0:T(8,128)(2,1)} async-done(((bf16[1,256,1024]{2,1,0:T(8,128)(2,1)}), bf16[1,1024,1024]{2,1,0:T(8,128)(2,1)}) %all-gather.18.cloned.1.call-update) | async-done | bytes 2097168 | tf_op jit(solution)/shard_map/all_gather | solution.py:91
  404.5 4.5 reshape.404
  409.0 7.8 while.37
  416.8 14.8 while.38
  420.9 3.3 fusion.152
  428.1 3.5 fusion.152
  431.6 2.6 multiply_reduce_fusion
  434.3 29.0 %while.39 = (s32[]{:T(128)}, f32[256,4,256]{0,2,1:T(8,128)}, bf16[2,512,2048]{1,2,0:T(8,128)(2,1)}, bf16[2,512,4,256]{3,1,2,0:T(8,128)(2,1)}, s32[2]{0:T(128)S(1...) while((s32[]{:T(128)}, f32[256,4,256]{0,2,1:T(8,128)}, ...), condition=%wide.region_13.14_spmd.clone, body=%wide.region_12.13_spmd.clone.sunk | while | flops 1352794880 | bytes 31735028 | solution.py:198
  442.3 2.8 fusion.164
  456.7 3.1 fusion.164
  463.3 6.2 copy.113
  471.3 220.1 %all-gather.14.cloned.1.call-done = bf16[2048,4096]{1,0:T(8,128)(2,1)} async-done(((bf16[512,4096]{1,0:T(8,128)(2,1)}), bf16[2048,4096]{1,0:T(8,128)(2,1)}) %all-gather.14.cloned.1.call-update) | async-done | bytes 16777232 | tf_op jit(solution)/shard_map/all_gather | solution.py:67
  691.4 18.6 multiply_convert_fusion
  710.0 267.8 %all-gather.16.cloned.1.call-done = bf16[4096,2048]{1,0:T(8,128)(2,1)} async-done(((bf16[4096,512]{1,0:T(8,128)(2,1)}), bf16[4096,2048]{1,0:T(8,128)(2,1)}) %all-gather.16.cloned.1.call-update) | async-done | bytes 16777232 | tf_op jit(solution)/shard_map/all_gather | solution.py:68
  977.8 8.9 fusion.102
  986.7 2.2 fusion.63
  989.6 19.1 convert_reduce_fusion
  1008.7 12.0 convolution_convert_fusion.3
  1020.7 35.0 %reduce-scatter.6.cloned.1.call-done = bf16[256,2048]{1,0:T(8,128)(2,1)} async-done(((bf16[1024,2048]{1,0:T(8,128)(2,1)}), bf16[256,2048]{1,0:T(8,128)(2,1)}) %reduce-scatter.6.cloned.1.call-update) | async-done | bytes 1048592 | tf_op jit(solution)/shard_map/reduce_scatter | solution.py:203
  1055.7 2.2 fusion.100
  1069.3 2.9 pad_maximum_fusion.4
  1072.2 2.2 stack_reshape.9
  1074.4 9.3 fusion.64
  1083.8 3.3 convolution_convert_fusion.2
  1088.2 8.0 convert_bitcast_fusion
  1096.2 11.0 convolution_convert_fusion.1
  1107.3 9.8 convolution_convert_fusion
  1117.9 2.1 convert_reduce_fusion.1
  1119.9 3.4 fusion.72
  1123.3 4.1 fusion.80
  1127.4 4.3 convert_reduce_fusion.4
  1131.7 56.9 %reduce-scatter.10.cloned.1.call-done = bf16[1024,512]{1,0:T(8,128)(2,1)} async-done(((bf16[1024,2048]{1,0:T(8,128)(2,1)}), bf16[1024,512]{1,0:T(8,128)(2,1)}) %reduce-scatter.10.cloned.1.call-update) | async-done | bytes 1048592 | tf_op jit(solution)/shard_map/reduce_scatter | solution.py:248
  1188.6 214.7 %reduce-scatter.8.cloned.1.call-done = bf16[3,512,1024]{1,2,0:T(8,128)(2,1)} async-done(((bf16[3,2048,1024]{1,2,0:T(8,128)(2,1)}), bf16[3,512,1024]{1,2,0:T(8,128)(2,1)}) %reduce-scatter.8.cloned.1.call-update) | async-done | bytes 3145744 | tf_op jit(solution)/shard_map/reduce_scatter | solution.py:245
  1403.3 283.9 %reduce-scatter.12.cloned.1.call-done = bf16[512,4096]{1,0:T(8,128)(2,1)} async-done(((bf16[2048,4096]{1,0:T(8,128)(2,1)}), bf16[512,4096]{1,0:T(8,128)(2,1)}) %reduce-scatter.12.cloned.1.call-update) | async-done | bytes 4194320 | tf_op jit(solution)/shard_map/reduce_scatter | solution.py:251
  1687.2 283.3 %reduce-scatter.14.cloned.1.call-done = bf16[4096,512]{1,0:T(8,128)(2,1)} async-done(((bf16[4096,2048]{1,0:T(8,128)(2,1)}), bf16[4096,512]{1,0:T(8,128)(2,1)}) %reduce-scatter.14.cloned.1.call-update) | async-done | bytes 4194320 | tf_op jit(solution)/shard_map/reduce_scatter | solution.py:254
  1970.5 116.1 %all-reduce.7.cloned.1.call-done = (f32[2048]{0:T(1024)}, f32[2048]{0:T(1024)}, f32[3,1024]{1,0:T(4,128)}, f32[2048]{0:T(1024)}, f32[2048]{0:T(1024)}, /*index=5*/f32[2048]{0:T(1024)}, f32[4096]{0:T(1024)}) async-done(((f32[2048]{0:T(1024)}, f32[2048]{0:T(1024)}, f32[3,1024]{1,0:T(4,128)}, f32[2048]{0:T(1024)}, f32[2048]{0:T(1024)}, /*index=5*/f32[2048]{0:T(1024)}, f32[4096]{0:T(1024)}), (f32[2048]{0:T(1024)}, ...) | async-done | bytes 69648 | tf_op jit(solution)/shard_map/psum | solution.py:232
  2086.5 245.9 %all-reduce.9.cloned.1.call-done = (bf16[3,512,1024]{1,2,0:T(8,128)(2,1)}, bf16[1024,512]{1,0:T(8,128)(2,1)}, bf16[512,4096]{1,0:T(8,128)(2,1)}, bf16[4096,512]{1,0:T(8,128)(2,1)}) async-done(((bf16[3,512,1024]{1,2,0:T(8,128)(2,1)}, bf16[1024,512]{1,0:T(8,128)(2,1)}, bf16[512,4096]{1,0:T(8,128)(2,1)}, bf16[4096,512]{1,0:T(8,128)(2,1)}), (bf16[3,512,1024]{1,2,0:T(8,128)(2,1)}, bf16[1024,512]{1,0:T(8,128)(2,1)}, ...) | async-done | bytes 12582928 | tf_op jit(solution)/shard_map/psum | solution.py:259
  2332.5 3.0 convert_element_type.189
  2335.5 3.8 copy.118
  2339.2 6.8 convert_element_type.191
  2346.1 4.6 convert_element_type.194
  (239 shorter events, 75.4 us)
Async XLA Ops:
  7.2 1.9 copy-start
  7.2 223.3 %all-gather.8.cloned.1.call-start = ((), (), s32[]{:S(2)}) async-start(), calls=%async_computation.5 | async-start | bytes 15728640 | tf_op jit(solution)/shard_map/all_gather | solution.py:65
  8.0 303.2 %all-gather.12.cloned.1.call-start = ((), (), s32[]{:S(2)}) async-start(), calls=%async_computation.7 | async-start | bytes 5242880 | tf_op jit(solution)/shard_map/all_gather | solution.py:66
  8.7 349.1 %all-gather.10.cloned.1.call-start = ((), (), s32[]{:S(2)}) async-start(), calls=%async_computation.6 | async-start | bytes 2621440 | tf_op jit(solution)/shard_map/all_gather | solution.py:90
  8.8 221.8 %copy-start.14 = (f32[2048]{0:T(1024)}, f32[2048]{0:T(1024)S(1)}, u32[]{:S(2)}) copy-start(f32[2048]{0:T(1024)S(1)} %convert_element_type.155) | copy-start | bytes 24580
  8.8 221.8 %copy-start.30 = (f32[2048]{0:T(1024)}, f32[2048]{0:T(1024)S(1)}, u32[]{:S(2)}) copy-start(f32[2048]{0:T(1024)S(1)} %convert_element_type.156) | copy-start | bytes 24580
  9.4 221.2 %copy-start.16 = (f32[256]{0:T(256)}, f32[256]{0:T(256)S(1)}, u32[]{:S(2)}) copy-start(f32[256]{0:T(256)S(1)} %broadcast_multiply_fusion) | copy-start | bytes 3076
  9.8 220.8 %copy-start.26 = (f32[256]{0:T(256)}, f32[256]{0:T(256)S(1)}, u32[]{:S(2)}) copy-start(f32[256]{0:T(256)S(1)} %fusion.71) | copy-start | bytes 3076
  9.9 220.7 %copy-start.20 = (f32[256]{0:T(256)}, f32[256]{0:T(256)S(1)}, u32[]{:S(2)}) copy-start(f32[256]{0:T(256)S(1)} %fusion.94) | copy-start | bytes 3076
  244.9 159.6 %all-gather.18.cloned.1.call-start = ((), (), s32[]{:S(2)}) async-start(), calls=%async_computation.15 | async-start | bytes 2621440 | tf_op jit(solution)/shard_map/all_gather | solution.py:91
  247.1 64.0 %copy-start.6 = (bf16[1,256,2048]{2,1,0:T(8,128)(2,1)S(1)}, bf16[1,256,2048]{2,1,0:T(8,128)(2,1)}, u32[]{:S(2)}) copy-start(bf16[1,256,2048]{2,1,0:T(8,128)(2,1)} %param.35) | copy-start | bytes 3145732
  247.1 444.3 %all-gather.14.cloned.1.call-start = ((), (), s32[]{:S(2)}) async-start(), calls=%async_computation.8 | async-start | bytes 20971520 | tf_op jit(solution)/shard_map/all_gather | solution.py:67
  247.7 730.1 %all-gather.16.cloned.1.call-start = ((), (), s32[]{:S(2)}) async-start(), calls=%async_computation.9 | async-start | bytes 20971520 | tf_op jit(solution)/shard_map/all_gather | solution.py:68
  248.3 807.4 %reduce-scatter.6.cloned.1.call-start = ((), (), s32[]{:S(2)}) async-start(), calls=%async_computation.10 | async-start | bytes 5242880 | tf_op jit(solution)/shard_map/reduce_scatter | solution.py:203
  434.3 6.5 copy-start.2
  448.7 6.5 copy-start.2
  469.5 221.9 %copy-start.1 = (bf16[1,256,2048]{2,1,0:T(8,128)(2,1)S(1)}, bf16[1,256,2048]{2,1,0:T(8,128)(2,1)}, u32[]{:S(2)}) copy-start(bf16[1,256,2048]{2,1,0:T(8,128)(2,1)} %param.21) | copy-start | bytes 3145732
  469.5 221.9 %copy-start.17 = (f32[256]{0:T(256)S(1)}, f32[256]{0:T(256)}, u32[]{:S(2)}) copy-start(f32[256]{0:T(256)} %copy-done.16) | copy-start | bytes 3076
  469.5 221.9 %copy-start.21 = (f32[256]{0:T(256)S(1)}, f32[256]{0:T(256)}, u32[]{:S(2)}) copy-start(f32[256]{0:T(256)} %copy-done.20) | copy-start | bytes 3076
  469.5 221.9 %copy-start.23 = (f32[4096]{0:T(1024)S(1)}, f32[4096]{0:T(1024)}, u32[]{:S(2)}) copy-start(f32[4096]{0:T(1024)} %convert_element_type.167) | copy-start | bytes 49156
  470.9 649.1 %all-reduce.11.cloned.1.call-start = ((), (), s32[]{:S(2)}) async-start(), calls=%async_computation.18 | async-start | bytes 6291456 | tf_op jit(solution)/shard_map/psum | solution.py:152
  977.8 8.9 copy-start.9
  977.8 8.9 copy-start.42
  986.7 2.3 copy-start.7
  986.7 2.9 copy-start.44
  1083.7 3.5 copy-start.15
  1083.8 3.5 copy-start.18
  1083.8 3.5 copy-start.22
  1083.8 3.4 copy-start.31
  1083.8 104.8 %reduce-scatter.10.cloned.1.call-start = ((), (), s32[]{:S(2)}) async-start(), calls=%async_computation.12 | async-start | bytes 5242880 | tf_op jit(solution)/shard_map/reduce_scatter | solution.py:248
  1087.1 316.2 %reduce-scatter.8.cloned.1.call-start = ((), (), s32[]{:S(2)}) async-start(), calls=%async_computation.11 | async-start | bytes 15728640 | tf_op jit(solution)/shard_map/reduce_scatter | solution.py:245
  1096.2 591.0 %reduce-scatter.12.cloned.1.call-start = ((), (), s32[]{:S(2)}) async-start(), calls=%async_computation.13 | async-start | bytes 20971520 | tf_op jit(solution)/shard_map/reduce_scatter | solution.py:251
  1107.3 863.1 %reduce-scatter.14.cloned.1.call-start = ((), (), s32[]{:S(2)}) async-start(), calls=%async_computation.14 | async-start | bytes 20971520 | tf_op jit(solution)/shard_map/reduce_scatter | solution.py:254
  1117.2 6.1 copy-start.27
  1117.2 969.4 %all-reduce.7.cloned.1.call-start = ((), (), s32[]{:S(2)}) async-start(), calls=%async_computation.16 | async-start | bytes 147456 | tf_op jit(solution)/shard_map/psum | solution.py:232
  1119.9 7.5 copy-start.4
  1119.9 7.5 copy-start.5
  1119.9 7.5 copy-start.13
  1131.7 1200.8 %all-reduce.9.cloned.1.call-start = ((), (), s32[]{:S(2)}) async-start(), calls=%async_computation.17 | async-start | bytes 25165824 | tf_op jit(solution)/shard_map/psum | solution.py:259
  2332.5 3.0 copy-start.10
  2339.2 6.8 copy-start.8
  2346.1 4.7 copy-start.19
  2346.1 5.3 copy-start.35
  2346.1 5.9 copy-start.34
  2346.1 6.5 copy-start.25
  2346.1 7.6 copy-start.33
  2346.1 8.2 copy-start.32
  2346.1 8.8 copy-start.24
  (13 other events, 18.0 us)
Sparse Core Ops, SparseCore 0:
  9.6 220.8 all-gather.7
  232.1 78.9 all-gather.11
  313.3 44.4 all-gather.9
  359.8 44.6 all-gather.17
  405.9 285.4 all-gather.13
  692.8 284.9 all-gather.15
  980.7 74.9 reduce-scatter.5
  1083.9 23.8 all-reduce.10
  1110.6 77.9 reduce-scatter.9
  1190.9 212.3 reduce-scatter.7
  1405.8 281.3 reduce-scatter.11
  1689.4 281.0 reduce-scatter.13
  1979.1 107.3 all-reduce.6
  2090.8 241.6 all-reduce.8
where the time goes:
time: 2370 us; the launch traced here: 2360 us
  waiting for transfers between devices  2090 us (88%)
  matrix products  142 us (6%)
  local copies, waits for them, and re-layouts  63.1 us (3%)
  other arithmetic  49.8 us (2%)
    reduce_scatter x1, waiting for transfers between devices, per_device(): lax.psum_scatter(up_grad.astype(jnp.bfloat16), 'ctx', scatter_dimension=0...  284 us
    reduce_scatter x1, waiting for transfers between devices, per_device(): lax.psum_scatter(down_grad.astype(jnp.bfloat16), 'ctx', scatter_dimension...  283 us
    all_gather x1, waiting for transfers between devices, per_device(): lax.all_gather(down_weight, 'ctx', axis=1, tiled=True)  268 us
    psum x1, waiting for transfers between devices, per_device(): lax.psum(slices[0].astype(jnp.bfloat16), 'stream').astype(jnp.float32)  246 us
    all_gather x1, waiting for transfers between devices, per_device(): lax.all_gather(up_weight, 'ctx', axis=0, tiled=True)  220 us
    all_gather x1, waiting for transfers between devices, per_device(): lax.all_gather(qkv_weight, 'ctx', axis=1, tiled=True)  220 us
    reduce_scatter x1, waiting for transfers between devices, per_device(): lax.psum_scatter(qkv_grad.astype(jnp.bfloat16), 'ctx', scatter_dimension=...  215 us
    psum x1, waiting for transfers between devices, per_device(): lax.psum((gain_grad_one, offset_grad_one, qkv_bias_grad, bias_grad, gain_...  116 us
  transfers between devices with their start and end apart: 14, of which 13 were waited for; matrix products, arithmetic and copies ran while one was open for 8% of the time, Pallas kernels for 0%

commit v1 on v0

--- a/solution.py
+++ b/solution.py
@@ -30,12 +30,13 @@
 
 
 def doc_starts(doc_sizes, positions):
-    ends = jnp.cumsum(doc_sizes)
-    starts = ends - doc_sizes
+    place = jnp.arange(doc_sizes.shape[0])
+    before = place[None, :] < place[:, None]
+    starts = jnp.sum(jnp.where(before, doc_sizes[None, :], 0), axis=1)
     return jnp.max(jnp.where(starts[None, :] <= positions[:, None], starts[None, :], 0), axis=1)
 
 
-def per_device(
+def general_device(
     tokens,
     doc_lengths,
     ln1_gain,
@@ -279,6 +280,204 @@
     )
 
 
+def token_places(doc_sizes, length):
+    positions = jnp.arange(length, dtype=jnp.int32)
+    return positions, doc_starts(doc_sizes, positions)
+
+
+def regroup(piece, axis):
+    return lax.all_to_all(piece, "ctx", split_axis=0, concat_axis=axis, tiled=False)
+
+
+def per_device(
+    tokens,
+    doc_lengths,
+    ln1_gain,
+    ln1_bias,
+    qkv_weight,
+    qkv_bias,
+    out_weight,
+    out_bias,
+    ln2_gain,
+    ln2_bias,
+    up_weight,
+    up_bias,
+    down_weight,
+    down_bias,
+    cotangent,
+):
+    f32, bf16 = jnp.float32, jnp.bfloat16
+    ctx_count, stream_count = lax.axis_size("ctx"), lax.axis_size("stream")
+    head_count = lax.axis_size("head")
+    c = lax.axis_index("ctx")
+    h = lax.axis_index("head")
+    count, model = tokens.shape[1], tokens.shape[2]
+    length = count * ctx_count
+    slab = model // ctx_count
+    width = qkv_weight.shape[2] // ctx_count
+    units = up_weight.shape[1] // ctx_count
+
+    all_tokens = lax.all_gather(tokens[0], "ctx", axis=0, tiled=True)
+    upstream = lax.all_gather(cotangent[0], "ctx", axis=0, tiled=True)
+    w_qkv = regroup(
+        qkv_weight.reshape(3, slab, ctx_count, width).transpose(2, 0, 1, 3), 1
+    ).reshape(3, model, width)
+    w_up = regroup(up_weight.reshape(slab, ctx_count, units).transpose(1, 0, 2), 0).reshape(
+        model, units
+    )
+    w_out = regroup(out_weight.reshape(ctx_count, width, slab), 1).reshape(width, model)
+    w_down = regroup(down_weight.reshape(ctx_count, units, slab), 1).reshape(units, model)
+
+    gain_one, offset_one = ln1_gain.astype(f32), ln1_bias.astype(f32)
+    gain_two, offset_two = ln2_gain.astype(f32), ln2_bias.astype(f32)
+    wide = all_tokens.astype(f32)
+    centred = wide - jnp.mean(wide, axis=-1, keepdims=True)
+    scale_of = lax.rsqrt(jnp.mean(centred * centred, axis=-1, keepdims=True) + 1e-05)
+    unit = centred * scale_of
+    low_one = (unit * gain_one + offset_one).astype(bf16)
+    low_two = (unit * gain_two + offset_two).astype(bf16)
+
+    positions, starts = token_places(doc_lengths[0], length)
+    frequency = 10000.0 ** (-jnp.arange(0, ROT, 2, dtype=f32) / ROT)
+    angles = (positions - starts).astype(f32)[:, None] * frequency[None, :]
+    bias = lax.dynamic_slice_in_dim(qkv_bias, c * width, width, 1).astype(f32)
+    projected = jnp.einsum("nd,cde->cne", low_one, w_qkv, preferred_element_type=f32)
+    projected = projected + bias[:, None, :]
+    heads = width // HEAD
+    query = rotary(projected[0].reshape(length, heads, HEAD), angles).astype(bf16)
+    keys = rotary(projected[1].reshape(length, heads, HEAD), angles).astype(bf16)
+    values = projected[2].reshape(length, heads, HEAD).astype(bf16)
+    scale = HEAD ** (-0.5)
+    allowed = (positions[None, :] <= positions[:, None]) & (positions[None, :] >= starts[:, None])
+    scores = jnp.einsum("qhe,khe->hqk", query, keys, preferred_element_type=f32) * scale
+    masked = jnp.where(allowed[None], scores, -1e30)
+    raised = jnp.where(
+        allowed[None], jnp.exp(masked - jnp.max(masked, axis=-1, keepdims=True)), 0.0
+    )
+    shares = raised / jnp.sum(raised, axis=-1, keepdims=True)
+    shares_low = shares.astype(bf16)
+    mixed = jnp.einsum("hqk,khe->qhe", shares_low, values, preferred_element_type=f32)
+    mixed_low = mixed.reshape(length, width).astype(bf16)
+
+    up_part = lax.dynamic_slice_in_dim(up_bias, c * units, units, 0).astype(f32)
+    hidden = jnp.dot(low_two, w_up, preferred_element_type=f32) + up_part
+    activated = jax.nn.gelu(hidden, approximate=False).astype(bf16)
+    branches = jnp.dot(mixed_low, w_out, preferred_element_type=f32) + jnp.dot(
+        activated, w_down, preferred_element_type=f32
+    )
+
+    _, gelu_back = jax.vjp(partial(jax.nn.gelu, approximate=False), hidden)
+    activated_grad = jnp.dot(upstream, w_down.T, preferred_element_type=f32)
+    hidden_grad = gelu_back(activated_grad)[0].astype(bf16)
+    down_grad = jnp.dot(activated.T, upstream, preferred_element_type=f32)
+    up_grad = jnp.dot(low_two.T, hidden_grad, preferred_element_type=f32)
+    out_grad = jnp.dot(mixed_low.T, upstream, preferred_element_type=f32)
+    mixed_grad = (
+        jnp.dot(upstream, w_out.T, preferred_element_type=f32)
+        .astype(bf16)
+        .reshape(length, heads, HEAD)
+    )
+    delta = jnp.sum(mixed_grad.astype(f32) * mixed, axis=-1).T
+    share_grad = jnp.einsum("qhe,khe->hqk", mixed_grad, values, preferred_element_type=f32)
+    score_grad = (shares * (share_grad - delta[..., None])).astype(bf16)
+    query_grad = (
+        jnp.einsum("hqk,khe->qhe", score_grad, keys, preferred_element_type=f32) * scale
+    )
+    key_grad = jnp.einsum("hqk,qhe->khe", score_grad, query, preferred_element_type=f32) * scale
+    value_grad = jnp.einsum("hqk,qhe->khe", shares_low, mixed_grad, preferred_element_type=f32)
+    projected_grad = jnp.stack(
+        [
+            rotary(query_grad, -angles).reshape(length, width),
+            rotary(key_grad, -angles).reshape(length, width),
+            value_grad.reshape(length, width),
+        ]
+    ).astype(bf16)
+    qkv_grad = jnp.einsum("nd,cne->cde", low_one, projected_grad, preferred_element_type=f32)
+    normed_one_grad = jnp.einsum("cne,cde->nd", projected_grad, w_qkv, preferred_element_type=f32)
+    normed_two_grad = jnp.dot(hidden_grad, w_up.T, preferred_element_type=f32)
+
+    joint = lax.psum(
+        lax.psum_scatter(branches.astype(bf16), "ctx", scatter_dimension=0, tiled=True), "head"
+    ).astype(f32)
+    inward = gain_one * normed_one_grad + gain_two * normed_two_grad
+    inward = lax.psum(
+        lax.psum_scatter(inward.astype(bf16), "ctx", scatter_dimension=0, tiled=True), "head"
+    ).astype(f32)
+
+    own = tokens[0].astype(f32)
+    own_upstream = cotangent[0].astype(f32)
+    output = own + joint + out_bias.astype(f32) + down_bias.astype(f32)
+    own_centred = own - jnp.mean(own, axis=-1, keepdims=True)
+    own_scale = lax.rsqrt(jnp.mean(own_centred * own_centred, axis=-1, keepdims=True) + 1e-05)
+    own_unit = own_centred * own_scale
+    input_grad = own_upstream + own_scale * (
+        inward
+        - jnp.mean(inward, axis=-1, keepdims=True)
+        - own_unit * jnp.mean(inward * own_unit, axis=-1, keepdims=True)
+    )
+
+    bias_grad = jnp.sum(own_upstream, axis=0) * (1.0 / head_count)
+    qkv_small = lax.dynamic_update_slice(
+        jnp.zeros((3, head_count * ctx_count * width), f32),
+        jnp.sum(projected_grad.astype(f32), axis=1),
+        (0, (h * ctx_count + c) * width),
+    )
+    up_small = lax.dynamic_update_slice(
+        jnp.zeros((head_count * ctx_count * units,), f32),
+        jnp.sum(hidden_grad.astype(f32), axis=0),
+        ((h * ctx_count + c) * units,),
+    )
+    small = lax.psum(
+        (
+            jnp.sum(normed_one_grad * unit, axis=0),
+            jnp.sum(normed_one_grad, axis=0),
+            qkv_small,
+            bias_grad,
+            jnp.sum(normed_two_grad * unit, axis=0),
+            jnp.sum(normed_two_grad, axis=0),
+            up_small,
+        ),
+        ("stream", "ctx", "head"),
+    )
+    qkv_bias_grad = lax.dynamic_slice_in_dim(small[2], h * ctx_count * width, ctx_count * width, 1)
+    up_bias_grad = lax.dynamic_slice_in_dim(small[6], h * ctx_count * units, ctx_count * units, 0)
+
+    def settle(grad):
+        part = lax.psum_scatter(
+            grad.astype(bf16), "stream", scatter_dimension=1, tiled=True
+        )[:, 0]
+        part = lax.all_to_all(part, "ctx", split_axis=0, concat_axis=0, tiled=True)
+        return lax.all_gather(part, "stream", axis=1, tiled=False)
+
+    n, k = ctx_count, stream_count
+    qkv_out = settle(
+        qkv_grad.reshape(3, n, k, slab // k, width).transpose(1, 2, 0, 3, 4)
+    )
+    qkv_out = qkv_out.transpose(2, 1, 3, 0, 4).reshape(3, slab, n * width)
+    up_out = settle(up_grad.reshape(n, k, slab // k, units))
+    up_out = up_out.transpose(1, 2, 0, 3).reshape(slab, n * units)
+    out_out = settle(out_grad.reshape(k, width // k, n, slab).transpose(2, 0, 1, 3))
+    out_out = out_out.reshape(n * width, slab)
+    down_out = settle(down_grad.reshape(k, units // k, n, slab).transpose(2, 0, 1, 3))
+    down_out = down_out.reshape(n * units, slab)
+    return (
+        output.astype(bf16)[None],
+        input_grad[None],
+        small[0],
+        small[1],
+        qkv_out.astype(f32),
+        qkv_bias_grad,
+        out_out.astype(f32),
+        small[3],
+        small[4],
+        small[5],
+        up_out.astype(f32),
+        up_bias_grad,
+        down_out.astype(f32),
+        small[3],
+    )
+
+
 def solution(mesh):
     in_specs = (
         P("stream", "ctx", None),
@@ -313,6 +512,17 @@
         P("head", "ctx"),
         P(),
     )
-    return jax.shard_map(
-        per_device, mesh=mesh, in_specs=in_specs, out_specs=out_specs, check_vma=False
-    )
+    split = mesh.shape["ctx"] * mesh.shape["head"]
+
+    def whole(*arrays):
+        heads, units = arrays[4].shape[2] // HEAD, arrays[10].shape[1]
+        fits = heads % split == 0 and units % (split * 128 * mesh.shape["stream"]) == 0
+        return jax.shard_map(
+            per_device if fits else general_device,
+            mesh=mesh,
+            in_specs=in_specs,
+            out_specs=out_specs,
+            check_vma=False,
+        )(*arrays)
+
+    return whole

time: 2370 us -> 1230 us (0.52)
  waiting for transfers between devices: 2090 us -> 812 us
  blocking collectives: 0 us -> 86 us
  local copies, waits for them, and re-layouts: 63.1 us -> 134 us
  matrix products: 142 us -> 109 us
  starting transfers between devices: 1.15 us -> 27.8 us
    reduce_scatter x5 -> x2, waiting for transfers between devices: 874 us -> 78.3 us  [the longest x1 78.2 us: per_device(): lax.psum_scatter(branches.astype(bf16), 'ctx', scatter_dimension=0, tiled...]
    all_gather x6, waiting for transfers between devices: 853 us -> 125 us  [the longest x4 125 us: settle(): return lax.all_gather(part, 'stream', axis=1, tiled=False)]
    all_to_all x0 -> x5, waiting for transfers between devices: none -> 332 us  [the longest x4 321 us: regroup(): lax.all_to_all(piece, 'ctx', split_axis=0, concat_axis=axis, tiled=False)]
    psum x3 -> x2, waiting for transfers between devices: 362 us -> 121 us  [the longest x1 101 us: per_device(): lax.psum((jnp.sum(normed_one_grad * unit, axis=0), jnp.sum(normed_one_gra...]
    unnamed x14 -> x18, waiting for transfers between devices: 2.6 us -> 155 us
    all_to_all x0 -> x3, blocking collectives: none -> 86 us  [settle(): part = lax.all_to_all(part, 'ctx', split_axis=0, concat_axis=0, tiled=True)]
    convert_element_type x1 -> x7, local copies, waits for them, and re-layouts: 6.2 us -> 49.4 us  [the longest x4 21.6 us: settle(): grad.astype(bf16)]
    dot_general x25 -> x17, matrix products: 134 us -> 101 us  [the longest x1 19.2 us: per_device(): hidden = jnp.dot(low_two, w_up, preferred_element_type=f32) + up_part]
  transfers between devices with their start and end apart: 14 -> 19, of which waited for: 13 -> 15; matrix products, arithmetic and copies ran while one was open for 8% -> 21% of each run, Pallas kernels for 0% -> 0%
where the time goes in v1:
time: 1230 us; the launch traced here: 1220 us
  waiting for transfers between devices  812 us (66%)
  local copies, waits for them, and re-layouts  134 us (11%)
  matrix products  109 us (9%)
  blocking collectives  86 us (7%)
  other arithmetic  38.6 us (3%)
  starting transfers between devices  27.8 us (2%)
  between operations  15.1 us (1%)
    all_to_all x4, waiting for transfers between devices, regroup(): lax.all_to_all(piece, 'ctx', split_axis=0, concat_axis=axis, tiled=False)  321 us
    unnamed x18, waiting for transfers between devices  155 us
    all_gather x4, waiting for transfers between devices, settle(): return lax.all_gather(part, 'stream', axis=1, tiled=False)  125 us
    psum x1, waiting for transfers between devices, per_device(): lax.psum((jnp.sum(normed_one_grad * unit, axis=0), jnp.sum(normed_one_gra...  101 us
    all_to_all x3, blocking collectives, settle(): part = lax.all_to_all(part, 'ctx', split_axis=0, concat_axis=0, tiled=True)  86 us
    reduce_scatter x1, waiting for transfers between devices, per_device(): lax.psum_scatter(branches.astype(bf16), 'ctx', scatter_dimension=0, tiled...  78.2 us
    unnamed x132, local copies, waits for them, and re-layouts  40.2 us
  transfers between devices with their start and end apart: 19, of which 15 were waited for; matrix products, arithmetic and copies ran while one was open for 21% of the time, Pallas kernels for 0%

profile of v1, /device:TPU:0, one launch (start us, length us, event | category | flops | bytes accessed | tf_op | source)
XLA Modules:
  0.0 1222.6 jit_solution(12755390977449677245)
XLA Ops:
  7.2 6.3 all-to-all-start.1
  19.5 37.1 %all-to-all-done.1 = bf16[4,256,1,512]{3,1,2,0:T(8,128)(2,1)} async-done(((bf16[4,256,1,512]{3,1,2,0:T(8,128)(2,1)}), bf16[4,256,1,512]{3,1,2,0:T(8,128)(2,1)}, u32[]{:S(2)}, u32[]{:S(2)}) %all-to-all-start.1) | async-done | bytes 1048608 | tf_op jit(solution)/shard_map/all_to_all | solution.py:289
  56.6 7.1 all-to-all-start
  63.7 6.4 copy.114
  70.1 104.1 %all-to-all-done = bf16[4,3,1,512,256]{3,4,1,2,0:T(8,128)(2,1)S(1)} async-done(((bf16[4,3,1,512,256]{3,4,1,2,0:T(8,128)(2,1)}), bf16[4,3,1,512,256]{3,4,1,2,0:T(8,128)(2,1)S(1)}, u32[]{:S(2)}, u32[]{:S(2)}) %all-to-all-start) | async-done | bytes 3145760 | tf_op jit(solution)/shard_map/all_to_all | solution.py:289
  174.2 5.0 all-to-all-start.2
  185.7 4.1 copy.111
  189.8 4.8 reshape_squeeze.16
  199.4 5.3 add_bitcast_fusion
  204.7 134.7 %all-to-all-done.2 = bf16[4,512,1024]{1,2,0:T(8,128)(2,1)} async-done(((bf16[4,512,1024]{1,2,0:T(8,128)(2,1)}), bf16[4,512,1024]{1,2,0:T(8,128)(2,1)}, u32[]{:S(2)}, u32[]{:S(2)}) %all-to-all-start.2) | async-done | bytes 4194336 | tf_op jit(solution)/shard_map/all_to_all | solution.py:289
  339.4 4.9 all-to-all-start.3
  365.6 6.4 copy.126
  372.0 4.6 fusion.53
  377.1 6.2 copy.115
  387.8 4.5 fusion.59
  392.3 44.7 %all-to-all-done.3 = bf16[4,1024,1,512]{3,1,2,0:T(8,128)(2,1)} async-done(((bf16[4,1024,1,512]{3,1,2,0:T(8,128)(2,1)}), bf16[4,1024,1,512]{3,1,2,0:T(8,128)(2,1)}, u32[]{:S(2)}, u32[]{:S(2)}) %all-to-all-start.3) | async-done | bytes 4194336 | tf_op jit(solution)/shard_map/all_to_all | solution.py:289
  437.0 6.4 copy.118
  443.4 19.2 %multiply_convert_fusion.1 = (bf16[1024,1024]{0,1:T(8,128)(2,1)}, f32[1024,1024]{0,1:T(8,128)}, f32[1024,1024]{0,1:T(8,128)}) fusion(f32[1024]{0:T(1024)S(1)} %copy-done.54, bf16[2048,1024]{1,0:T(8,128)(2,1)} %bitcast.274, bf16[1,1024,2048]{2,1,0:T(8,128)(2,1)} %all-gather.13.cloned.1.call-done, f32[2048]{0:T(1024)S(1)} %copy-done.40, ...), kind=kOutput, calls=%fused_computation.37 | convolution fusion | flops 4376756224 | bytes 18903040 | tf_op jit(solution)/shard_map/dot_general | solution.py:363
  462.7 9.9 convert_reduce_fusion.1
  476.2 12.5 %fusion.120 = (f32[2048]{0:T(1024)}, f32[2048]{0:T(1024)}, bf16[1024,2048]{1,0:T(8,128)(2,1)}, f32[2048]{0:T(1024)}, f32[2048]{0:T(1024)}) fusion(f32[1024]{0:T(1024)S(1)} %copy-done.53, f32[1024]{0:T(1024)S(1)} %broadcast_multiply_fusion.1, bf16[1,1024,2048]{2,1,0:T(8,128)(2,1)S(1)} %copy-done.2, f32[2048]{0:T(1024)S(1)} %copy-done.39, ...), kind=kOutput, calls=%fused_computation.183 | convolution fusion | flops 4322222080 | bytes 23126016 | tf_op jit(solution)/shard_map/dot_general | solution.py:397
  490.3 6.9 fusion.122
  502.1 9.4 convolution_convert_fusion
  512.9 7.5 fusion.34
  520.4 4.7 convert_element_type.211
  529.1 9.4 fusion.30
  538.5 7.8 convert_element_type.228
  546.3 5.2 copy.141
  558.2 11.7 all-to-all-done.5
  570.7 78.2 %reduce-scatter.15.cloned.1.call-done = bf16[256,2048]{1,0:T(8,128)(2,1)} async-done(((bf16[1024,2048]{1,0:T(8,128)(2,1)}), bf16[256,2048]{1,0:T(8,128)(2,1)}) %reduce-scatter.15.cloned.1.call-update) | async-done | bytes 1048592 | tf_op jit(solution)/shard_map/reduce_scatter | solution.py:400
  649.6 107.8 %all-reduce.10.cloned.1.call-done = bf16[4,4,128,1024]{3,2,1,0:T(8,128)(2,1)} async-done(((bf16[4,4,128,1024]{3,2,1,0:T(8,128)(2,1)}), bf16[4,4,128,1024]{3,2,1,0:T(8,128)(2,1)}) %all-reduce.10.cloned.1.call-update) | async-done | bytes 4194320
  759.3 30.2 %all_to_all.70 = bf16[4,128,1024]{2,1,0:T(8,128)(2,1)} all-to-all(bf16[4,128,1024]{2,1,0:T(8,128)(2,1)S(1)} %dynamic-slice_bitcast_fusion), channel_id=1, replica_groups=mesh['stream'=4,'ctx'=4,'head'=2] {'ctx'}, dimensions={0} | all-to-all | bytes 2097152 | tf_op jit(solution)/shard_map/all_to_all | solution.py:449
  789.6 14.7 %reduce-scatter.19.cloned.1.call-done = bf16[4,1,3,128,256]{4,3,2,0,1:T(8,128)(2,1)} async-done(((bf16[4,4,3,128,256]{4,3,2,0,1:T(8,128)(2,1)}), bf16[4,1,3,128,256]{4,3,2,0,1:T(8,128)(2,1)}) %reduce-scatter.19.cloned.1.call-update) | async-done | bytes 786448
  804.3 24.8 %all_to_all.71 = bf16[4,3,128,256]{3,2,1,0:T(8,128)(2,1)} all-to-all(bf16[4,3,128,256]{3,2,1,0:T(8,128)(2,1)} %bitcast.282), channel_id=1, replica_groups=mesh['stream'=4,'ctx'=4,'head'=2] {'ctx'}, dimensions={0} | all-to-all | bytes 1572864 | tf_op jit(solution)/shard_map/all_to_all | solution.py:449
  829.2 30.8 %reduce-scatter.23.cloned.1.call-done = bf16[4,1,256,512]{3,2,0,1:T(8,128)(2,1)} async-done(((bf16[4,4,256,512]{3,2,0,1:T(8,128)(2,1)}), bf16[4,1,256,512]{3,2,0,1:T(8,128)(2,1)}) %reduce-scatter.23.cloned.1.call-update) | async-done | bytes 1048592
  860.0 31.0 %all_to_all.72 = bf16[4,256,512]{2,1,0:T(8,128)(2,1)S(1)} all-to-all(bf16[4,256,512]{2,1,0:T(8,128)(2,1)} %bitcast.281), channel_id=1, replica_groups=mesh['stream'=4,'ctx'=4,'head'=2] {'ctx'}, dimensions={0} | all-to-all | bytes 2097152 | tf_op jit(solution)/shard_map/all_to_all | solution.py:449
  893.5 100.6 %all-reduce.12.cloned.1.call-done = (f32[2048]{0:T(1024)}, f32[2048]{0:T(1024)}, f32[3,2048]{1,0:T(4,128)}, f32[2048]{0:T(1024)}, f32[2048]{0:T(1024)}, /*index=5*/f32[2048]{0:T(1024)}, f32[8192]{0:T(1024)}) async-done(((f32[2048]{0:T(1024)}, f32[2048]{0:T(1024)}, f32[3,2048]{1,0:T(4,128)}, f32[2048]{0:T(1024)}, f32[2048]{0:T(1024)}, /*index=5*/f32[2048]{0:T(1024)}, f32[8192]{0:T(1024)}), (f32[2048]{0:T(1024)}, ...) | async-done | bytes 98320 | tf_op jit(solution)/shard_map/psum | solution.py:430
  996.8 27.3 %all-gather.19.cloned.1.call-done = bf16[4,256,512]{2,1,0:T(8,128)(2,1)} async-done(((bf16[4,64,512]{2,1,0:T(8,128)(2,1)}), bf16[4,256,512]{2,1,0:T(8,128)(2,1)}) %all-gather.19.cloned.1.call-update) | async-done | bytes 1048592 | tf_op jit(solution)/shard_map/all_gather | solution.py:450
  1026.9 20.9 %all-reduce.14.cloned.1.call-done = (bf16[256,2048]{1,0:T(8,128)(2,1)}, bf16[256,2048]{1,0:T(8,128)(2,1)}) async-done(((bf16[256,2048]{1,0:T(8,128)(2,1)}, bf16[256,2048]{1,0:T(8,128)(2,1)}), (bf16[256,2048]{1,0:T(8,128)(2,1)}, bf16[256,2048]{1,0:T(8,128)(2,1)})) %all-reduce.14.cloned.1.call-update) | async-done | bytes 2097168 | tf_op jit(solution)/shard_map/psum | solution.py:399
  1049.7 4.4 fusion.47
  1054.1 49.4 %all-gather.21.cloned.1.call-done = bf16[4,512,1024]{2,1,0:T(8,128)(2,1)} async-done(((bf16[4,128,1024]{2,1,0:T(8,128)(2,1)}), bf16[4,512,1024]{2,1,0:T(8,128)(2,1)}) %all-gather.21.cloned.1.call-update) | async-done | bytes 4194320 | tf_op jit(solution)/shard_map/all_gather | solution.py:450
  1103.6 6.7 convert_bitcast_fusion.1
  1110.2 12.6 %copy.127 = f32[4,128,4,1024]{3,2,1,0:T(4,128)} copy(f32[4,128,4,1024]{3,1,0,2:T(8,128)} %convert_bitcast_fusion.1) | data formatting | bytes 16777216 | tf_op jit(solution)/shard_map/convert_element_type | solution.py:474
  1122.8 15.1 %copy.139 = f32[64,8,4,1024]{3,1,2,0:T(8,128)} copy(f32[64,8,4,1024]{3,2,1,0:T(4,128)} %bitcast.261) | data formatting | bytes 16777216
  1137.9 11.7 all-gather.17.cloned.1.call-done
  1152.3 6.8 copy.125
  1159.1 8.3 reshape.394
  1167.4 36.7 %all-gather.23.cloned.1.call-done = bf16[4,1024,512]{2,0,1:T(4,128)(2,1)} async-done(((bf16[4,256,512]{2,0,1:T(4,128)(2,1)}), bf16[4,1024,512]{2,0,1:T(4,128)(2,1)}) %all-gather.23.cloned.1.call-update) | async-done | bytes 4194320 | tf_op jit(solution)/shard_map/all_gather | solution.py:450
  1207.2 4.9 bitcast_convert_fusion
  (220 shorter events, 87.8 us)
Async XLA Ops:
  7.2 49.4 %all-to-all-start.1 = ((bf16[4,256,1,512]{3,1,2,0:T(8,128)(2,1)}), bf16[4,256,1,512]{3,1,2,0:T(8,128)(2,1)}, u32[]{:S(2)}, u32[]{:S(2)}) async-start(bf16[4,256,1,512]{3,1,2,0:T(8,128)(2,1)} %bitcast.280), calls=%async_computation.1 | async-start | bytes 2097152 | tf_op jit(solution)/shard_map/all_to_all | solution.py:289
  13.5 181.1 %all-gather.13.cloned.1.call-start = ((), (), s32[]{:S(2)}) async-start(), calls=%async_computation.15 | async-start | bytes 5242880 | tf_op jit(solution)/shard_map/all_gather | solution.py:320
  56.6 117.6 %all-to-all-start = ((bf16[4,3,1,512,256]{3,4,1,2,0:T(8,128)(2,1)}), bf16[4,3,1,512,256]{3,4,1,2,0:T(8,128)(2,1)S(1)}, u32[]{:S(2)}, u32[]{:S(2)}) async-start(bf16[4,3,1,512,256]{3,4,1,2,0:T(8,128)(2,1)} %copy.110), calls=%async_computation | async-start | bytes 6291456 | tf_op jit(solution)/shard_map/all_to_all | solution.py:289
  174.2 5.8 copy-start.46
  174.2 5.8 copy-start.47
  174.2 5.9 copy-start.48
  174.2 6.5 copy-start.49
  174.2 9.0 copy-start.56
  174.2 165.2 %all-to-all-start.2 = ((bf16[4,512,1024]{1,2,0:T(8,128)(2,1)}), bf16[4,512,1024]{1,2,0:T(8,128)(2,1)}, u32[]{:S(2)}, u32[]{:S(2)}) async-start(bf16[4,512,1024]{1,2,0:T(8,128)(2,1)} %bitcast.263), calls=%async_computation.2 | async-start | bytes 8388608 | tf_op jit(solution)/shard_map/all_to_all | solution.py:289
  179.2 171.5 %all-gather.15.cloned.1.call-start = ((), (), s32[]{:S(2)}) async-start(), calls=%async_computation.16 | async-start | bytes 5242880 | tf_op jit(solution)/shard_map/all_gather | solution.py:321
  180.0 19.3 %copy-start.35 = (f32[2048]{0:T(1024)}, f32[2048]{0:T(1024)S(1)}, u32[]{:S(2)}) copy-start(f32[2048]{0:T(1024)S(1)} %convert_element_type.182) | copy-start | bytes 24580
  180.0 19.3 %copy-start.37 = (f32[2048]{0:T(1024)}, f32[2048]{0:T(1024)S(1)}, u32[]{:S(2)}) copy-start(f32[2048]{0:T(1024)S(1)} %convert_element_type.183) | copy-start | bytes 24580
  181.3 165.0 %copy-start.55 = (f32[32]{0:T(128)}, f32[32]{0:T(128)S(1)}, u32[]{:S(2)}) copy-start(f32[32]{0:T(128)S(1)} %multiply_power_fusion) | copy-start | bytes 388
  339.4 97.6 %all-to-all-start.3 = ((bf16[4,1024,1,512]{3,1,2,0:T(8,128)(2,1)}), bf16[4,1024,1,512]{3,1,2,0:T(8,128)(2,1)}, u32[]{:S(2)}, u32[]{:S(2)}) async-start(bf16[4,1024,1,512]{3,1,2,0:T(8,128)(2,1)} %bitcast.271), calls=%async_computation.3 | async-start | bytes 8388608 | tf_op jit(solution)/shard_map/all_to_all | solution.py:289
  344.3 208.6 %reduce-scatter.21.cloned.1.call-start = ((), (), s32[]{:S(2)}) async-start(), calls=%async_computation.23 | async-start | bytes 1310720
  376.7 194.0 %reduce-scatter.17.cloned.1.call-start = ((), (), s32[]{:S(2)}) async-start(), calls=%async_computation.14 | async-start | bytes 5242880 | tf_op jit(solution)/shard_map/reduce_scatter | solution.py:404
  392.3 51.1 %copy-start.39 = (f32[2048]{0:T(1024)S(1)}, f32[2048]{0:T(1024)}, u32[]{:S(2)}) copy-start(f32[2048]{0:T(1024)} %convert_element_type.191) | copy-start | bytes 24580
  392.3 51.1 %copy-start.40 = (f32[2048]{0:T(1024)S(1)}, f32[2048]{0:T(1024)}, u32[]{:S(2)}) copy-start(f32[2048]{0:T(1024)} %convert_element_type.192) | copy-start | bytes 24580
  392.3 51.1 %copy-start.53 = (f32[1024]{0:T(1024)S(1)}, f32[1024]{0:T(1024)}, u32[]{:S(2)}) copy-start(f32[1024]{0:T(1024)} %copy-done.52) | copy-start | bytes 12292
  392.3 51.1 %copy-start.54 = (f32[1024]{0:T(1024)S(1)}, f32[1024]{0:T(1024)}, u32[]{:S(2)}) copy-start(f32[1024]{0:T(1024)} %dynamic-slice_convert_fusion) | copy-start | bytes 12292
  443.4 19.2 %copy-start.12 = (bf16[1,1024,2048]{2,1,0:T(8,128)(2,1)S(1)}, bf16[1,1024,2048]{2,1,0:T(8,128)(2,1)}, u32[]{:S(2)}) copy-start(bf16[1,1024,2048]{2,1,0:T(8,128)(2,1)} %all-gather.15.cloned.1.call-done) | copy-start | bytes 12582916
  443.4 19.2 %copy-start.13 = (bf16[4,1024,1,512]{1,3,0,2:T(8,128)(2,1)S(1)}, bf16[4,1024,1,512]{1,3,0,2:T(8,128)(2,1)}, u32[]{:S(2)}) copy-start(bf16[4,1024,1,512]{1,3,0,2:T(8,128)(2,1)} %copy.118) | copy-start | bytes 12582916
  462.6 10.0 copy-start.4
  462.6 10.0 copy-start.7
  462.7 10.0 copy-start.14
  488.7 160.2 %reduce-scatter.15.cloned.1.call-start = ((), (), s32[]{:S(2)}) async-start(), calls=%async_computation.13 | async-start | bytes 5242880 | tf_op jit(solution)/shard_map/reduce_scatter | solution.py:400
  490.3 6.9 copy-start.10
  490.3 6.9 copy-start.19
  500.6 256.8 %all-reduce.10.cloned.1.call-start = ((), (), s32[]{:S(2)}) async-start(), calls=%async_computation.21 | async-start | bytes 8388608
  511.6 292.8 %reduce-scatter.19.cloned.1.call-start = ((), (), s32[]{:S(2)}) async-start(), calls=%async_computation.22 | async-start | bytes 3932160
  529.1 330.9 %reduce-scatter.23.cloned.1.call-start = ((), (), s32[]{:S(2)}) async-start(), calls=%async_computation.24 | async-start | bytes 5242880
  551.5 5.7 copy-start.6
  551.5 5.7 copy-start.9
  551.5 5.7 copy-start.16
  551.5 97.5 %copy-start.57 = (u32[32]{0:T(128)S(1)}, u32[32]{0:T(128)}, u32[]{:S(2)}) copy-start(u32[32]{0:T(128)} %constant.122) | copy-start | bytes 388
  552.9 17.0 %all-to-all-start.5 = ((bf16[4,64,512]{2,1,0:T(8,128)(2,1)}), bf16[4,64,512]{2,1,0:T(8,128)(2,1)S(1)}, u32[]{:S(2)}, u32[]{:S(2)}) async-start(bf16[4,64,512]{2,1,0:T(8,128)(2,1)} %bitcast.284), calls=%async_computation.7 | async-start | bytes 524288 | tf_op jit(solution)/shard_map/all_to_all | solution.py:449
  556.3 437.8 %all-reduce.12.cloned.1.call-start = ((), (), s32[]{:S(2)}) async-start(), calls=%async_computation.25 | async-start | bytes 212992 | tf_op jit(solution)/shard_map/psum | solution.py:430
  558.1 465.9 %all-gather.19.cloned.1.call-start = ((), (), s32[]{:S(2)}) async-start(), calls=%async_computation.18 | async-start | bytes 1310720 | tf_op jit(solution)/shard_map/all_gather | solution.py:450
  570.6 477.2 %all-reduce.14.cloned.1.call-start = ((), (), s32[]{:S(2)}) async-start(), calls=%async_computation.26 | async-start | bytes 4194304 | tf_op jit(solution)/shard_map/psum | solution.py:399
  649.0 454.6 %all-gather.21.cloned.1.call-start = ((), (), s32[]{:S(2)}) async-start(), calls=%async_computation.19 | async-start | bytes 5242880 | tf_op jit(solution)/shard_map/all_gather | solution.py:450
  789.5 103.3 %copy-start.50 = (bf16[2048]{0:T(1024)(128)(2,1)S(1)}, bf16[2048]{0:T(1024)(128)(2,1)}, u32[]{:S(2)}) copy-start(bf16[2048]{0:T(1024)(128)(2,1)} %param.22) | copy-start | bytes 12292
  789.5 103.3 %copy-start.51 = (bf16[2048]{0:T(1024)(128)(2,1)S(1)}, bf16[2048]{0:T(1024)(128)(2,1)}, u32[]{:S(2)}) copy-start(bf16[2048]{0:T(1024)(128)(2,1)} %param.28) | copy-start | bytes 12292
  789.6 103.3 %copy-start = (bf16[1,256,2048]{2,1,0:T(8,128)(2,1)S(1)}, bf16[1,256,2048]{2,1,0:T(8,128)(2,1)}, u32[]{:S(2)}) copy-start(bf16[1,256,2048]{2,1,0:T(8,128)(2,1)} %param.15) | copy-start | bytes 3145732
  789.6 360.0 %all-gather.17.cloned.1.call-start = ((), (), s32[]{:S(2)}) async-start(), calls=%async_computation.17 | async-start | bytes 3932160 | tf_op jit(solution)/shard_map/all_gather | solution.py:450
  829.2 375.0 %all-gather.23.cloned.1.call-start = ((), (), s32[]{:S(2)}) async-start(), calls=%async_computation.20 | async-start | bytes 5242880 | tf_op jit(solution)/shard_map/all_gather | solution.py:450
  1207.2 6.1 copy-start.43
  1207.2 7.3 copy-start.42
  1207.2 7.9 copy-start.41
  (32 other events, 65.5 us)
Sparse Core Ops, SparseCore 0:
  15.9 151.0 all-gather.12
  181.6 147.8 all-gather.14
  376.8 29.0 reduce-scatter.20
  488.8 78.5 reduce-scatter.16
  570.1 78.7 reduce-scatter.14
  653.0 104.3 all-reduce.9
  760.4 43.9 reduce-scatter.18
  807.3 52.6 reduce-scatter.22
  868.7 125.3 all-reduce.11
  996.4 27.6 all-gather.18
  1026.5 21.2 all-reduce.13
  1049.6 53.8 all-gather.20
  1105.5 43.9 all-gather.16
  1151.4 52.6 all-gather.22

commit v2 on v1

--- a/solution.py
+++ b/solution.py
@@ -4,6 +4,8 @@
 import jax
 import jax.numpy as jnp
 from jax import lax
+from jax.experimental import pallas as pl
+from jax.experimental.pallas import tpu as pltpu
 from jax.sharding import PartitionSpec as P
 
 HEAD = 256
@@ -285,8 +287,522 @@
     return positions, doc_starts(doc_sizes, positions)
 
 
-def regroup(piece, axis):
-    return lax.all_to_all(piece, "ctx", split_axis=0, concat_axis=axis, tiled=False)
+MESH = pl.DeviceIdType.MESH
+
+
+def span(index, size):
+    return pl.ds(pl.multiple_of(index * size, size), size)
+
+
+def places():
+    return lax.axis_index("stream"), lax.axis_index("ctx"), lax.axis_index("head")
+
+
+def greet(peers):
+    barrier = pltpu.get_barrier_semaphore()
+    for peer in peers:
+        pl.semaphore_signal(barrier, inc=1, device_id=peer, device_id_type=MESH)
+    pl.semaphore_wait(barrier, len(peers))
+
+
+def gather_body(
+    x_ref, g_ref, qkv_ref, up_ref, out_ref, down_ref,
+    x_all, g_all, qkv_all, up_all, out_all, down_all,
+    z_send, z_recv, x_send, x_recv, y_send, y_recv, fx_send, fx_recv, fy_send, fy_recv,
+    line_send, line_recv, core_send, core_recv, own_sem,
+    *held,
+):
+    s, c, h = places()
+    x_peer = s + 1 - 2 * lax.rem(s, 2)
+    y_peer = lax.rem(s + 2, 4)
+    across = ((x_peer, c, h), (y_peer, c, h))
+    core_peer = (s, c, 1 - h)
+    ring = [(s, lax.rem(c + k, 4), h) for k in (1, 2, 3)]
+    greet([*across, core_peer, *ring])
+
+    count = x_ref.shape[0]
+    slab, width, units = up_ref.shape[0], out_ref.shape[0] // 4, down_ref.shape[0] // 4
+    quarter, half_count = slab // 4, count // 2
+
+    def rows(base, size):
+        return pl.ds(pl.multiple_of(base, size), size)
+
+    def landed(m, r, part, half):
+        def cut(total):
+            size = total // 4
+            if half is None:
+                return part * size, size
+            return part * size + half * (size // 2), size // 2
+
+        if m == 0:
+            at, size = cut(slab)
+            return qkv_all.at[:, rows(r * slab + at, size), :]
+        if m == 1:
+            at, size = cut(slab)
+            return up_all.at[rows(r * slab + at, size), :]
+        if m == 2:
+            at, size = cut(width)
+            return out_all.at[rows(at, size), span(r, slab)]
+        at, size = cut(units)
+        return down_all.at[rows(at, size), span(r, slab)]
+
+    def piece(m, to, part=None):
+        if m == 0:
+            inner = slice(None) if part is None else span(part, quarter)
+            return qkv_ref.at[:, inner, span(to, width)]
+        if m == 1:
+            inner = slice(None) if part is None else span(part, quarter)
+            return up_ref.at[inner, span(to, units)]
+        size = width if m == 2 else units
+        ref = out_ref if m == 2 else down_ref
+        if part is None:
+            return ref.at[span(to, size), :]
+        return ref.at[rows(to * size + part * (size // 4), size // 4), :]
+
+    def whole_piece(m, r):
+        if m == 0:
+            return qkv_all.at[:, span(r, slab), :]
+        if m == 1:
+            return up_all.at[span(r, slab), :]
+        return (out_all if m == 2 else down_all).at[:, span(r, slab)]
+
+    def remote(src, dst, send, recv, to):
+        return pltpu.make_async_remote_copy(
+            src_ref=src, dst_ref=dst, send_sem=send, recv_sem=recv, device_id=to, device_id_type=MESH
+        )
+
+    def z_copy(m, k):
+        to = lax.rem(c + 4 - k, 4)
+        return remote(
+            piece(m, to, s), landed(m, c, s, None), z_send.at[m, k - 1], z_recv.at[m, k - 1], (s, to, h)
+        )
+
+    def direct(m, k, axis):
+        r = lax.rem(c + k, 4)
+        send, recv = (x_send, x_recv) if axis == 0 else (y_send, y_recv)
+        here = landed(m, r, s, None)
+        return remote(here, here, send.at[m, k - 1], recv.at[m, k - 1], across[axis])
+
+    def onward(m, k, axis):
+        r = lax.rem(c + k, 4)
+        send, recv = (fx_send, fx_recv) if axis == 0 else (fy_send, fy_recv)
+        here = landed(m, r, y_peer if axis == 0 else x_peer, 1 if axis == 0 else 0)
+        return remote(here, here, send.at[m, k - 1], recv.at[m, k - 1], across[axis])
+
+    lines = ((x_ref, x_all), (g_ref, g_all))
+
+    def block(a, origin):
+        return lines[a][1].at[rows(origin * count + h * half_count, half_count), :]
+
+    def line_copy(a, t, side):
+        origin = c - t if side == 0 else c + t
+        src = lines[a][0].at[span(h, half_count), :] if t == 0 else block(a, origin)
+        to = c + 1 if side == 0 else c - 1
+        return remote(
+            src, block(a, origin), line_send.at[a, side, t], line_recv.at[a, side, t], (s, to, h)
+        )
+
+    def core_copy(a, t, side):
+        origin = c - t if side == 0 else c + t
+        here = block(a, origin)
+        return remote(here, here, core_send.at[a, side, t - 1], core_recv.at[a, side, t - 1], core_peer)
+
+    def sends(t, side):
+        if side == 0:
+            return (c >= t) & (c < 3)
+        return (c + t <= 3) & (c > 0)
+
+    def gets(t, side):
+        return c >= t if side == 0 else c + t <= 3
+
+    def line_step(a, t):
+        for side in (0, 1):
+            @pl.when(gets(t, side))
+            def _():
+                line_copy(a, t - 1, side).wait_recv()
+                core_copy(a, t, side).start()
+
+            if t < 3:
+                @pl.when(sends(t, side))
+                def _():
+                    line_copy(a, t, side).start()
+
+    near = (1, 3, 2)
+    order = [(m, k) for m in (0, 1, 3, 2) for k in near]
+
+    def start_lines():
+        for a in (0, 1):
+            for side in (0, 1):
+                @pl.when(sends(0, side))
+                def _():
+                    line_copy(a, 0, side).start()
+
+    def start_z(m):
+        for k in near:
+            z_copy(m, k).start()
+
+    def pass_on(m):
+        for k in near:
+            direct(m, k, 0).wait_recv()
+            onward(m, k, 1).start()
+            direct(m, k, 1).wait_recv()
+            onward(m, k, 0).start()
+
+    def spread(m):
+        for k in near:
+            z_copy(m, k).wait_recv()
+            direct(m, k, 0).start()
+            direct(m, k, 1).start()
+
+    start_z(0)
+    start_lines()
+    start_z(1)
+    sources = [lines[0][0], lines[1][0]] + [piece(m, c) for m in range(4)]
+    ends = [lines[a][1].at[span(c, count), :] for a in (0, 1)] + [whole_piece(m, c) for m in range(4)]
+    ins = [pltpu.make_async_copy(a, b, own_sem.at[i]) for i, (a, b) in enumerate(zip(sources, held))]
+    own = [pltpu.make_async_copy(b, e, own_sem.at[i]) for i, (b, e) in enumerate(zip(held, ends))]
+    for copy in ins:
+        copy.start()
+    for copy, out in zip(ins, own):
+        copy.wait()
+        out.start()
+
+    spread(0)
+    line_step(0, 1)
+    line_step(1, 1)
+    start_z(3)
+    spread(1)
+    pass_on(0)
+    start_z(2)
+    line_step(0, 2)
+    line_step(1, 2)
+    spread(3)
+    pass_on(1)
+    spread(2)
+    pass_on(3)
+    line_step(0, 3)
+    line_step(1, 3)
+    pass_on(2)
+    for m, k in order:
+        onward(m, k, 0).wait_recv()
+        onward(m, k, 1).wait_recv()
+    for a in (0, 1):
+        for side in (0, 1):
+            for t in (1, 2, 3):
+                @pl.when(gets(t, side))
+                def _():
+                    core_copy(a, t, side).wait()
+                @pl.when(sends(t - 1, side))
+                def _():
+                    line_copy(a, t - 1, side).wait_send()
+    for m, k in order:
+        z_copy(m, k).wait_send()
+        for axis in (0, 1):
+            direct(m, k, axis).wait_send()
+            onward(m, k, axis).wait_send()
+    for copy in own:
+        copy.wait()
+
+
+def gather_all(tokens, cotangent, w_qkv, w_up, w_out, w_down):
+    count, model = tokens.shape
+    slab = w_up.shape[0]
+    width, units = w_out.shape[0] // 4, w_down.shape[0] // 4
+    bf16 = jnp.bfloat16
+    dma = pltpu.SemaphoreType.DMA
+    return pl.pallas_call(
+        gather_body,
+        out_shape=[
+            jax.ShapeDtypeStruct((4 * count, model), bf16),
+            jax.ShapeDtypeStruct((4 * count, model), bf16),
+            jax.ShapeDtypeStruct((3, model, width), bf16),
+            jax.ShapeDtypeStruct((model, units), bf16),
+            jax.ShapeDtypeStruct((width, model), bf16),
+            jax.ShapeDtypeStruct((units, model), bf16),
+        ],
+        in_specs=[pl.BlockSpec(memory_space=pl.ANY)] * 6,
+        out_specs=[pl.BlockSpec(memory_space=pl.ANY)] * 6,
+        scratch_shapes=[dma((4, 3))] * 10 + [dma((2, 2, 3))] * 4 + [dma((6,))]
+        + [
+            pltpu.VMEM(shape, bf16)
+            for shape in (
+                (count, model), (count, model), (3, slab, width), (slab, units), (width, slab), (units, slab)
+            )
+        ],
+        compiler_params=pltpu.CompilerParams(
+            collective_id=0, has_side_effects=True, vmem_limit_bytes=32 << 20
+        ),
+        name="gather",
+    )(tokens, cotangent, w_qkv, w_up, w_out, w_down)
+
+
+LEADS = (12, 4, 1, 1)
+
+
+def settle_body(
+    bra_ref, inw_ref, g0, g1, g2, g3,
+    joint, inward, o0, o1, o2, o3,
+    s1x_send, s1x_recv, s1y_send, s1y_recv, s2x_send, s2x_recv, s2y_send, s2y_recv,
+    z_send, z_recv, x_send, x_recv, y_send, y_recv, fx_send, fx_recv, fy_send, fy_recv,
+    own_sem, core_send, core_recv, row_send, row_recv, back_send, back_recv, keep_sem, half_sem,
+    *bufs,
+):
+    s, c, h = places()
+    x_at, y_at = lax.rem(s, 2), lax.div(s, 2)
+    x_off, y_off = 1 - x_at, 1 - y_at
+    x_peer, y_peer = y_at * 2 + x_off, y_off * 2 + x_at
+    across = ((x_peer, c, h), (y_peer, c, h))
+    core_peer = (s, c, 1 - h)
+    ring = [(s, lax.rem(c + k, 4), h) for k in (1, 2, 3)]
+    greet([*across, core_peer, *ring])
+    grads, outs = (g0, g1, g2, g3), (o0, o1, o2, o3)
+    mine = [bufs[2 * m : 2 * m + 2] for m in range(4)]
+    first = [bufs[8 + 2 * m : 10 + 2 * m] for m in range(4)]
+    second = [bufs[16 + 2 * m : 18 + 2 * m] for m in range(4)]
+    own_half, core_half, row_parts, done_half = bufs[24:26], bufs[26:28], bufs[28:30], bufs[30:32]
+    slab = o2.shape[-1]
+
+    def remote(src, dst, send, recv, to):
+        return pltpu.make_async_remote_copy(
+            src_ref=src, dst_ref=dst, send_sem=send, recv_sem=recv, device_id=to, device_id_type=MESH
+        )
+
+    def one(m, half):
+        src = grads[m].at[:, :, x_off, 0] if half == 0 else grads[m].at[:, y_off, :, 1]
+        send, recv = (s1x_send, s1x_recv) if half == 0 else (s1y_send, s1y_recv)
+        return remote(src, first[m][half], send.at[m], recv.at[m], across[half])
+
+    def load(m, half):
+        src = grads[m].at[:, :, x_at, 0] if half == 0 else grads[m].at[:, y_at, :, 1]
+        return pltpu.make_async_copy(src, mine[m][half], own_sem.at[m, half])
+
+    def two(m, half):
+        src = mine[m][half].at[:, y_off if half == 0 else x_off]
+        send, recv = (s2y_send, s2y_recv) if half == 0 else (s2x_send, s2x_recv)
+        return remote(src, second[m][half], send.at[m], recv.at[m], across[1 - half])
+
+    def add_first(m, half):
+        into, more = mine[m][half], first[m][half]
+        lead, _, height, _ = into.shape
+        tall = min(height, 32)
+
+        @pl.loop(0, lead * 2 * (height // tall))
+        def _(i):
+            at = lax.rem(i, height // tall)
+            pair = lax.div(i, height // tall)
+            l, j, rows = lax.div(pair, 2), lax.rem(pair, 2), span(at, tall)
+            total = into[l, j, rows, :].astype(jnp.float32) + more[l, j, rows, :].astype(jnp.float32)
+            into[l, j, rows, :] = total.astype(into.dtype)
+
+    def add_second(m, half):
+        into, more = second[m][half], mine[m][half]
+        keep = y_at if half == 0 else x_at
+        lead, height, _ = into.shape
+        tall = min(height, 32)
+
+        @pl.loop(0, lead * (height // tall))
+        def _(i):
+            l, rows = lax.div(i, height // tall), span(lax.rem(i, height // tall), tall)
+            total = into[l, rows, :].astype(jnp.float32) + more[l, keep, rows, :].astype(jnp.float32)
+            into[l, rows, :] = total.astype(into.dtype)
+
+    def share_of(m, half, to):
+        ref = second[m][half]
+        if m == 0:
+            return ref.reshape(3, 4, *ref.shape[1:]).at[:, to]
+        if m == 1:
+            return ref.at[to]
+        return ref.at[0, :, span(to, slab)]
+
+    def home(m, half):
+        if m == 0:
+            return outs[0].at[:, s, half, :, span(c, second[0][0].shape[-1])]
+        if m == 1:
+            return outs[1].at[s, half, :, span(c, second[1][0].shape[-1])]
+        return outs[m].at[c, s, half]
+
+    def z_copy(m, half, k):
+        to = lax.rem(c + 4 - k, 4)
+        i = (m * 2 + half) * 3 + k - 1
+        return remote(share_of(m, half, to), home(m, half), z_send.at[i], z_recv.at[i], (s, to, h))
+
+    def keep(m, half):
+        return pltpu.make_async_copy(share_of(m, half, c), home(m, half), keep_sem.at[m, half])
+
+    def quarter(m, q, half=None):
+        if half is None:
+            return outs[m].at[q] if m == 1 else outs[m].at[:, q]
+        return outs[m].at[q, half] if m == 1 else outs[m].at[:, q, half]
+
+    def direct(m, axis):
+        send, recv = (x_send, x_recv) if axis == 0 else (y_send, y_recv)
+        here = quarter(m, s)
+        return remote(here, here, send.at[m], recv.at[m], across[axis])
+
+    def onward(m, axis):
+        send, recv = (fx_send, fx_recv) if axis == 0 else (fy_send, fy_recv)
+        here = quarter(m, y_peer if axis == 0 else x_peer, 1 - axis)
+        return remote(here, here, send.at[m], recv.at[m], across[axis])
+
+    wholes, sums = (bra_ref, inw_ref), (joint, inward)
+    span_cols = own_half[0].shape[1]
+    count = joint.shape[0]
+
+    def core_copy(a):
+        return remote(
+            wholes[a].at[:, span(1 - h, span_cols)], core_half[a], core_send.at[a], core_recv.at[a], core_peer
+        )
+
+    def half_load(a):
+        return pltpu.make_async_copy(wholes[a].at[:, span(h, span_cols)], own_half[a], half_sem.at[a])
+
+    def row_copy(a, k):
+        to = lax.rem(c + 4 - k, 4)
+        return remote(
+            own_half[a].at[span(to, count)], row_parts[a].at[k - 1],
+            row_send.at[a, k - 1], row_recv.at[a, k - 1], (s, to, h),
+        )
+
+    def back_copy(a):
+        here = sums[a].at[:, span(h, span_cols)]
+        return remote(done_half[a], here, back_send.at[a], back_recv.at[a], core_peer)
+
+    def back_keep(a):
+        return pltpu.make_async_copy(done_half[a], sums[a].at[:, span(h, span_cols)], half_sem.at[a])
+
+    order = (3, 1, 0, 2)
+    for m in order:
+        for half in (0, 1):
+            one(m, half).start()
+    for a in (0, 1):
+        core_copy(a).start()
+        half_load(a).start()
+    for m in order:
+        for half in (0, 1):
+            load(m, half).start()
+    for a in (0, 1):
+        half_load(a).wait()
+        core_copy(a).wait_recv()
+        tall = 32
+
+        @pl.loop(0, own_half[a].shape[0] // tall)
+        def _(i):
+            rows = span(i, tall)
+            total = own_half[a][rows, :].astype(jnp.float32) + core_half[a][rows, :].astype(jnp.float32)
+            own_half[a][rows, :] = total.astype(own_half[a].dtype)
+
+        for k in (1, 3, 2):
+            row_copy(a, k).start()
+
+    def stage_two(m):
+        for half in (0, 1):
+            load(m, half).wait()
+            one(m, half).wait_recv()
+            add_first(m, half)
+            two(m, half).start()
+
+    def stage_z(m):
+        for half in (0, 1):
+            two(m, half).wait_recv()
+            add_second(m, half)
+            for k in (1, 3, 2):
+                z_copy(m, half, k).start()
+            keep(m, half).start()
+
+    def stage_out(m):
+        for half in (0, 1):
+            for k in (1, 3, 2):
+                z_copy(m, half, k).wait_recv()
+            keep(m, half).wait()
+        for axis in (0, 1):
+            direct(m, axis).start()
+
+    def stage_on(m):
+        direct(m, 0).wait_recv()
+        onward(m, 1).start()
+        direct(m, 1).wait_recv()
+        onward(m, 0).start()
+
+    def line_sum(a):
+        for k in (1, 3, 2):
+            row_copy(a, k).wait_recv()
+        tall = 32
+
+        @pl.loop(0, count // tall)
+        def _(i):
+            rows = span(i, tall)
+            total = own_half[a][pl.ds(pl.multiple_of(c * count + i * tall, tall), tall), :].astype(jnp.float32)
+            for k in range(3):
+                total = total + row_parts[a][k, rows, :].astype(jnp.float32)
+            done_half[a][rows, :] = total.astype(done_half[a].dtype)
+
+        back_copy(a).start()
+        back_keep(a).start()
+
+    stages = (stage_two, stage_z, stage_out, stage_on)
+    lag = 1
+    for step in range(len(order) + lag * (len(stages) - 1)):
+        for i, stage in enumerate(stages):
+            j = step - i * lag
+            if 0 <= j < len(order):
+                stage(order[j])
+        if step in (2, 3):
+            line_sum(step - 2)
+    for m in order:
+        for axis in (0, 1):
+            onward(m, axis).wait_recv()
+    for a in (0, 1):
+        back_copy(a).wait()
+        back_keep(a).wait()
+        core_copy(a).wait_send()
+        for k in (1, 2, 3):
+            row_copy(a, k).wait_send()
+    for m in order:
+        for half in (0, 1):
+            one(m, half).wait_send()
+            two(m, half).wait_send()
+            for k in (1, 2, 3):
+                z_copy(m, half, k).wait_send()
+        for axis in (0, 1):
+            direct(m, axis).wait_send()
+            onward(m, axis).wait_send()
+
+
+def settle_all(branches, inward, g_qkv, g_up, g_out, g_down):
+    length, model = branches.shape
+    width, units = g_qkv.shape[2], g_up.shape[1]
+    slab, count = model // 4, length // 4
+    bf16 = jnp.bfloat16
+    dma = pltpu.SemaphoreType.DMA
+    rows = (slab // 8, slab // 8, width // 8, units // 8)
+    cols = (width, units, model, model)
+    views = [
+        g.reshape(lead, 2, 2, 2, r, k)
+        for g, lead, r, k in zip((g_qkv, g_up, g_out, g_down), LEADS, rows, cols)
+    ]
+    out_shapes = [
+        (count, model), (count, model),
+        (3, 4, 2, rows[0], 4 * width), (4, 2, rows[1], 4 * units),
+        (4, 4, 2, rows[2], slab), (4, 4, 2, rows[3], slab),
+    ]
+    pairs = [(l, 2, r, k) for l, r, k in zip(LEADS, rows, cols)]
+    scratch = [dma((4,))] * 8 + [dma((24,))] * 2 + [dma((4,))] * 8
+    scratch += [dma((4, 2)), dma((2,)), dma((2,)), dma((2, 3)), dma((2, 3)), dma((2,)), dma((2,)), dma((4, 2)), dma((2,))]
+    vmem = [p for p in pairs for _ in (0, 1)] * 2 + [(p[0], p[2], p[3]) for p in pairs for _ in (0, 1)]
+    vmem += [(length, model // 2)] * 4 + [(3, count, model // 2)] * 2 + [(count, model // 2)] * 2
+    scratch += [pltpu.VMEM(v, bf16) for v in vmem]
+    joint, inward, q, u, o, d = pl.pallas_call(
+        settle_body,
+        out_shape=[jax.ShapeDtypeStruct(v, bf16) for v in out_shapes],
+        in_specs=[pl.BlockSpec(memory_space=pl.ANY)] * 6,
+        out_specs=[pl.BlockSpec(memory_space=pl.ANY)] * 6,
+        scratch_shapes=scratch,
+        compiler_params=pltpu.CompilerParams(
+            collective_id=1, has_side_effects=True, vmem_limit_bytes=48 << 20
+        ),
+        name="settle",
+    )(branches, inward, *views)
+    return joint, inward, q.reshape(3, slab, 4 * width), u.reshape(slab, 4 * units), o.reshape(4 * width, slab), d.reshape(4 * units, slab)
 
 
 def per_device(
@@ -307,7 +823,7 @@
     cotangent,
 ):
     f32, bf16 = jnp.float32, jnp.bfloat16
-    ctx_count, stream_count = lax.axis_size("ctx"), lax.axis_size("stream")
+    ctx_count = lax.axis_size("ctx")
     head_count = lax.axis_size("head")
     c = lax.axis_index("ctx")
     h = lax.axis_index("head")
@@ -317,16 +833,9 @@
     width = qkv_weight.shape[2] // ctx_count
     units = up_weight.shape[1] // ctx_count
 
-    all_tokens = lax.all_gather(tokens[0], "ctx", axis=0, tiled=True)
-    upstream = lax.all_gather(cotangent[0], "ctx", axis=0, tiled=True)
-    w_qkv = regroup(
-        qkv_weight.reshape(3, slab, ctx_count, width).transpose(2, 0, 1, 3), 1
-    ).reshape(3, model, width)
-    w_up = regroup(up_weight.reshape(slab, ctx_count, units).transpose(1, 0, 2), 0).reshape(
-        model, units
-    )
-    w_out = regroup(out_weight.reshape(ctx_count, width, slab), 1).reshape(width, model)
-    w_down = regroup(down_weight.reshape(ctx_count, units, slab), 1).reshape(units, model)
+    all_tokens, upstream, w_qkv, w_up, w_out, w_down = gather_all(
+        tokens[0], cotangent[0], qkv_weight, up_weight, out_weight, down_weight
+    )
 
     gain_one, offset_one = ln1_gain.astype(f32), ln1_bias.astype(f32)
     gain_two, offset_two = ln2_gain.astype(f32), ln2_bias.astype(f32)
@@ -396,13 +905,16 @@
     normed_one_grad = jnp.einsum("cne,cde->nd", projected_grad, w_qkv, preferred_element_type=f32)
     normed_two_grad = jnp.dot(hidden_grad, w_up.T, preferred_element_type=f32)
 
-    joint = lax.psum(
-        lax.psum_scatter(branches.astype(bf16), "ctx", scatter_dimension=0, tiled=True), "head"
-    ).astype(f32)
     inward = gain_one * normed_one_grad + gain_two * normed_two_grad
-    inward = lax.psum(
-        lax.psum_scatter(inward.astype(bf16), "ctx", scatter_dimension=0, tiled=True), "head"
-    ).astype(f32)
+    joint, inward, qkv_out, up_out, out_out, down_out = settle_all(
+        branches.astype(bf16),
+        inward.astype(bf16),
+        qkv_grad.astype(bf16),
+        up_grad.astype(bf16),
+        out_grad.astype(bf16),
+        down_grad.astype(bf16),
+    )
+    joint, inward = joint.astype(f32), inward.astype(f32)
 
     own = tokens[0].astype(f32)
     own_upstream = cotangent[0].astype(f32)
@@ -442,24 +954,6 @@
     qkv_bias_grad = lax.dynamic_slice_in_dim(small[2], h * ctx_count * width, ctx_count * width, 1)
     up_bias_grad = lax.dynamic_slice_in_dim(small[6], h * ctx_count * units, ctx_count * units, 0)
 
-    def settle(grad):
-        part = lax.psum_scatter(
-            grad.astype(bf16), "stream", scatter_dimension=1, tiled=True
-        )[:, 0]
-        part = lax.all_to_all(part, "ctx", split_axis=0, concat_axis=0, tiled=True)
-        return lax.all_gather(part, "stream", axis=1, tiled=False)
-
-    n, k = ctx_count, stream_count
-    qkv_out = settle(
-        qkv_grad.reshape(3, n, k, slab // k, width).transpose(1, 2, 0, 3, 4)
-    )
-    qkv_out = qkv_out.transpose(2, 1, 3, 0, 4).reshape(3, slab, n * width)
-    up_out = settle(up_grad.reshape(n, k, slab // k, units))
-    up_out = up_out.transpose(1, 2, 0, 3).reshape(slab, n * units)
-    out_out = settle(out_grad.reshape(k, width // k, n, slab).transpose(2, 0, 1, 3))
-    out_out = out_out.reshape(n * width, slab)
-    down_out = settle(down_grad.reshape(k, units // k, n, slab).transpose(2, 0, 1, 3))
-    down_out = down_out.reshape(n * units, slab)
     return (
         output.astype(bf16)[None],
         input_grad[None],
@@ -516,7 +1010,8 @@
 
     def whole(*arrays):
         heads, units = arrays[4].shape[2] // HEAD, arrays[10].shape[1]
-        fits = heads % split == 0 and units % (split * 128 * mesh.shape["stream"]) == 0
+        grouped = (mesh.shape["stream"], mesh.shape["ctx"], mesh.shape["head"]) == (4, 4, 2)
+        fits = grouped and heads == split and units % (split * 128) == 0
         return jax.shard_map(
             per_device if fits else general_device,
             mesh=mesh,

time: 1230 us -> 678 us (0.55)
  waiting for transfers between devices: 812 us -> 112 us
  Pallas kernels: 0 us -> 386 us
  local copies, waits for them, and re-layouts: 134 us -> 30.6 us
  blocking collectives: 86 us -> 0 us
  starting transfers between devices: 27.8 us -> 0.04 us
  matrix products: 109 us -> 95.3 us
    pallas_call x0 -> x2, Pallas kernels: none -> 386 us  [the longest x1 238 us: settle_all(): pl.pallas_call(settle_body, out_shape=[jax.ShapeDtypeStruct(v, bf16) for...]
    all_to_all x5 -> x0, waiting for transfers between devices: 332 us -> none  [the longest x4 321 us: regroup(): lax.all_to_all(piece, 'ctx', split_axis=0, concat_axis=axis, tiled=False)]
    unnamed x18 -> x1, waiting for transfers between devices: 155 us -> 0.02 us
    all_gather x6 -> x0, waiting for transfers between devices: 125 us -> none  [the longest x4 125 us: settle(): return lax.all_gather(part, 'stream', axis=1, tiled=False)]
    all_to_all x3 -> x0, blocking collectives: 86 us -> none  [settle(): part = lax.all_to_all(part, 'ctx', split_axis=0, concat_axis=0, tiled=True)]
    reduce_scatter x2 -> x0, waiting for transfers between devices: 78.3 us -> none  [the longest x1 78.2 us: per_device(): lax.psum_scatter(branches.astype(bf16), 'ctx', scatter_dimension=0, tiled...]
    convert_element_type x7 -> x1, local copies, waits for them, and re-layouts: 49.4 us -> 4.63 us  [per_device(): qkv_grad.astype(bf16)]
    all_to_all x5 -> x0, starting transfers between devices: 26.7 us -> none  [the longest x4 23.3 us: regroup(): lax.all_to_all(piece, 'ctx', split_axis=0, concat_axis=axis, tiled=False)]
  transfers between devices with their start and end apart: 19 -> 1, of which waited for: 15 -> 1; matrix products, arithmetic and copies ran while one was open for 21% -> 3% of each run, Pallas kernels for 0% -> 0%
where the time goes in v2:
time: 678 us; the launch traced here: 668 us
  Pallas kernels  386 us (57%)
  waiting for transfers between devices  112 us (17%)
  matrix products  95.3 us (14%)
  local copies, waits for them, and re-layouts  30.6 us (5%)
  other arithmetic  29.6 us (4%)
  between operations  14.9 us (2%)
    pallas_call x1, Pallas kernels, settle_all(): pl.pallas_call(settle_body, out_shape=[jax.ShapeDtypeStruct(v, bf16) for...  238 us
    pallas_call x1, Pallas kernels, gather_all(): pl.pallas_call(gather_body, out_shape=[jax.ShapeDtypeStruct((4 * count, m...  148 us
    psum x1, waiting for transfers between devices, per_device(): lax.psum((jnp.sum(normed_one_grad * unit, axis=0), jnp.sum(normed_one_gra...  112 us
    unnamed x76, local copies, waits for them, and re-layouts  22.7 us
    dot_general x1, matrix products, per_device(): activated_grad = jnp.dot(upstream, w_down.T, preferred_element_type=f32)  15.8 us
  transfers between devices with their start and end apart: 1, of which 1 were waited for; matrix products, arithmetic and copies ran while one was open for 3% of the time, Pallas kernels for 0%

profile of v2, /device:TPU:0, one launch (start us, length us, event | category | flops | bytes accessed | tf_op | source)
XLA Modules:
  0.0 668.2 jit_solution(7617750649510990069)
XLA Ops:
  7.3 1.2 copy-done
  8.5 1.2 copy-done.5
  9.7 1.9 copy-done.7
  11.6 1.2 copy-done.8
  12.8 147.9 %gather.1 = (bf16[1024,2048]{1,0:T(8,128)(2,1)S(1)}, bf16[1024,2048]{1,0:T(8,128)(2,1)S(1)}, bf16[3,2048,256]{2,1,0:T(8,128)(2,1)S(1)}, bf16[2048,1024]{1,0:T(8,...) custom-call(bf16[256,2048]{1,0:T(8,128)(2,1)S(1)} %bitcast.118, bf16[256,2048]{1,0:T(8,128)(2,1)S(1)} %bitcast.119, ...), custom_call_target="tpu_custom_call" | custom-call | tf_op jit(solution)/shard_map/gather/pallas_call | solution.py:513
  160.7 1.7 copy-done.16
  163.0 1.2 fusion.12
  164.4 1.3 copy-done.13
  166.7 6.8 %add_bitcast_fusion = f32[3,1024,256]{1,2,0:T(8,128)S(1)} fusion(bf16[3,2048,256]{2,1,0:T(8,128)(2,1)} %copy-done.16, f32[3,256]{1,0:T(4,128)S(1)} %dynamic-slice_convert_fusion.1, bf16[1024,2048]{1,0:T(8,128)(2,1)} %copy-done.2, f32[2048]{0:T(1024)S(1)} %convert_element_type.158, f32[2048]{0:T(1024)S(1)} %convert_element_type.157, ...), kind=kOutput, calls=%fused_computation.56 | convolution fusion | flops 3234594816 | bytes 10513408 | tf_op jit(solution)/shard_map/nd,cde->cne/dot_general | solution.py:853
  173.6 2.0 copy-done.14
  175.7 1.4 convolution_convert_fusion.5
  177.8 1.0 fusion.23
  178.8 0.9 fusion.29
  179.6 2.1 fusion.44
  181.8 1.2 fusion.40
  183.0 2.8 multiply_convert_fusion
  185.9 0.7 fusion.38
  186.7 0.7 fusion.39
  188.5 5.7 fusion.98
  194.3 5.4 fusion.24
  200.4 8.3 %fusion.100 = f32[1024,1024]{0,1:T(8,128)S(1)} fusion(bf16[2048,1024]{1,0:T(8,128)(2,1)} %get-tuple-element.29, bf16[1024,2048]{1,0:T(8,128)(2,1)} %copy-done.2, f32[2048]{0:T(1024)S(1)} %convert_element_type.167, f32[2048]{0:T(1024)S(1)} %convert_element_type.166, f32[1024]{0:T(1024)S(1)} %add_rsqrt_fusion, f32[1024]{0:T(1024)S(1)} %broadcast_multiply_fusion.1), kind=kOutput, calls=%fused_computation.173 | convolution fusion | flops 4307550208 | bytes 12607488 | tf_op jit(solution)/shard_map/dot_general | solution.py:872
  208.7 15.8 %convert_reduce_fusion.1 = (f32[1024]{0:T(1024)S(1)}, bf16[1024,1024]{0,1:T(8,128)(2,1)}, f32[1024,1024]{0,1:T(8,128)S(1)}) fusion(f32[1024,1024]{0,1:T(8,128)S(1)} %fusion.100, f32[1024]{0:T(1024)S(1)} %dynamic-slice_convert_fusion, bf16[1024,2048]{1,0:T(8,128)(2,1)S(1)} %copy-done.15, bf16[1024,2048]{1,0:T(8,128)(2,1)S(1)} %copy-done.32), kind=kOutput, calls=%fused_computation.25 | convolution fusion | flops 4373609472 | bytes 18882560 | tf_op jit(solution)/shard_map/dot_general | solution.py:879
  225.2 6.8 %fusion.106 = f32[1024,2048]{1,0:T(8,128)} fusion(bf16[1024,1024]{0,1:T(8,128)(2,1)S(1)} %multiply_convert_fusion.1, bf16[1024,2048]{1,0:T(8,128)(2,1)S(1)} %copy-done.32), kind=kOutput, calls=%fused_computation.175 | convolution fusion | flops 4294967296 | bytes 14680064 | tf_op jit(solution)/shard_map/dot_general | solution.py:874
  232.1 6.2 convolution_convert_fusion
  238.8 4.6 convolution_convert_fusion.3
  243.4 6.8 %add_convert_fusion.bra_ref = bf16[1024,2048]{1,0:T(8,128)(2,1)} fusion(f32[1024,2048]{1,0:T(8,128)} %fusion.106, bf16[256,2048]{1,0:T(8,128)(2,1)S(1)} %get-tuple-element.28, bf16[1024,1,256]{0,2,1:T(8,128)(2,1)S(1)} %copy-done.20), kind=kOutput, calls=%fused_computation.19 | convolution fusion | flops 1077936128 | bytes 14155776 | tf_op jit(solution)/shard_map/dot_general | solution.py:874
  250.2 7.0 %convolution_convert_fusion.1 = bf16[2048,1024]{1,0:T(8,128)(2,1)} fusion(bf16[1024,1024]{0,1:T(8,128)(2,1)S(1)} %copy-done.34, bf16[1024,2048]{1,0:T(8,128)(2,1)S(1)} %copy-done.4, f32[2048]{0:T(1024)S(1)} %convert_element_type.167, f32[2048]{0:T(1024)S(1)} %convert_element_type.166, f32[1024]{0:T(1024)S(1)} %add_rsqrt_fusion, ...), kind=kOutput, calls=%fused_computation.48 | convolution fusion | flops 4309647360 | bytes 10510336 | tf_op jit(solution)/shard_map/dot_general | solution.py:882
  257.2 11.7 %fusion.104 = (f32[2048]{0:T(1024)}, f32[2048]{0:T(1024)}, bf16[1024,2048]{1,0:T(8,128)(2,1)}, f32[2048]{0:T(1024)}, f32[2048]{0:T(1024)}) fusion(f32[1024]{0:T(1024)S(1)} %add_rsqrt_fusion, f32[1024]{0:T(1024)S(1)} %broadcast_multiply_fusion.1, bf16[1024,2048]{1,0:T(8,128)(2,1)S(1)} %copy-done.4, f32[2048]{0:T(1024)S(1)} %convert_element_type.166, ...), kind=kOutput, calls=%fused_computation.174 | convolution fusion | flops 4322222080 | bytes 23126016 | tf_op jit(solution)/shard_map/dot_general | solution.py:906
  268.9 4.6 copy.42
  274.0 1.2 copy-done.11
  275.2 237.8 %settle.1 = (bf16[256,2048]{1,0:T(8,128)(2,1)S(1)}, bf16[256,2048]{1,0:T(8,128)(2,1)S(1)}, bf16[3,4,2,64,1024]{4,3,2,1,0:T(8,128)(2,1)}, bf16[4,2,64,4096]{3,2,1...) custom-call(bf16[1024,2048]{1,0:T(8,128)(2,1)} %add_convert_fusion.bra_ref, ...), custom_call_target="tpu_custom_call" | custom-call | tf_op jit(solution)/shard_map/settle/pallas_call | solution.py:794
  513.0 1.0 copy-done.9
  514.0 1.0 copy-done.12
  515.0 0.7 convert_reduce_fusion.3
  515.7 4.3 convert_reduce_fusion.5
  521.6 5.5 bitcast_convert_fusion.2
  527.1 4.8 bitcast_convert_fusion.1
  531.8 4.9 bitcast_convert_fusion
  536.7 1.7 bitcast_convert_fusion.3
  538.4 112.1 %all-reduce.3.cloned.1.call-done = (f32[2048]{0:T(1024)}, f32[2048]{0:T(1024)}, f32[3,2048]{1,0:T(4,128)}, f32[2048]{0:T(1024)}, f32[2048]{0:T(1024)}, /*index=5*/f32[2048]{0:T(1024)}, f32[8192]{0:T(1024)}) async-done(((f32[2048]{0:T(1024)}, f32[2048]{0:T(1024)}, f32[3,2048]{1,0:T(4,128)}, f32[2048]{0:T(1024)}, f32[2048]{0:T(1024)}, /*index=5*/f32[2048]{0:T(1024)}, f32[8192]{0:T(1024)}), (f32[2048]{0:T(1024)}, ...) | async-done | bytes 98320 | tf_op jit(solution)/shard_map/psum | solution.py:942
  650.5 1.3 constant_dynamic-slice_fusion
  651.8 1.3 dynamic_slice.15
  653.1 1.3 copy.58
  654.4 1.3 copy.59
  655.7 1.3 copy.60
  657.0 1.3 copy.61
  658.3 1.3 copy.62
  659.6 1.3 copy.63
  (98 shorter events, 7.6 us)
Async XLA Ops:
  7.2 643.3 %all-reduce.3.cloned.1.call-start = ((), (), s32[]{:S(2)}) async-start(), calls=%async_computation | async-start | bytes 212992 | tf_op jit(solution)/shard_map/psum | solution.py:942
  7.2 1.2 copy-start
  8.5 1.2 copy-start.5
  9.7 1.9 copy-start.7
  11.6 1.2 copy-start.8
  160.7 1.7 copy-start.16
  162.4 2.0 copy-start.2
  162.4 3.3 copy-start.13
  162.4 3.3 copy-start.33
  162.4 3.6 copy-start.25
  162.4 3.6 copy-start.26
  173.5 2.2 copy-start.14
  183.0 11.2 %copy-start.21 = (bf16[1,1024,256]{1,2,0:T(8,128)(2,1)}, bf16[1,1024,256]{1,2,0:T(8,128)(2,1)S(1)}, u32[]{:S(2)}) copy-start(bf16[1,1024,256]{1,2,0:T(8,128)(2,1)S(1)} %fusion.40) | copy-start | bytes 1572868
  186.6 1.9 copy-start.17
  188.5 5.7 copy-start.3
  194.3 5.4 copy-start.27
  194.3 5.4 copy-start.28
  200.4 8.3 %copy-start.15 = (bf16[1024,2048]{1,0:T(8,128)(2,1)S(1)}, bf16[1024,2048]{1,0:T(8,128)(2,1)}, u32[]{:S(2)}) copy-start(bf16[1024,2048]{1,0:T(8,128)(2,1)} %copy-done.13) | copy-start | bytes 12582916
  200.4 8.3 %copy-start.32 = (bf16[1024,2048]{1,0:T(8,128)(2,1)S(1)}, bf16[1024,2048]{1,0:T(8,128)(2,1)}, u32[]{:S(2)}) copy-start(bf16[1024,2048]{1,0:T(8,128)(2,1)} %get-tuple-element.30) | copy-start | bytes 12582916
  232.0 6.2 copy-start.1
  232.1 6.4 copy-start.22
  238.8 4.6 copy-start.20
  243.4 6.8 %copy-start.4 = (bf16[1024,2048]{1,0:T(8,128)(2,1)S(1)}, bf16[1024,2048]{1,0:T(8,128)(2,1)}, u32[]{:S(2)}) copy-start(bf16[1024,2048]{1,0:T(8,128)(2,1)} %copy-done.2) | copy-start | bytes 12582916
  243.4 6.8 %copy-start.34 = (bf16[1024,1024]{0,1:T(8,128)(2,1)S(1)}, bf16[1024,1024]{0,1:T(8,128)(2,1)}, u32[]{:S(2)}) copy-start(bf16[1024,1024]{0,1:T(8,128)(2,1)} %get-tuple-element.52) | copy-start | bytes 6291460
  250.2 7.0 %copy-start.31 = (bf16[2048,1024]{1,0:T(8,128)(2,1)S(1)}, bf16[2048,1024]{1,0:T(8,128)(2,1)}, u32[]{:S(2)}) copy-start(bf16[2048,1024]{1,0:T(8,128)(2,1)} %get-tuple-element.29) | copy-start | bytes 12582916
  274.0 1.2 copy-start.11
  275.2 240.5 %copy-start.29 = (bf16[2048]{0:T(1024)(128)(2,1)S(1)}, bf16[2048]{0:T(1024)(128)(2,1)}, u32[]{:S(2)}) copy-start(bf16[2048]{0:T(1024)(128)(2,1)} %param.28) | copy-start | bytes 12292
  275.2 240.5 %copy-start.30 = (bf16[2048]{0:T(1024)(128)(2,1)S(1)}, bf16[2048]{0:T(1024)(128)(2,1)}, u32[]{:S(2)}) copy-start(bf16[2048]{0:T(1024)(128)(2,1)} %param.22) | copy-start | bytes 12292
  275.2 240.5 %copy-start.6 = (bf16[1,256,2048]{2,1,0:T(8,128)(2,1)S(1)}, bf16[1,256,2048]{2,1,0:T(8,128)(2,1)}, u32[]{:S(2)}) copy-start(bf16[1,256,2048]{2,1,0:T(8,128)(2,1)} %param.29) | copy-start | bytes 3145732
  513.0 1.0 copy-start.9
  514.0 1.0 copy-start.12
  520.6 0.6 copy-start.24
  520.9 0.6 copy-start.23
  521.6 5.5 copy-start.19
  527.1 4.8 copy-start.18
  531.8 4.9 copy-start.10
Sparse Core Ops, SparseCore 0:
  521.7 128.7 all-reduce.2

commit v3 on v2

--- a/solution.py
+++ b/solution.py
@@ -537,15 +537,25 @@
 
 
 LEADS = (12, 4, 1, 1)
+F32, BF16 = jnp.float32, jnp.bfloat16
+
+
+def dot(a, b, over):
+    return lax.dot_general(a, b, ((over[0:1], over[1:2]), ((), ())), preferred_element_type=F32)
 
 
 def settle_body(
-    bra_ref, inw_ref, g0, g1, g2, g3,
-    joint, inward, o0, o1, o2, o3,
+    act_in, up_in, unit_in, dh_in, dqkv_in, mixed_in, wq_in, wu_in, wo_in, wd_in, cols_ref, rows_ref,
+    joint, inward, o0, o1, o2, o3, small_out,
     s1x_send, s1x_recv, s1y_send, s1y_recv, s2x_send, s2x_recv, s2y_send, s2y_recv,
-    z_send, z_recv, x_send, x_recv, y_send, y_recv, fx_send, fx_recv, fy_send, fy_recv,
-    own_sem, core_send, core_recv, row_send, row_recv, back_send, back_recv, keep_sem, half_sem,
-    *bufs,
+    x_send, x_recv, y_send, y_recv, fx_send, fx_recv, fy_send, fy_recv,
+    z_send, z_recv, keep_sem, load_sem, weight_sem,
+    core_send, core_recv, row_send, row_recv, back_send, back_recv, back_sem,
+    sum_send, sum_recv, sum_sem,
+    act, up, unit, dh, dqkv, mixed, w_wide, w_out, w_qkv,
+    gb0, gb1, gb2, gb3, fa0, fb0, fa1, fb1, fa2, fb2, fa3, fb3, ga0, hb0, ga1, hb1, ga2, hb2, ga3, hb3,
+    own_half, core_half, send_half, row_parts, done_half,
+    sums, sums_core, slots, total_own, total_x, total_y,
 ):
     s, c, h = places()
     x_at, y_at = lax.rem(s, 2), lax.div(s, 2)
@@ -553,36 +563,60 @@
     x_peer, y_peer = y_at * 2 + x_off, y_off * 2 + x_at
     across = ((x_peer, c, h), (y_peer, c, h))
     core_peer = (s, c, 1 - h)
-    ring = [(s, lax.rem(c + k, 4), h) for k in (1, 2, 3)]
-    greet([*across, core_peer, *ring])
-    grads, outs = (g0, g1, g2, g3), (o0, o1, o2, o3)
-    mine = [bufs[2 * m : 2 * m + 2] for m in range(4)]
-    first = [bufs[8 + 2 * m : 10 + 2 * m] for m in range(4)]
-    second = [bufs[16 + 2 * m : 18 + 2 * m] for m in range(4)]
-    own_half, core_half, row_parts, done_half = bufs[24:26], bufs[26:28], bufs[28:30], bufs[30:32]
+    near = (1, 3, 2)
+    greet([*across, core_peer, *[(s, lax.rem(c + k, 4), h) for k in near]])
+    grads, outs = (gb0, gb1, gb2, gb3), (o0, o1, o2, o3)
+    first = ((fa0, fb0), (fa1, fb1), (fa2, fb2), (fa3, fb3))
+    second = ((ga0, hb0), (ga1, hb1), (ga2, hb2), (ga3, hb3))
     slab = o2.shape[-1]
+    length, model = up.shape
+    units, width = act.shape[1], mixed.shape[1]
+    half_cols = model // 2
+    count = joint.shape[0]
+    tile = 256
 
     def remote(src, dst, send, recv, to):
         return pltpu.make_async_remote_copy(
             src_ref=src, dst_ref=dst, send_sem=send, recv_sem=recv, device_id=to, device_id_type=MESH
         )
+
+    loads = [
+        pltpu.make_async_copy(a, b, load_sem.at[i])
+        for i, (a, b) in enumerate(
+            ((act_in, act), (up_in, up), (dh_in, dh), (unit_in, unit), (dqkv_in, dqkv), (mixed_in, mixed))
+        )
+    ]
+    for load in loads:
+        load.start()
+
+    def side(which):
+        return 1 - h if which == 0 else h
+
+    def weight_load(i):
+        at = span(side(i % 2), half_cols)
+        if i < 2:
+            return pltpu.make_async_copy(wd_in.at[:, at], w_wide.at[i], weight_sem.at[i])
+        if i < 4:
+            return pltpu.make_async_copy(wu_in.at[at, :], w_wide.at[i % 2], weight_sem.at[i])
+        if i < 6:
+            return pltpu.make_async_copy(wo_in.at[:, at], w_out.at[i % 2], weight_sem.at[i])
+        return pltpu.make_async_copy(wq_in.at[:, at, :], w_qkv.at[i % 2], weight_sem.at[i])
+
+    for i in (0, 4, 1, 5, 6, 7):
+        weight_load(i).start()
 
     def one(m, half):
         src = grads[m].at[:, :, x_off, 0] if half == 0 else grads[m].at[:, y_off, :, 1]
         send, recv = (s1x_send, s1x_recv) if half == 0 else (s1y_send, s1y_recv)
         return remote(src, first[m][half], send.at[m], recv.at[m], across[half])
 
-    def load(m, half):
-        src = grads[m].at[:, :, x_at, 0] if half == 0 else grads[m].at[:, y_at, :, 1]
-        return pltpu.make_async_copy(src, mine[m][half], own_sem.at[m, half])
-
     def two(m, half):
-        src = mine[m][half].at[:, y_off if half == 0 else x_off]
+        src = first[m][half].at[:, y_off if half == 0 else x_off]
         send, recv = (s2y_send, s2y_recv) if half == 0 else (s2x_send, s2x_recv)
         return remote(src, second[m][half], send.at[m], recv.at[m], across[1 - half])
 
     def add_first(m, half):
-        into, more = mine[m][half], first[m][half]
+        into, more = first[m][half], grads[m]
         lead, _, height, _ = into.shape
         tall = min(height, 32)
 
@@ -591,20 +625,20 @@
             at = lax.rem(i, height // tall)
             pair = lax.div(i, height // tall)
             l, j, rows = lax.div(pair, 2), lax.rem(pair, 2), span(at, tall)
-            total = into[l, j, rows, :].astype(jnp.float32) + more[l, j, rows, :].astype(jnp.float32)
-            into[l, j, rows, :] = total.astype(into.dtype)
+            term = more[l, j, x_at, 0, rows, :] if half == 0 else more[l, y_at, j, 1, rows, :]
+            into[l, j, rows, :] = (into[l, j, rows, :].astype(F32) + term.astype(F32)).astype(BF16)
 
     def add_second(m, half):
-        into, more = second[m][half], mine[m][half]
-        keep = y_at if half == 0 else x_at
+        into, more = second[m][half], first[m][half]
+        mine = y_at if half == 0 else x_at
         lead, height, _ = into.shape
         tall = min(height, 32)
 
         @pl.loop(0, lead * (height // tall))
         def _(i):
             l, rows = lax.div(i, height // tall), span(lax.rem(i, height // tall), tall)
-            total = into[l, rows, :].astype(jnp.float32) + more[l, keep, rows, :].astype(jnp.float32)
-            into[l, rows, :] = total.astype(into.dtype)
+            term = more[l, mine, rows, :].astype(F32)
+            into[l, rows, :] = (into[l, rows, :].astype(F32) + term).astype(BF16)
 
     def share_of(m, half, to):
         ref = second[m][half]
@@ -616,9 +650,9 @@
 
     def home(m, half):
         if m == 0:
-            return outs[0].at[:, s, half, :, span(c, second[0][0].shape[-1])]
+            return outs[0].at[:, s, half, :, span(c, width)]
         if m == 1:
-            return outs[1].at[s, half, :, span(c, second[1][0].shape[-1])]
+            return outs[1].at[s, half, :, span(c, units)]
         return outs[m].at[c, s, half]
 
     def z_copy(m, half, k):
@@ -644,59 +678,207 @@
         here = quarter(m, y_peer if axis == 0 else x_peer, 1 - axis)
         return remote(here, here, send.at[m], recv.at[m], across[axis])
 
-    wholes, sums = (bra_ref, inw_ref), (joint, inward)
-    span_cols = own_half[0].shape[1]
-    count = joint.shape[0]
+    finals = (joint, inward)
 
     def core_copy(a):
-        return remote(
-            wholes[a].at[:, span(1 - h, span_cols)], core_half[a], core_send.at[a], core_recv.at[a], core_peer
-        )
-
-    def half_load(a):
-        return pltpu.make_async_copy(wholes[a].at[:, span(h, span_cols)], own_half[a], half_sem.at[a])
+        return remote(send_half, core_half.at[a], core_send.at[a], core_recv.at[a], core_peer)
 
     def row_copy(a, k):
         to = lax.rem(c + 4 - k, 4)
         return remote(
-            own_half[a].at[span(to, count)], row_parts[a].at[k - 1],
+            own_half.at[a, span(to, count)], row_parts.at[a, k - 1],
             row_send.at[a, k - 1], row_recv.at[a, k - 1], (s, to, h),
         )
 
     def back_copy(a):
-        here = sums[a].at[:, span(h, span_cols)]
-        return remote(done_half[a], here, back_send.at[a], back_recv.at[a], core_peer)
+        return remote(
+            done_half.at[a], finals[a].at[:, span(h, half_cols)], back_send.at[a], back_recv.at[a], core_peer
+        )
 
     def back_keep(a):
-        return pltpu.make_async_copy(done_half[a], sums[a].at[:, span(h, span_cols)], half_sem.at[a])
-
-    order = (3, 1, 0, 2)
-    for m in order:
-        for half in (0, 1):
-            one(m, half).start()
-    for a in (0, 1):
-        core_copy(a).start()
-        half_load(a).start()
-    for m in order:
-        for half in (0, 1):
-            load(m, half).start()
-    for a in (0, 1):
-        half_load(a).wait()
+        return pltpu.make_async_copy(done_half.at[a], finals[a].at[:, span(h, half_cols)], back_sem.at[a])
+
+    def line_start(a):
         core_copy(a).wait_recv()
         tall = 32
 
-        @pl.loop(0, own_half[a].shape[0] // tall)
+        @pl.loop(0, length // tall)
         def _(i):
             rows = span(i, tall)
-            total = own_half[a][rows, :].astype(jnp.float32) + core_half[a][rows, :].astype(jnp.float32)
-            own_half[a][rows, :] = total.astype(own_half[a].dtype)
-
-        for k in (1, 3, 2):
+            own_half[a, rows, :] = (
+                own_half[a, rows, :].astype(F32) + core_half[a, rows, :].astype(F32)
+            ).astype(BF16)
+
+        for k in near:
             row_copy(a, k).start()
+
+    def line_sum(a):
+        for k in near:
+            row_copy(a, k).wait_recv()
+        tall = 32
+
+        @pl.loop(0, count // tall)
+        def _(i):
+            rows = span(i, tall)
+            total = own_half[a, pl.ds(pl.multiple_of(c * count + i * tall, tall), tall), :].astype(F32)
+            for k in range(3):
+                total = total + row_parts[a, k, rows, :].astype(F32)
+            done_half[a, rows, :] = total.astype(BF16)
+
+        back_copy(a).start()
+        back_keep(a).start()
+
+    def down_grad():
+        rows = units // 8
+
+        @pl.loop(0, 4)
+        def _(q):
+            left = act[:, span(q, 2 * rows)]
+            for j in range(model // 512):
+                part = dot(left, up[:, j * 512 : (j + 1) * 512], (0, 0)).astype(BF16)
+                for half in (0, 1):
+                    gb3[0, lax.div(q, 2), lax.rem(q, 2), half, :, j * 512 : (j + 1) * 512] = part[
+                        half * rows : (half + 1) * rows
+                    ]
+
+    def out_grad():
+        rows = width // 8
+        for j in range(model // 512):
+            part = dot(mixed[...], up[:, j * 512 : (j + 1) * 512], (0, 0)).astype(BF16)
+            for i in range(8):
+                gb2[0, i // 4, (i // 2) % 2, i % 2, :, j * 512 : (j + 1) * 512] = part[i * rows : (i + 1) * rows]
+
+    def scaled(part, t, at, column_sum):
+        rows = span(t, tile)
+        return (part * cols_ref[rows, at : at + 1] + cols_ref[rows, at + 1 : at + 2] * column_sum).astype(BF16)
+
+    def column_sum(ref, cols):
+        total = jnp.zeros((1, cols.stop - cols.start), F32)
+        for i in range(length // tile):
+            total = total + jnp.sum(ref[i * tile : (i + 1) * tile, cols].astype(F32), axis=0, keepdims=True)
+        return total
+
+    def up_grad():
+        rows = tile // 4
+
+        @pl.loop(0, model // tile)
+        def _(t):
+            left = unit[:, span(t, tile)]
+            for j in range(units // 512):
+                cols = slice(j * 512, (j + 1) * 512)
+                near_sum = sums[5:6, 3 * width + j * 512 : 3 * width + (j + 1) * 512]
+                part = scaled(dot(left, dh[:, cols], (0, 0)), t, 2, near_sum)
+                for i in range(4):
+                    gb1[lax.div(t, 2), lax.rem(t, 2), i // 2, i % 2, :, cols] = part[i * rows : (i + 1) * rows]
+
+    def qkv_grad():
+        rows = tile // 4
+
+        @pl.loop(0, model // tile)
+        def _(t):
+            left = unit[:, span(t, tile)]
+            for p in range(3):
+                cols = slice(p * width, (p + 1) * width)
+                part = scaled(dot(left, dqkv[:, cols], (0, 0)), t, 0, sums[5:6, cols])
+                for i in range(4):
+                    gb0[p * 4 + lax.div(t, 2), lax.rem(t, 2), i // 2, i % 2] = part[i * rows : (i + 1) * rows]
+
+    def branches(which):
+        into = send_half if which == 0 else own_half.at[0]
+
+        @pl.loop(0, length // tile)
+        def _(i):
+            rows = span(i, tile)
+            for j in range(half_cols // 512):
+                cols = slice(j * 512, (j + 1) * 512)
+                part = dot(mixed[rows, :], w_out[which, :, cols], (1, 0))
+                part = part + dot(act[rows, :], w_wide[which, :, cols], (1, 0))
+                into[rows, cols] = part.astype(BF16)
+
+    def inwards(which):
+        into = send_half if which == 0 else own_half.at[1]
+        base = side(which) * half_cols
+        for j in range(half_cols // 512):
+            cols = slice(j * 512, (j + 1) * 512)
+            far = span(side(which) * (half_cols // 512) + j, 512)
+            zero = jnp.zeros((8, 512), F32)
+
+            def step(i, carry):
+                rows = span(i, tile)
+                one_part = dot(dqkv[rows, 0:width], w_qkv[which, 0, cols, :], (1, 1))
+                for p in (1, 2):
+                    one_part = one_part + dot(
+                        dqkv[rows, p * width : (p + 1) * width], w_qkv[which, p, cols, :], (1, 1)
+                    )
+                two_part = dot(dh[rows, :], w_wide[which, cols, :], (1, 1))
+                into[rows, cols] = (one_part * rows_ref[0:1, far] + two_part * rows_ref[2:3, far]).astype(BF16)
+                place = unit[rows, far].astype(F32)
+
+                def fold(v):
+                    return jnp.sum(v.reshape(tile // 8, 8, 512), axis=0)
+
+                return (
+                    carry[0] + fold(one_part * place),
+                    carry[1] + fold(one_part),
+                    carry[2] + fold(two_part * place),
+                    carry[3] + fold(two_part),
+                )
+
+            found = lax.fori_loop(0, length // tile, step, (zero, zero, zero, zero))
+            for n in range(4):
+                sums[n : n + 1, far] = jnp.sum(found[n], axis=0, keepdims=True)
+
+    def sum_core():
+        return remote(sums, sums_core, sum_send.at[0], sum_recv.at[0], core_peer)
+
+    def sum_line(k):
+        return remote(
+            sums, slots.at[c], sum_send.at[k], sum_recv.at[k], (s, lax.rem(c + 4 - k, 4), h)
+        )
+
+    def sum_x():
+        return remote(total_own, total_x, sum_send.at[4], sum_recv.at[4], across[0])
+
+    def sum_y():
+        return remote(total_own, total_y, sum_send.at[5], sum_recv.at[5], across[1])
+
+    order = (3, 1, 0, 2)
+    loads[0].wait()
+    loads[1].wait()
+    down_grad()
+    one(3, 0).start()
+    one(3, 1).start()
+    sums[4:5, :] = jnp.sum(up[span(c, count), :].astype(F32), axis=0, keepdims=True) * 0.5
+    sums[5:8, :] = jnp.zeros((3, model), F32)
+    loads[2].wait()
+    loads[3].wait()
+    for j in range(units // 512):
+        sums[5:6, 3 * width + j * 512 : 3 * width + (j + 1) * 512] = column_sum(dh, slice(j * 512, (j + 1) * 512))
+    up_grad()
+    one(1, 0).start()
+    one(1, 1).start()
+    loads[4].wait()
+    for p in range(3):
+        sums[5:6, p * width : (p + 1) * width] = column_sum(dqkv, slice(p * width, (p + 1) * width))
+    qkv_grad()
+    one(0, 0).start()
+    one(0, 1).start()
+    loads[5].wait()
+    out_grad()
+    one(2, 0).start()
+    one(2, 1).start()
+    weight_load(0).wait()
+    weight_load(4).wait()
+    branches(0)
+    core_copy(0).start()
+    weight_load(2).start()
+    weight_load(1).wait()
+    weight_load(5).wait()
+    branches(1)
+    weight_load(3).start()
 
     def stage_two(m):
         for half in (0, 1):
-            load(m, half).wait()
             one(m, half).wait_recv()
             add_first(m, half)
             two(m, half).start()
@@ -705,13 +887,13 @@
         for half in (0, 1):
             two(m, half).wait_recv()
             add_second(m, half)
-            for k in (1, 3, 2):
+            for k in near:
                 z_copy(m, half, k).start()
             keep(m, half).start()
 
     def stage_out(m):
         for half in (0, 1):
-            for k in (1, 3, 2):
+            for k in near:
                 z_copy(m, half, k).wait_recv()
             keep(m, half).wait()
         for axis in (0, 1):
@@ -723,86 +905,116 @@
         direct(m, 1).wait_recv()
         onward(m, 0).start()
 
-    def line_sum(a):
-        for k in (1, 3, 2):
-            row_copy(a, k).wait_recv()
-        tall = 32
-
-        @pl.loop(0, count // tall)
-        def _(i):
-            rows = span(i, tall)
-            total = own_half[a][pl.ds(pl.multiple_of(c * count + i * tall, tall), tall), :].astype(jnp.float32)
-            for k in range(3):
-                total = total + row_parts[a][k, rows, :].astype(jnp.float32)
-            done_half[a][rows, :] = total.astype(done_half[a].dtype)
-
-        back_copy(a).start()
-        back_keep(a).start()
-
-    stages = (stage_two, stage_z, stage_out, stage_on)
-    lag = 1
-    for step in range(len(order) + lag * (len(stages) - 1)):
-        for i, stage in enumerate(stages):
-            j = step - i * lag
-            if 0 <= j < len(order):
-                stage(order[j])
-        if step in (2, 3):
-            line_sum(step - 2)
+    stage_two(3)
+    line_start(0)
+    core_copy(0).wait_send()
+    weight_load(2).wait()
+    weight_load(6).wait()
+    inwards(0)
+    core_copy(1).start()
+    weight_load(3).wait()
+    weight_load(7).wait()
+    inwards(1)
+    sum_core().start()
+    stage_two(1)
+    stage_z(3)
+    line_start(1)
+    sum_core().wait()
+    sums[0:5, :] = sums[0:5, :] + sums_core[0:5, :]
+    for k in near:
+        sum_line(k).start()
+    slots[c] = sums[...]
+    stage_two(0)
+    stage_z(1)
+    stage_out(3)
+    line_sum(0)
+    for k in near:
+        sum_line(k).wait()
+    total_own[0:8, :] = slots[0] + slots[1] + slots[2] + slots[3]
+    for i in range(4):
+        total_own[8 + i : 9 + i, :] = slots[i, 5:6, :]
+    total_own[12:16, :] = jnp.zeros((4, model), F32)
+    sum_x().start()
+    stage_two(2)
+    stage_z(0)
+    stage_out(1)
+    stage_on(3)
+    line_sum(1)
+    sum_x().wait()
+    total_own[...] = total_own[...] + total_x[...]
+    sum_y().start()
+    stage_z(2)
+    stage_out(0)
+    stage_on(1)
+    sum_y().wait()
+    total_own[...] = total_own[...] + total_y[...]
+    small_copy = pltpu.make_async_copy(total_own, small_out, sum_sem.at[0])
+    small_copy.start()
+    stage_out(2)
+    stage_on(0)
+    stage_on(2)
     for m in order:
         for axis in (0, 1):
             onward(m, axis).wait_recv()
+    small_copy.wait()
     for a in (0, 1):
         back_copy(a).wait()
         back_keep(a).wait()
-        core_copy(a).wait_send()
-        for k in (1, 2, 3):
+        for k in near:
             row_copy(a, k).wait_send()
+    core_copy(1).wait_send()
     for m in order:
         for half in (0, 1):
             one(m, half).wait_send()
             two(m, half).wait_send()
-            for k in (1, 2, 3):
+            for k in near:
                 z_copy(m, half, k).wait_send()
         for axis in (0, 1):
             direct(m, axis).wait_send()
             onward(m, axis).wait_send()
 
 
-def settle_all(branches, inward, g_qkv, g_up, g_out, g_down):
-    length, model = branches.shape
-    width, units = g_qkv.shape[2], g_up.shape[1]
-    slab, count = model // 4, length // 4
-    bf16 = jnp.bfloat16
+def settle_all(act, up, unit, dh, dqkv, mixed, w_qkv, w_up, w_out, w_down, cols, rows):
+    length, model = up.shape
+    units, width = act.shape[1], mixed.shape[1]
+    slab, count, half = model // 4, length // 4, model // 2
     dma = pltpu.SemaphoreType.DMA
-    rows = (slab // 8, slab // 8, width // 8, units // 8)
-    cols = (width, units, model, model)
-    views = [
-        g.reshape(lead, 2, 2, 2, r, k)
-        for g, lead, r, k in zip((g_qkv, g_up, g_out, g_down), LEADS, rows, cols)
-    ]
+    heights = (slab // 8, slab // 8, width // 8, units // 8)
+    widths = (width, units, model, model)
     out_shapes = [
         (count, model), (count, model),
-        (3, 4, 2, rows[0], 4 * width), (4, 2, rows[1], 4 * units),
-        (4, 4, 2, rows[2], slab), (4, 4, 2, rows[3], slab),
+        (3, 4, 2, heights[0], 4 * width), (4, 2, heights[1], 4 * units),
+        (4, 4, 2, heights[2], slab), (4, 4, 2, heights[3], slab),
     ]
-    pairs = [(l, 2, r, k) for l, r, k in zip(LEADS, rows, cols)]
-    scratch = [dma((4,))] * 8 + [dma((24,))] * 2 + [dma((4,))] * 8
-    scratch += [dma((4, 2)), dma((2,)), dma((2,)), dma((2, 3)), dma((2, 3)), dma((2,)), dma((2,)), dma((4, 2)), dma((2,))]
-    vmem = [p for p in pairs for _ in (0, 1)] * 2 + [(p[0], p[2], p[3]) for p in pairs for _ in (0, 1)]
-    vmem += [(length, model // 2)] * 4 + [(3, count, model // 2)] * 2 + [(count, model // 2)] * 2
-    scratch += [pltpu.VMEM(v, bf16) for v in vmem]
-    joint, inward, q, u, o, d = pl.pallas_call(
+    scratch = [dma((4,))] * 16 + [dma((24,))] * 2 + [dma((4, 2)), dma((6,)), dma((8,))]
+    scratch += [dma((2,)), dma((2,)), dma((2, 3)), dma((2, 3)), dma((2,)), dma((2,)), dma((2,))]
+    scratch += [dma((6,)), dma((6,)), dma((1,))]
+    vmem = [(length, units), (length, model), (length, model), (length, units), (length, 3 * width), (length, width)]
+    vmem += [(2, units, half), (2, width, half), (2, 3, half, width)]
+    shapes = list(zip(LEADS, heights, widths))
+    vmem += [(l, 2, 2, 2, r, k) for l, r, k in shapes]
+    vmem += [(l, 2, r, k) for l, r, k in shapes for _ in (0, 1)]
+    vmem += [(l, r, k) for l, r, k in shapes for _ in (0, 1)]
+    vmem += [(2, length, half), (2, length, half), (length, half), (2, 3, count, half), (2, count, half)]
+    scratch += [pltpu.VMEM(v, BF16) for v in vmem]
+    scratch += [pltpu.VMEM(v, F32) for v in ((8, model), (8, model), (4, 8, model), (16, model), (16, model), (16, model))]
+    any_space = pl.BlockSpec(memory_space=pl.ANY)
+    vmem_space = pl.BlockSpec(memory_space=pltpu.VMEM)
+    joint, inward, q, u, o, d, small = pl.pallas_call(
         settle_body,
-        out_shape=[jax.ShapeDtypeStruct(v, bf16) for v in out_shapes],
-        in_specs=[pl.BlockSpec(memory_space=pl.ANY)] * 6,
-        out_specs=[pl.BlockSpec(memory_space=pl.ANY)] * 6,
+        out_shape=[jax.ShapeDtypeStruct(v, BF16) for v in out_shapes] + [jax.ShapeDtypeStruct((16, model), F32)],
+        in_specs=[any_space] * 10 + [vmem_space] * 2,
+        out_specs=[any_space] * 7,
         scratch_shapes=scratch,
         compiler_params=pltpu.CompilerParams(
-            collective_id=1, has_side_effects=True, vmem_limit_bytes=48 << 20
+            collective_id=1, has_side_effects=True, vmem_limit_bytes=63 << 20
         ),
         name="settle",
-    )(branches, inward, *views)
-    return joint, inward, q.reshape(3, slab, 4 * width), u.reshape(slab, 4 * units), o.reshape(4 * width, slab), d.reshape(4 * units, slab)
+    )(act, up, unit, dh, dqkv, mixed, w_qkv, w_up, w_out, w_down, cols, rows)
+    return (
+        joint, inward, q.reshape(3, slab, 4 * width), u.reshape(slab, 4 * units),
+        o.reshape(4 * width, slab), d.reshape(4 * units, slab), small,
+    )
 
 
 def per_device(
@@ -824,12 +1036,9 @@
 ):
     f32, bf16 = jnp.float32, jnp.bfloat16
     ctx_count = lax.axis_size("ctx")
-    head_count = lax.axis_size("head")
     c = lax.axis_index("ctx")
-    h = lax.axis_index("head")
     count, model = tokens.shape[1], tokens.shape[2]
     length = count * ctx_count
-    slab = model // ctx_count
     width = qkv_weight.shape[2] // ctx_count
     units = up_weight.shape[1] // ctx_count
 
@@ -871,16 +1080,9 @@
     up_part = lax.dynamic_slice_in_dim(up_bias, c * units, units, 0).astype(f32)
     hidden = jnp.dot(low_two, w_up, preferred_element_type=f32) + up_part
     activated = jax.nn.gelu(hidden, approximate=False).astype(bf16)
-    branches = jnp.dot(mixed_low, w_out, preferred_element_type=f32) + jnp.dot(
-        activated, w_down, preferred_element_type=f32
-    )
-
     _, gelu_back = jax.vjp(partial(jax.nn.gelu, approximate=False), hidden)
     activated_grad = jnp.dot(upstream, w_down.T, preferred_element_type=f32)
     hidden_grad = gelu_back(activated_grad)[0].astype(bf16)
-    down_grad = jnp.dot(activated.T, upstream, preferred_element_type=f32)
-    up_grad = jnp.dot(low_two.T, hidden_grad, preferred_element_type=f32)
-    out_grad = jnp.dot(mixed_low.T, upstream, preferred_element_type=f32)
     mixed_grad = (
         jnp.dot(upstream, w_out.T, preferred_element_type=f32)
         .astype(bf16)
@@ -894,25 +1096,29 @@
     )
     key_grad = jnp.einsum("hqk,qhe->khe", score_grad, query, preferred_element_type=f32) * scale
     value_grad = jnp.einsum("hqk,qhe->khe", shares_low, mixed_grad, preferred_element_type=f32)
-    projected_grad = jnp.stack(
+    projected_grad = jnp.concatenate(
         [
             rotary(query_grad, -angles).reshape(length, width),
             rotary(key_grad, -angles).reshape(length, width),
             value_grad.reshape(length, width),
-        ]
+        ],
+        axis=1,
     ).astype(bf16)
-    qkv_grad = jnp.einsum("nd,cne->cde", low_one, projected_grad, preferred_element_type=f32)
-    normed_one_grad = jnp.einsum("cne,cde->nd", projected_grad, w_qkv, preferred_element_type=f32)
-    normed_two_grad = jnp.dot(hidden_grad, w_up.T, preferred_element_type=f32)
-
-    inward = gain_one * normed_one_grad + gain_two * normed_two_grad
-    joint, inward, qkv_out, up_out, out_out, down_out = settle_all(
-        branches.astype(bf16),
-        inward.astype(bf16),
-        qkv_grad.astype(bf16),
-        up_grad.astype(bf16),
-        out_grad.astype(bf16),
-        down_grad.astype(bf16),
+
+    gains = jnp.stack([gain_one, offset_one, gain_two, offset_two])
+    joint, inward, qkv_out, up_out, out_out, down_out, small = settle_all(
+        activated,
+        upstream,
+        unit.astype(bf16),
+        hidden_grad,
+        projected_grad,
+        mixed_low,
+        w_qkv,
+        w_up,
+        w_out,
+        w_down,
+        jnp.pad(gains.T, ((0, 0), (0, 124))),
+        jnp.pad(gains, ((0, 4), (0, 0))),
     )
     joint, inward = joint.astype(f32), inward.astype(f32)
 
@@ -928,32 +1134,10 @@
         - own_unit * jnp.mean(inward * own_unit, axis=-1, keepdims=True)
     )
 
-    bias_grad = jnp.sum(own_upstream, axis=0) * (1.0 / head_count)
-    qkv_small = lax.dynamic_update_slice(
-        jnp.zeros((3, head_count * ctx_count * width), f32),
-        jnp.sum(projected_grad.astype(f32), axis=1),
-        (0, (h * ctx_count + c) * width),
-    )
-    up_small = lax.dynamic_update_slice(
-        jnp.zeros((head_count * ctx_count * units,), f32),
-        jnp.sum(hidden_grad.astype(f32), axis=0),
-        ((h * ctx_count + c) * units,),
-    )
-    small = lax.psum(
-        (
-            jnp.sum(normed_one_grad * unit, axis=0),
-            jnp.sum(normed_one_grad, axis=0),
-            qkv_small,
-            bias_grad,
-            jnp.sum(normed_two_grad * unit, axis=0),
-            jnp.sum(normed_two_grad, axis=0),
-            up_small,
-        ),
-        ("stream", "ctx", "head"),
-    )
-    qkv_bias_grad = lax.dynamic_slice_in_dim(small[2], h * ctx_count * width, ctx_count * width, 1)
-    up_bias_grad = lax.dynamic_slice_in_dim(small[6], h * ctx_count * units, ctx_count * units, 0)
-
+    qkv_bias_grad = (
+        small[8:12, : 3 * width].reshape(ctx_count, 3, width).transpose(1, 0, 2).reshape(3, -1)
+    )
+    up_bias_grad = small[8:12, 3 * width : 3 * width + units].reshape(-1)
     return (
         output.astype(bf16)[None],
         input_grad[None],
@@ -962,13 +1146,13 @@
         qkv_out.astype(f32),
         qkv_bias_grad,
         out_out.astype(f32),
+        small[4],
+        small[2],
         small[3],
-        small[4],
-        small[5],
         up_out.astype(f32),
         up_bias_grad,
         down_out.astype(f32),
-        small[3],
+        small[4],
     )
 
 
@@ -1011,7 +1195,7 @@
     def whole(*arrays):
         heads, units = arrays[4].shape[2] // HEAD, arrays[10].shape[1]
         grouped = (mesh.shape["stream"], mesh.shape["ctx"], mesh.shape["head"]) == (4, 4, 2)
-        fits = grouped and heads == split and units % (split * 128) == 0
+        fits = grouped and heads == split and units % (split * 512) == 0
         return jax.shard_map(
             per_device if fits else general_device,
             mesh=mesh,

time: 678 us -> 535 us (0.79)
  the two profiles are of different devices: /device:TPU:0 before, /device:TPU:26 now
where the time goes in v3:
time: 535 us; the launch traced here: 527 us
  Pallas kernels  428 us (80%)
  other arithmetic  42.5 us (8%)
  matrix products  38.5 us (7%)
  local copies, waits for them, and re-layouts  16 us (3%)
    pallas_call x1, Pallas kernels, settle_all(): pl.pallas_call(settle_body, out_shape=[jax.ShapeDtypeStruct(v, BF16) for...  283 us
    pallas_call x1, Pallas kernels, gather_all(): pl.pallas_call(gather_body, out_shape=[jax.ShapeDtypeStruct((4 * count, m...  145 us
    dot_general x1, matrix products, per_device(): activated_grad = jnp.dot(upstream, w_down.T, preferred_element_type=f32)  18 us
    unnamed x65, local copies, waits for them, and re-layouts  12.7 us

profile of v3, /device:TPU:26, one launch (start us, length us, event | category | flops | bytes accessed | tf_op | source)
XLA Modules:
  0.0 526.9 jit_solution(13661262192154867770)
XLA Ops:
  0.7 1.2 copy-done.3
  1.9 1.2 copy-done.5
  3.1 1.9 copy-done.9
  5.0 1.2 copy-done.13
  6.2 145.3 %gather.1 = (bf16[1024,2048]{1,0:T(8,128)(2,1)S(1)}, bf16[1024,2048]{1,0:T(8,128)(2,1)S(1)}, bf16[3,2048,256]{2,1,0:T(8,128)(2,1)S(1)}, bf16[2048,1024]{1,0:T(8,...) custom-call(bf16[256,2048]{1,0:T(8,128)(2,1)S(1)} %bitcast.114, bf16[256,2048]{1,0:T(8,128)(2,1)S(1)} %bitcast.115, ...), custom_call_target="tpu_custom_call" | custom-call | tf_op jit(solution)/shard_map/gather/pallas_call | solution.py:513
  151.5 1.0 copy-done.11
  152.5 0.6 convert_reduce_fusion
  153.1 1.2 fusion.9
  154.5 1.4 copy-done.7
  155.9 0.7 dynamic-slice_convert_fusion
  156.6 5.8 %add_bitcast_fusion = f32[3,1024,256]{2,1,0:T(8,128)S(1)} fusion(bf16[3,2048,256]{2,1,0:T(8,128)(2,1)S(1)} %get-tuple-element.31.wq_in, bf16[1024,2048]{1,0:T(8,128)(2,1)} %copy-done, f32[2048]{0:T(1024)S(1)} %convert_element_type.144, f32[2048]{0:T(1024)S(1)} %convert_element_type.143, f32[1024]{0:T(1024)S(1)} %add_rsqrt_fusion, ...), kind=kOutput, calls=%fused_computation.53 | convolution fusion | flops 3234594816 | bytes 10513408 | tf_op jit(solution)/shard_map/nd,cde->cne/dot_general | solution.py:1062
  162.6 0.5 copy-done.29
  163.3 2.5 fusion.92
  165.9 0.4 fusion.88
  166.3 1.6 fusion.30
  167.9 2.4 fusion.35
  170.3 2.9 fusion.34
  173.2 1.3 convolution_convert_fusion.1
  174.5 1.5 convert_bitcast_fusion
  176.0 0.8 multiply_convert_fusion
  176.8 0.9 fusion.47
  177.7 1.3 fusion.48
  179.0 2.6 fusion.73
  181.8 0.5 maximum_bitcast_fusion
  182.6 0.5 maximum_bitcast_fusion.1
  183.1 0.9 fusion.49
  184.1 1.3 pad_maximum_fusion.dqkv_in
  185.3 0.4 copy-done.1
  185.8 1.4 copy-done.14
  187.1 6.3 %fusion.14 = f32[1024,1024]{1,0:T(8,128)} fusion(bf16[2048,1024]{1,0:T(8,128)(2,1)S(1)} %copy-done.14, bf16[1024,2048]{1,0:T(8,128)(2,1)S(1)} %copy-done.1, f32[2048]{0:T(1024)S(1)} %convert_element_type.137, f32[2048]{0:T(1024)S(1)} %convert_element_type.136, f32[1024]{0:T(1024)S(1)} %add_rsqrt_fusion, f32[1024]{0:T(1024)S(1)} %broadcast_multiply_fusion), kind=kOutput, calls=%fused_computation.16 | convolution fusion | flops 4307550208 | bytes 12607488 | tf_op jit(solution)/shard_map/dot_general | solution.py:1081
  193.5 0.7 dynamic-slice_convert_fusion.1
  194.2 18.0 %add_convert_fusion = (bf16[1024,1024]{1,0:T(8,128)(2,1)}, f32[1024,1024]{1,0:T(8,128)S(1)}) fusion(f32[1024,1024]{1,0:T(8,128)} %fusion.14, f32[1024]{0:T(1024)S(1)} %dynamic-slice_convert_fusion.1, bf16[1024,2048]{1,0:T(8,128)(2,1)} %copy-done.7, bf16[1024,2048]{1,0:T(8,128)(2,1)} %get-tuple-element.30.wd_in), kind=kOutput, calls=%fused_computation.26 | convolution fusion | flops 4371513344 | bytes 18878464 | tf_op jit(solution)/shard_map/dot_general | solution.py:1084
  212.1 2.5 multiply_convert_fusion.1.act_in
  214.6 2.6 fusion.3.unit_in
  217.7 1.0 pad.8.clone.cols_ref
  218.7 0.6 pad.9.rows_ref
  219.4 283.1 %settle.1 = (bf16[256,2048]{1,0:T(8,128)(2,1)}, bf16[256,2048]{1,0:T(8,128)(2,1)}, bf16[3,4,2,64,1024]{4,3,2,1,0:T(8,128)(2,1)}, bf16[4,2,64,4096]{3,2,1,0:T(8,1...) custom-call(bf16[1024,1024]{1,0:T(8,128)(2,1)} %multiply_convert_fusion.1.ac, ...), custom_call_target="tpu_custom_call" | custom-call | tf_op jit(solution)/shard_map/settle/pallas_call | solution.py:1003
  502.5 6.9 %bitcast_convert_fusion = f32[4096,512]{1,0:T(8,128)} fusion(bf16[4,4,2,128,512]{4,3,2,1,0:T(8,128)(2,1)} %get-tuple-element.39), kind=kLoop, calls=%fused_computation.17 | loop fusion | flops 2097152 | bytes 12582912 | tf_op jit(solution)/shard_map/convert_element_type | solution.py:1154
  509.4 4.8 bitcast_convert_fusion.1
  514.2 3.7 bitcast_convert_fusion.2
  518.1 0.4 fusion.40
  518.5 0.7 convert_reduce_fusion.1
  519.4 2.9 fusion.39
  522.3 1.7 bitcast_convert_fusion.3
  524.0 0.6 fusion.100
  524.6 0.6 copy.79
  525.3 0.6 copy.76
  525.9 0.6 copy.81
  (75 shorter events, 1.8 us)
Async XLA Ops:
  0.6 1.2 copy-start.3
  1.9 1.2 copy-start.5
  3.1 1.9 copy-start.9
  5.0 1.2 copy-start.13
  151.5 1.0 copy-start.11
  152.5 2.0 copy-start
  152.5 3.4 copy-start.7
  152.5 9.9 %copy-start.10 = (bf16[3,2048,256]{2,1,0:T(8,128)(2,1)}, bf16[3,2048,256]{2,1,0:T(8,128)(2,1)S(1)}, u32[]{:S(2)}) copy-start(bf16[3,2048,256]{2,1,0:T(8,128)(2,1)S(1)} %get-tuple-element.31.wq_in) | copy-start | bytes 9437188
  152.5 4.1 copy-start.23
  152.5 4.1 copy-start.24
  162.4 0.7 copy-start.29
  170.3 2.9 copy-start.8
  170.3 2.9 copy-start.12
  182.6 2.8 copy-start.25
  183.1 2.2 copy-start.26
  183.1 2.6 copy-start.1
  183.1 4.0 copy-start.14
  194.2 18.0 %copy-start.16 = (f32[1024,1024]{1,0:T(8,128)S(1)}, f32[1024,1024]{1,0:T(8,128)}, u32[]{:S(2)}) copy-start(f32[1024,1024]{1,0:T(8,128)} %fusion.14) | copy-start | bytes 12582916
  212.1 2.5 copy-start.2
  502.5 6.9 %copy-start.15 = (bf16[4,2,64,4096]{3,2,1,0:T(8,128)(2,1)S(1)}, bf16[4,2,64,4096]{3,2,1,0:T(8,128)(2,1)}, u32[]{:S(2)}) copy-start(bf16[4,2,64,4096]{3,2,1,0:T(8,128)(2,1)} %get-tuple-element.38) | copy-start | bytes 12582916
  509.4 4.8 copy-start.18
  514.2 3.7 copy-start.4
  514.2 4.3 copy-start.17
  517.9 1.4 copy-start.27
  517.9 1.4 copy-start.28
  517.9 1.5 copy-start.6
  517.9 1.6 copy-start.20
  519.2 3.1 copy-start.19
  519.4 4.6 copy-start.21
  524.6 1.8 copy-start.22

commit v4 on v3

--- a/solution.py
+++ b/solution.py
@@ -288,6 +288,11 @@
 
 
 MESH = pl.DeviceIdType.MESH
+F32, BF16 = jnp.float32, jnp.bfloat16
+
+
+def dot(a, b, over):
+    return lax.dot_general(a, b, ((over[0:1], over[1:2]), ((), ())), preferred_element_type=F32)
 
 
 def span(index, size):
@@ -306,11 +311,13 @@
 
 
 def gather_body(
-    x_ref, g_ref, qkv_ref, up_ref, out_ref, down_ref,
+    x_ref, g_ref, qkv_ref, up_ref, out_ref, down_ref, rows_ref, bias_ref, turn_ref, start_ref,
+    g_out, unit_out, act_out, dh_out, dqkv_out, mixed_out, qkv_out, up_out, out_out, down_out,
+    z_send, z_recv, x_send, x_recv, y_send, y_recv, fx_send, fx_recv, fy_send, fy_recv,
+    line_send, line_recv, core_send, core_recv, own_sem, give_sem, block_sem,
     x_all, g_all, qkv_all, up_all, out_all, down_all,
-    z_send, z_recv, x_send, x_recv, y_send, y_recv, fx_send, fx_recv, fy_send, fy_recv,
-    line_send, line_recv, core_send, core_recv, own_sem,
-    *held,
+    low_one, low_two, unit, query, keys, values, act, dh, dqkv, mixed_low,
+    slope, mixed, norm, key_grad, value_grad,
 ):
     s, c, h = places()
     x_peer = s + 1 - 2 * lax.rem(s, 2)
@@ -430,13 +437,6 @@
     near = (1, 3, 2)
     order = [(m, k) for m in (0, 1, 3, 2) for k in near]
 
-    def start_lines():
-        for a in (0, 1):
-            for side in (0, 1):
-                @pl.when(sends(0, side))
-                def _():
-                    line_copy(a, 0, side).start()
-
     def start_z(m):
         for k in near:
             z_copy(m, k).start()
@@ -454,44 +454,221 @@
             direct(m, k, 0).start()
             direct(m, k, 1).start()
 
-    start_z(0)
-    start_lines()
-    start_z(1)
-    sources = [lines[0][0], lines[1][0]] + [piece(m, c) for m in range(4)]
-    ends = [lines[a][1].at[span(c, count), :] for a in (0, 1)] + [whole_piece(m, c) for m in range(4)]
-    ins = [pltpu.make_async_copy(a, b, own_sem.at[i]) for i, (a, b) in enumerate(zip(sources, held))]
-    own = [pltpu.make_async_copy(b, e, own_sem.at[i]) for i, (b, e) in enumerate(zip(held, ends))]
+    ins = [
+        pltpu.make_async_copy(a, b, own_sem.at[i])
+        for i, (a, b) in enumerate(
+            [(lines[a][0], lines[a][1].at[span(c, count), :]) for a in (0, 1)]
+            + [(piece(m, c), whole_piece(m, c)) for m in range(4)]
+        )
+    ]
     for copy in ins:
         copy.start()
-    for copy, out in zip(ins, own):
-        copy.wait()
-        out.start()
-
+    tile = count
+    length, model = x_all.shape
+    rot = turn_ref.shape[2]
+    scale = width**-0.5
+
+    def finish(m):
+        for k in near:
+            onward(m, k, 0).wait_recv()
+            onward(m, k, 1).wait_recv()
+        ins[2 + m].wait()
+
+    def give(i):
+        pairs = (
+            (qkv_all, qkv_out), (up_all, up_out), (out_all, out_out), (down_all, down_out),
+            (act, act_out), (dh, dh_out), (dqkv, dqkv_out), (mixed_low, mixed_out),
+        )
+        return pltpu.make_async_copy(*pairs[i], give_sem.at[i])
+
+    def give_block(a, origin):
+        src, dst = ((unit, unit_out), (g_all, g_out))[a]
+        at = span(origin, tile)
+        return pltpu.make_async_copy(src.at[at, :], dst.at[at, :], block_sem.at[a])
+
+    def blocks_of(t, do):
+        if t == 0:
+            do(c)
+            return
+
+        @pl.loop(0, 2)
+        def _(side):
+            origin = c + t * (2 * side - 1)
+
+            @pl.when((origin >= 0) & (origin <= 3))
+            def _():
+                do(origin)
+
+    def core_wait(a, t):
+        for side in (0, 1):
+            @pl.when(gets(t, side))
+            def _():
+                core_copy(a, t, side).wait_recv()
+
+    def norm_block(origin):
+        tall = 32
+
+        @pl.loop(0, tile // tall)
+        def _(i):
+            at = pl.ds(pl.multiple_of(origin * tile + i * tall, tall), tall)
+            wide = x_all[at, :].astype(F32)
+            centred = wide - jnp.mean(wide, axis=-1, keepdims=True)
+            spread_of = jnp.mean(centred * centred, axis=-1, keepdims=True)
+            found = centred * lax.rsqrt(spread_of + 1e-05)
+            unit[at, :] = found.astype(BF16)
+            low_one[at, :] = (found * rows_ref[0:1, :] + rows_ref[1:2, :]).astype(BF16)
+            low_two[at, :] = (found * rows_ref[2:3, :] + rows_ref[3:4, :]).astype(BF16)
+
+        give_block(0, origin).start()
+
+    def turned(v, at, sign):
+        near_part = v[:, :rot]
+        moved = pltpu.roll(near_part, 32, 1) * turn_ref[1, at, :] + pltpu.roll(near_part, rot - 32, 1) * turn_ref[2, at, :]
+        return jnp.concatenate([near_part * turn_ref[0, at, :] + sign * moved, v[:, rot:]], axis=1)
+
+    def project():
+        @pl.loop(0, length // tile)
+        def _(i):
+            at = span(i, tile)
+            for p, into in enumerate((query, keys, values)):
+                part = dot(low_one[at, :], qkv_all[p], (1, 0)) + bias_ref[0:1, p * width : (p + 1) * width]
+                into[at, :] = (turned(part, at, 1.0) if p < 2 else part).astype(BF16)
+
+    def allowed_of(i, wide):
+        first = lax.broadcasted_iota(jnp.int32, (tile, wide), 1)
+        place = i * tile + lax.broadcasted_iota(jnp.int32, (tile, wide), 0)
+        return (first <= place) & (first >= start_ref[span(i, tile), :])
+
+    def attend(i):
+        wide = (i + 1) * tile
+        at = slice(i * tile, wide)
+        scores = dot(query[at, :], keys[0:wide, :], (1, 1)) * scale
+        allowed = allowed_of(i, wide)
+        masked = jnp.where(allowed, scores, -1e30)
+        peak = jnp.max(masked, axis=-1, keepdims=True)
+        raised = jnp.where(allowed, jnp.exp(masked - peak), 0.0)
+        total = jnp.sum(raised, axis=-1, keepdims=True)
+        norm[at, :] = peak + jnp.log(total)
+        found = dot((raised / total).astype(BF16), values[0:wide, :], (1, 0))
+        mixed[at, :] = found
+        mixed_low[at, :] = found.astype(BF16)
+
+    def feed(i):
+        at = span(i, tile)
+        for j in range(units // 256):
+            cols = slice(j * 256, (j + 1) * 256)
+            hidden = dot(low_two[at, :], up_all[:, cols], (1, 0)) + bias_ref[1:2, cols]
+            share = 0.5 + 0.5 * lax.erf(hidden * (0.5**0.5))
+            act[at, cols] = (hidden * share).astype(BF16)
+            slope[at, cols] = share + hidden * jnp.exp(-0.5 * hidden * hidden) * ((0.5 / jnp.pi) ** 0.5)
+
+    def back_attend(origin):
+        at = span(origin, tile)
+        grad = dot(g_all[at, :], out_all[...], (1, 1)).astype(BF16)
+        scores = dot(query[at, :], keys[...], (1, 1)) * scale
+        shares = jnp.where(allowed_of(origin, length), jnp.exp(scores - norm[at, :]), 0.0)
+        delta = jnp.sum(grad.astype(F32) * mixed[at, :], axis=-1, keepdims=True)
+        share_grad = dot(grad, values[...], (1, 1))
+        score_grad = (shares * (share_grad - delta)).astype(BF16)
+        value_grad[...] += dot(shares.astype(BF16), grad, (0, 0))
+        key_grad[...] += dot(score_grad, query[at, :], (0, 0))
+        part = dot(score_grad, keys[...], (1, 0)) * scale
+        dqkv[at, 0:width] = turned(part, at, -1.0).astype(BF16)
+
+    def back_feed(origin):
+        at = span(origin, tile)
+        for j in range(units // 256):
+            cols = slice(j * 256, (j + 1) * 256)
+            part = dot(g_all[at, :], down_all[cols, :], (1, 1))
+            dh[at, cols] = (part * slope[at, cols]).astype(BF16)
+
+    def start_line(a):
+        for side in (0, 1):
+            @pl.when(sends(0, side))
+            def _():
+                line_copy(a, 0, side).start()
+
+    start_line(0)
+    start_z(0)
+    key_grad[...] = jnp.zeros_like(key_grad)
+    value_grad[...] = jnp.zeros_like(value_grad)
+    ins[0].wait()
+    norm_block(c)
+    line_step(0, 1)
+    start_z(1)
+    core_wait(0, 1)
+    blocks_of(1, norm_block)
     spread(0)
-    line_step(0, 1)
+    line_step(0, 2)
+    start_z(3)
+    pass_on(0)
+    core_wait(0, 2)
+    blocks_of(2, norm_block)
+    line_step(0, 3)
+    start_line(1)
+    core_wait(0, 3)
+    blocks_of(3, norm_block)
+    finish(0)
+    give(0).start()
+    project()
+    spread(1)
+    start_z(2)
+    for i in range(4):
+        attend(i)
+        if i == 1:
+            pass_on(1)
+    give(7).start()
+    finish(1)
+    give(1).start()
     line_step(1, 1)
-    start_z(3)
-    spread(1)
-    pass_on(0)
-    start_z(2)
-    line_step(0, 2)
-    line_step(1, 2)
-    spread(3)
-    pass_on(1)
-    spread(2)
-    pass_on(3)
-    line_step(0, 3)
+    for i in range(4):
+        feed(i)
+        if i == 0:
+            spread(3)
+        if i == 2:
+            spread(2)
+            line_step(1, 2)
+            pass_on(3)
+    give(4).start()
+    pass_on(2)
     line_step(1, 3)
-    pass_on(2)
-    for m, k in order:
-        onward(m, k, 0).wait_recv()
-        onward(m, k, 1).wait_recv()
+    finish(2)
+    give(2).start()
+    ins[1].wait()
+    give_block(1, c).start()
+    back_attend(c)
+    core_wait(1, 1)
+    blocks_of(1, back_attend)
+    finish(3)
+    give(3).start()
+    back_feed(c)
+    blocks_of(1, back_feed)
+    core_wait(1, 2)
+
+    def both(origin):
+        back_attend(origin)
+        back_feed(origin)
+
+    blocks_of(2, both)
+    core_wait(1, 3)
+    blocks_of(3, both)
+
+    @pl.loop(0, length // tile)
+    def _(i):
+        at = span(i, tile)
+        dqkv[at, width : 2 * width] = turned(key_grad[at, :] * scale, at, -1.0).astype(BF16)
+        dqkv[at, 2 * width : 3 * width] = value_grad[at, :].astype(BF16)
+
+    give(5).start()
+    give(6).start()
+    for t in (1, 2, 3):
+        blocks_of(t, lambda origin: give_block(1, origin).start())
     for a in (0, 1):
         for side in (0, 1):
             for t in (1, 2, 3):
                 @pl.when(gets(t, side))
                 def _():
-                    core_copy(a, t, side).wait()
+                    core_copy(a, t, side).wait_send()
                 @pl.when(sends(t - 1, side))
                 def _():
                     line_copy(a, t - 1, side).wait_send()
@@ -500,49 +677,43 @@
         for axis in (0, 1):
             direct(m, k, axis).wait_send()
             onward(m, k, axis).wait_send()
-    for copy in own:
-        copy.wait()
-
-
-def gather_all(tokens, cotangent, w_qkv, w_up, w_out, w_down):
+    pltpu.make_async_copy(unit, unit_out, block_sem.at[0]).wait()
+    pltpu.make_async_copy(g_all, g_out, block_sem.at[1]).wait()
+    for i in range(8):
+        give(i).wait()
+
+
+def gather_all(tokens, cotangent, w_qkv, w_up, w_out, w_down, rows, bias, turn, starts):
     count, model = tokens.shape
-    slab = w_up.shape[0]
+    length = 4 * count
     width, units = w_out.shape[0] // 4, w_down.shape[0] // 4
-    bf16 = jnp.bfloat16
     dma = pltpu.SemaphoreType.DMA
+    weights = [(3, model, width), (model, units), (width, model), (units, model)]
+    wide, narrow = (length, model), (length, width)
+    results = [wide, wide, (length, units), (length, units), (length, 3 * width), narrow] + weights
+    scratch = [dma((4, 3))] * 10 + [dma((2, 2, 3))] * 4 + [dma((6,)), dma((8,)), dma((2,))]
+    scratch += [
+        pltpu.VMEM(v, BF16)
+        for v in [wide, wide] + weights + [wide] * 3 + [narrow] * 3
+        + [(length, units)] * 2 + [(length, 3 * width), narrow]
+    ]
+    scratch += [pltpu.VMEM(v, F32) for v in ((length, units), narrow, (length, 1), narrow, narrow)]
+    any_space = pl.BlockSpec(memory_space=pl.ANY)
+    vmem_space = pl.BlockSpec(memory_space=pltpu.VMEM)
     return pl.pallas_call(
         gather_body,
-        out_shape=[
-            jax.ShapeDtypeStruct((4 * count, model), bf16),
-            jax.ShapeDtypeStruct((4 * count, model), bf16),
-            jax.ShapeDtypeStruct((3, model, width), bf16),
-            jax.ShapeDtypeStruct((model, units), bf16),
-            jax.ShapeDtypeStruct((width, model), bf16),
-            jax.ShapeDtypeStruct((units, model), bf16),
-        ],
-        in_specs=[pl.BlockSpec(memory_space=pl.ANY)] * 6,
-        out_specs=[pl.BlockSpec(memory_space=pl.ANY)] * 6,
-        scratch_shapes=[dma((4, 3))] * 10 + [dma((2, 2, 3))] * 4 + [dma((6,))]
-        + [
-            pltpu.VMEM(shape, bf16)
-            for shape in (
-                (count, model), (count, model), (3, slab, width), (slab, units), (width, slab), (units, slab)
-            )
-        ],
+        out_shape=[jax.ShapeDtypeStruct(v, BF16) for v in results],
+        in_specs=[any_space] * 6 + [vmem_space] * 4,
+        out_specs=[any_space] * 10,
+        scratch_shapes=scratch,
         compiler_params=pltpu.CompilerParams(
-            collective_id=0, has_side_effects=True, vmem_limit_bytes=32 << 20
+            collective_id=0, has_side_effects=True, vmem_limit_bytes=63 << 20
         ),
         name="gather",
-    )(tokens, cotangent, w_qkv, w_up, w_out, w_down)
+    )(tokens, cotangent, w_qkv, w_up, w_out, w_down, rows, bias, turn, starts)
 
 
 LEADS = (12, 4, 1, 1)
-F32, BF16 = jnp.float32, jnp.bfloat16
-
-
-def dot(a, b, over):
-    return lax.dot_general(a, b, ((over[0:1], over[1:2]), ((), ())), preferred_element_type=F32)
-
 
 def settle_body(
     act_in, up_in, unit_in, dh_in, dqkv_in, mixed_in, wq_in, wu_in, wo_in, wd_in, cols_ref, rows_ref,
@@ -917,16 +1088,14 @@
     inwards(1)
     sum_core().start()
     stage_two(1)
-    stage_z(3)
-    line_start(1)
+    stage_two(0)
     sum_core().wait()
     sums[0:5, :] = sums[0:5, :] + sums_core[0:5, :]
     for k in near:
         sum_line(k).start()
     slots[c] = sums[...]
-    stage_two(0)
-    stage_z(1)
-    stage_out(3)
+    stage_z(3)
+    stage_two(2)
     line_sum(0)
     for k in near:
         sum_line(k).wait()
@@ -935,24 +1104,26 @@
         total_own[8 + i : 9 + i, :] = slots[i, 5:6, :]
     total_own[12:16, :] = jnp.zeros((4, model), F32)
     sum_x().start()
-    stage_two(2)
+    stage_z(1)
     stage_z(0)
-    stage_out(1)
-    stage_on(3)
-    line_sum(1)
+    stage_z(2)
+    line_start(1)
+    stage_out(3)
     sum_x().wait()
     total_own[...] = total_own[...] + total_x[...]
     sum_y().start()
-    stage_z(2)
-    stage_out(0)
-    stage_on(1)
+    stage_on(3)
+    stage_out(1)
     sum_y().wait()
     total_own[...] = total_own[...] + total_y[...]
     small_copy = pltpu.make_async_copy(total_own, small_out, sum_sem.at[0])
     small_copy.start()
+    stage_on(1)
+    stage_out(0)
+    stage_on(0)
     stage_out(2)
-    stage_on(0)
     stage_on(2)
+    line_sum(1)
     for m in order:
         for axis in (0, 1):
             onward(m, axis).wait_recv()
@@ -1042,74 +1213,51 @@
     width = qkv_weight.shape[2] // ctx_count
     units = up_weight.shape[1] // ctx_count
 
-    all_tokens, upstream, w_qkv, w_up, w_out, w_down = gather_all(
-        tokens[0], cotangent[0], qkv_weight, up_weight, out_weight, down_weight
-    )
-
-    gain_one, offset_one = ln1_gain.astype(f32), ln1_bias.astype(f32)
-    gain_two, offset_two = ln2_gain.astype(f32), ln2_bias.astype(f32)
-    wide = all_tokens.astype(f32)
-    centred = wide - jnp.mean(wide, axis=-1, keepdims=True)
-    scale_of = lax.rsqrt(jnp.mean(centred * centred, axis=-1, keepdims=True) + 1e-05)
-    unit = centred * scale_of
-    low_one = (unit * gain_one + offset_one).astype(bf16)
-    low_two = (unit * gain_two + offset_two).astype(bf16)
-
+    gains = jnp.stack([ln1_gain, ln1_bias, ln2_gain, ln2_bias]).astype(f32)
+    gain_rows = jnp.pad(gains, ((0, 4), (0, 0)))
+    biases = jnp.stack(
+        [
+            jnp.pad(
+                lax.dynamic_slice_in_dim(qkv_bias, c * width, width, 1).reshape(-1),
+                (0, units - 3 * width),
+            ),
+            lax.dynamic_slice_in_dim(up_bias, c * units, units, 0),
+        ]
+    ).astype(f32)
+    biases = jnp.pad(biases, ((0, 6), (0, 0)))
     positions, starts = token_places(doc_lengths[0], length)
+    half = ROT // 2
+    lane = jnp.arange(2 * ROT)
     frequency = 10000.0 ** (-jnp.arange(0, ROT, 2, dtype=f32) / ROT)
     angles = (positions - starts).astype(f32)[:, None] * frequency[None, :]
-    bias = lax.dynamic_slice_in_dim(qkv_bias, c * width, width, 1).astype(f32)
-    projected = jnp.einsum("nd,cde->cne", low_one, w_qkv, preferred_element_type=f32)
-    projected = projected + bias[:, None, :]
-    heads = width // HEAD
-    query = rotary(projected[0].reshape(length, heads, HEAD), angles).astype(bf16)
-    keys = rotary(projected[1].reshape(length, heads, HEAD), angles).astype(bf16)
-    values = projected[2].reshape(length, heads, HEAD).astype(bf16)
-    scale = HEAD ** (-0.5)
-    allowed = (positions[None, :] <= positions[:, None]) & (positions[None, :] >= starts[:, None])
-    scores = jnp.einsum("qhe,khe->hqk", query, keys, preferred_element_type=f32) * scale
-    masked = jnp.where(allowed[None], scores, -1e30)
-    raised = jnp.where(
-        allowed[None], jnp.exp(masked - jnp.max(masked, axis=-1, keepdims=True)), 0.0
-    )
-    shares = raised / jnp.sum(raised, axis=-1, keepdims=True)
-    shares_low = shares.astype(bf16)
-    mixed = jnp.einsum("hqk,khe->qhe", shares_low, values, preferred_element_type=f32)
-    mixed_low = mixed.reshape(length, width).astype(bf16)
-
-    up_part = lax.dynamic_slice_in_dim(up_bias, c * units, units, 0).astype(f32)
-    hidden = jnp.dot(low_two, w_up, preferred_element_type=f32) + up_part
-    activated = jax.nn.gelu(hidden, approximate=False).astype(bf16)
-    _, gelu_back = jax.vjp(partial(jax.nn.gelu, approximate=False), hidden)
-    activated_grad = jnp.dot(upstream, w_down.T, preferred_element_type=f32)
-    hidden_grad = gelu_back(activated_grad)[0].astype(bf16)
-    mixed_grad = (
-        jnp.dot(upstream, w_out.T, preferred_element_type=f32)
-        .astype(bf16)
-        .reshape(length, heads, HEAD)
-    )
-    delta = jnp.sum(mixed_grad.astype(f32) * mixed, axis=-1).T
-    share_grad = jnp.einsum("qhe,khe->hqk", mixed_grad, values, preferred_element_type=f32)
-    score_grad = (shares * (share_grad - delta[..., None])).astype(bf16)
-    query_grad = (
-        jnp.einsum("hqk,khe->qhe", score_grad, keys, preferred_element_type=f32) * scale
-    )
-    key_grad = jnp.einsum("hqk,qhe->khe", score_grad, query, preferred_element_type=f32) * scale
-    value_grad = jnp.einsum("hqk,qhe->khe", shares_low, mixed_grad, preferred_element_type=f32)
-    projected_grad = jnp.concatenate(
+    cosine, sine = jnp.tile(jnp.cos(angles), (1, 4)), jnp.tile(jnp.sin(angles), (1, 4))
+    turn = jnp.stack(
         [
-            rotary(query_grad, -angles).reshape(length, width),
-            rotary(key_grad, -angles).reshape(length, width),
-            value_grad.reshape(length, width),
-        ],
-        axis=1,
-    ).astype(bf16)
-
-    gains = jnp.stack([gain_one, offset_one, gain_two, offset_two])
+            jnp.where(lane < ROT, cosine, 1.0),
+            jnp.where((lane >= half) & (lane < ROT), sine, 0.0),
+            jnp.where(lane < half, -sine, 0.0),
+        ]
+    )
+
+    upstream, unit, activated, hidden_grad, projected_grad, mixed_low, w_qkv, w_up, w_out, w_down = (
+        gather_all(
+            tokens[0],
+            cotangent[0],
+            qkv_weight,
+            up_weight,
+            out_weight,
+            down_weight,
+            gain_rows,
+            biases,
+            turn,
+            starts[:, None],
+        )
+    )
+
     joint, inward, qkv_out, up_out, out_out, down_out, small = settle_all(
         activated,
         upstream,
-        unit.astype(bf16),
+        unit,
         hidden_grad,
         projected_grad,
         mixed_low,
@@ -1118,7 +1266,7 @@
         w_out,
         w_down,
         jnp.pad(gains.T, ((0, 0), (0, 124))),
-        jnp.pad(gains, ((0, 4), (0, 0))),
+        gain_rows,
     )
     joint, inward = joint.astype(f32), inward.astype(f32)
 

time: 535 us -> 448 us (0.84)
  the two profiles are of different devices: /device:TPU:26 before, /device:TPU:0 now
where the time goes in v4:
time: 448 us; the launch traced here: 447 us
  Pallas kernels  413 us (92%)
  other arithmetic  24.7 us (6%)
  local copies, waits for them, and re-layouts  8.06 us (2%)
    pallas_call x1, Pallas kernels, settle_all(): pl.pallas_call(settle_body, out_shape=[jax.ShapeDtypeStruct(v, BF16) for...  232 us
    pallas_call x1, Pallas kernels, gather_all(): pl.pallas_call(gather_body, out_shape=[jax.ShapeDtypeStruct(v, BF16) for...  181 us

profile of v4, /device:TPU:0, one launch (start us, length us, event | category | flops | bytes accessed | tf_op | source)
XLA Modules:
  0.0 446.9 jit_solution(17368397993293884612)
XLA Ops:
  0.6 0.0 copy-start
  0.7 0.7 copy-done
  1.4 0.7 dynamic_slice.7
  2.1 0.6 fusion.16.bias_ref
  2.7 0.8 select_reduce_fusion.1
  3.5 0.1 select_reduce_fusion
  3.6 0.5 multiply_cosine_fusion
  4.2 0.2 copy.37
  4.4 0.1 broadcast_select_fusion
  4.5 0.2 copy.36
  4.8 0.0 copy-start.11
  4.8 0.0 copy-start.12
  4.8 0.0 copy-start.13
  4.8 0.0 copy-start.14
  4.9 1.2 pad_maximum_fusion.turn_ref
  6.1 0.0 copy-done.11
  6.1 0.0 copy-done.12
  6.1 0.0 copy-done.13
  6.2 0.0 copy-done.14
  6.2 0.6 pad.18.rows_ref
  6.9 1.0 copy.39.start_ref
  7.9 180.8 %gather.1 = (bf16[1024,2048]{1,0:T(8,128)(2,1)}, bf16[1024,2048]{1,0:T(8,128)(2,1)}, bf16[1024,1024]{1,0:T(8,128)(2,1)}, bf16[1024,1024]{1,0:T(8,128)(2,1)}, bf1...) custom-call(bf16[256,2048]{1,0:T(8,128)(2,1)} %bitcast.45, ...), custom_call_target="tpu_custom_call" | custom-call | tf_op jit(solution)/shard_map/gather/pallas_call | solution.py:703
  188.7 0.4 copy.41
  189.1 1.0 pad.22.clone.cols_ref
  190.1 232.3 %settle.1 = (bf16[256,2048]{1,0:T(8,128)(2,1)}, bf16[256,2048]{1,0:T(8,128)(2,1)}, bf16[3,4,2,64,1024]{4,3,2,1,0:T(8,128)(2,1)}, bf16[4,2,64,4096]{3,2,1,0:T(8,1...) custom-call(bf16[1024,1024]{1,0:T(8,128)(2,1)} %get-tuple-element.31.act_in,, ...), custom_call_target="tpu_custom_call" | custom-call | tf_op jit(solution)/shard_map/settle/pallas_call | solution.py:1174
  422.4 0.0 copy-start.3
  422.5 6.9 %bitcast_convert_fusion = f32[4096,512]{1,0:T(8,128)} fusion(bf16[4,4,2,128,512]{4,3,2,1,0:T(8,128)(2,1)} %get-tuple-element.47), kind=kLoop, calls=%fused_computation | loop fusion | flops 2097152 | bytes 12582912 | tf_op jit(solution)/shard_map/convert_element_type | solution.py:1302
  429.4 0.0 copy-done.3
  429.4 4.8 %bitcast_convert_fusion.1 = f32[512,4096]{1,0:T(8,128)} fusion(bf16[4,2,64,4096]{3,2,1,0:T(8,128)(2,1)S(1)} %copy-done.3), kind=kLoop, calls=%fused_computation.1 | loop fusion | flops 2097152 | bytes 12582912 | tf_op jit(solution)/shard_map/convert_element_type | solution.py:1300
  434.2 0.0 copy-done.6
  434.2 3.7 bitcast_convert_fusion.2
  437.8 0.0 copy-done.2
  437.8 0.0 copy-start.4
  437.8 0.0 copy-start.8
  437.8 0.2 convert_reduce_fusion.1
  438.1 0.4 fusion.7
  438.5 0.5 copy-done.5
  439.0 0.7 convert_reduce_fusion
  439.8 0.0 copy-done.15
  439.8 0.0 copy-done.16
  439.8 0.0 copy-start.1
  439.8 2.9 fusion.6
  442.7 1.7 bitcast_convert_fusion.3
  444.4 0.0 copy-done.9
  444.4 0.6 fusion.18
  445.0 0.6 copy.45
  445.7 0.6 copy.42
  446.3 0.6 copy.47
  (38 shorter events, 0.3 us)
Async XLA Ops:
  0.6 0.7 copy-start
  4.8 1.3 copy-start.11
  4.8 1.3 copy-start.12
  4.8 1.4 copy-start.13
  4.8 1.4 copy-start.14
  422.4 6.9 %copy-start.3 = (bf16[4,2,64,4096]{3,2,1,0:T(8,128)(2,1)S(1)}, bf16[4,2,64,4096]{3,2,1,0:T(8,128)(2,1)}, u32[]{:S(2)}) copy-start(bf16[4,2,64,4096]{3,2,1,0:T(8,128)(2,1)} %get-tuple-element.46) | copy-start | bytes 12582916
  429.4 4.8 %copy-start.6 = (bf16[3,4,2,64,1024]{4,3,2,1,0:T(8,128)(2,1)S(1)}, bf16[3,4,2,64,1024]{4,3,2,1,0:T(8,128)(2,1)}, u32[]{:S(2)}) copy-start(bf16[3,4,2,64,1024]{4,3,2,1,0:T(8,128)(2,1)} %get-tuple-element.44) | copy-start | bytes 9437188
  434.2 3.7 copy-start.2
  437.8 1.2 copy-start.5
  437.8 1.9 copy-start.15
  437.8 2.0 copy-start.16
  437.8 2.0 copy-start.4
  437.8 2.0 copy-start.8
  439.8 2.9 copy-start.7
  439.8 7.0 %copy-start.1 = (bf16[3,1024]{1,0:T(4,128)(2,1)S(1)}, bf16[3,1024]{1,0:T(4,128)(2,1)}, u32[]{:S(2)}) copy-start(bf16[3,1024]{1,0:T(4,128)(2,1)} %param.20) | copy-start | bytes 18436
  442.7 1.7 copy-start.9
  445.0 1.8 copy-start.10

commit v5 on v4

--- a/solution.py
+++ b/solution.py
@@ -3,6 +3,7 @@
 
 import jax
 import jax.numpy as jnp
+import numpy as np
 from jax import lax
 from jax.experimental import pallas as pl
 from jax.experimental.pallas import tpu as pltpu
@@ -282,12 +283,11 @@
     )
 
 
-def token_places(doc_sizes, length):
-    positions = jnp.arange(length, dtype=jnp.int32)
-    return positions, doc_starts(doc_sizes, positions)
-
-
 MESH = pl.DeviceIdType.MESH
+FRONT_PLAN = (
+    "z0", "z1", "l0", "P", "T", "N0", "s0", "z3", "s1", "p0", "L01", "z2", "p1", "N1", "L02", "l1", "s3", "N2", "L03", "p3", "s2", "N3", "f0", "Q", "L11", "p2", "A0", "A1", "A2",
+    "A3", "L12", "f1", "F0", "F1", "F2", "F3", "L13", "f2", "B0", "B1", "f3", "D0", "D1", "B2", "D2", "B3", "D3", "E",
+)
 F32, BF16 = jnp.float32, jnp.bfloat16
 
 
@@ -311,13 +311,15 @@
 
 
 def gather_body(
-    x_ref, g_ref, qkv_ref, up_ref, out_ref, down_ref, rows_ref, bias_ref, turn_ref, start_ref,
+    x_ref, g_ref, qkv_ref, up_ref, out_ref, down_ref,
+    gain_a_ref, off_a_ref, gain_b_ref, off_b_ref, qkv_bias_ref, up_bias_ref, rate_in, docs_ref,
     g_out, unit_out, act_out, dh_out, dqkv_out, mixed_out, qkv_out, up_out, out_out, down_out,
     z_send, z_recv, x_send, x_recv, y_send, y_recv, fx_send, fx_recv, fy_send, fy_recv,
-    line_send, line_recv, core_send, core_recv, own_sem, give_sem, block_sem,
+    line_send, line_recv, core_send, core_recv, own_sem, give_sem, block_sem, small_sem,
     x_all, g_all, qkv_all, up_all, out_all, down_all,
     low_one, low_two, unit, query, keys, values, act, dh, dqkv, mixed_low,
-    slope, mixed, norm, key_grad, value_grad,
+    slope, mixed, norm, key_grad, value_grad, turn_ref, start_ref,
+    gain_a, off_a, gain_b, off_b, qkv_bias, up_bias, rate_ref, rows_ref, bias_ref,
 ):
     s, c, h = places()
     x_peer = s + 1 - 2 * lax.rem(s, 2)
@@ -466,6 +468,7 @@
     tile = count
     length, model = x_all.shape
     rot = turn_ref.shape[2]
+    span_rot = rot // 4
     scale = width**-0.5
 
     def finish(m):
@@ -521,9 +524,52 @@
 
         give_block(0, origin).start()
 
+    smalls = [
+        pltpu.make_async_copy(a, b, small_sem.at[i])
+        for i, (a, b) in enumerate(
+            (
+                (gain_a_ref, gain_a), (off_a_ref, off_a), (gain_b_ref, gain_b), (off_b_ref, off_b),
+                (qkv_bias_ref, qkv_bias), (up_bias_ref, up_bias), (rate_in, rate_ref),
+            )
+        )
+    ]
+    for copy in smalls:
+        copy.start()
+
+    def parameters():
+        for copy in smalls:
+            copy.wait()
+        for i, ref in enumerate((gain_a, off_a, gain_b, off_b)):
+            rows_ref[i : i + 1, :] = ref[...].astype(F32).reshape(1, model)
+        part = qkv_bias[:, span(c, width)].astype(F32)
+        for p in range(3):
+            bias_ref[0:1, p * width : (p + 1) * width] = part[p : p + 1]
+        bias_ref[1:2, :] = up_bias[span(c, units)].astype(F32).reshape(1, units)
+
+    def tables():
+        starts, total = [], docs_ref[0, 0] * 0
+        for j in range(docs_ref.shape[1]):
+            starts.append(total)
+            total = total + docs_ref[0, j]
+
+        @pl.loop(0, length // tile)
+        def _(i):
+            at = span(i, tile)
+            place = i * tile + lax.broadcasted_iota(jnp.int32, (tile, rot), 0)
+            lane = lax.broadcasted_iota(jnp.int32, (tile, rot), 1)
+            first = jnp.zeros((tile, rot), jnp.int32)
+            for start in starts:
+                first = jnp.where(start <= place, jnp.maximum(first, start), first)
+            start_ref[at, :] = first[:, 0:1]
+            angle = (place - first).astype(F32) * rate_ref[0:1, :]
+            sine = jnp.sin(angle)
+            turn_ref[0, at, :] = jnp.where(lane < 2 * span_rot, jnp.cos(angle), 1.0)
+            turn_ref[1, at, :] = jnp.where((lane >= span_rot) & (lane < 2 * span_rot), sine, 0.0)
+            turn_ref[2, at, :] = jnp.where(lane < span_rot, -sine, 0.0)
+
     def turned(v, at, sign):
         near_part = v[:, :rot]
-        moved = pltpu.roll(near_part, 32, 1) * turn_ref[1, at, :] + pltpu.roll(near_part, rot - 32, 1) * turn_ref[2, at, :]
+        moved = pltpu.roll(near_part, span_rot, 1) * turn_ref[1, at, :] + pltpu.roll(near_part, rot - span_rot, 1) * turn_ref[2, at, :]
         return jnp.concatenate([near_part * turn_ref[0, at, :] + sign * moved, v[:, rot:]], axis=1)
 
     def project():
@@ -588,80 +634,67 @@
             def _():
                 line_copy(a, 0, side).start()
 
-    start_line(0)
-    start_z(0)
+    def close():
+        @pl.loop(0, length // tile)
+        def _(i):
+            at = span(i, tile)
+            dqkv[at, width : 2 * width] = turned(key_grad[at, :] * scale, at, -1.0).astype(BF16)
+            dqkv[at, 2 * width : 3 * width] = value_grad[at, :].astype(BF16)
+
+        give(5).start()
+        give(6).start()
+
+    def run(step):
+        op, rest = step[0], [int(d) for d in step[1:]]
+        if op == "z":
+            start_z(*rest)
+        elif op == "s":
+            spread(*rest)
+        elif op == "p":
+            pass_on(*rest)
+        elif op == "f":
+            finish(*rest)
+            give(*rest).start()
+        elif op == "l":
+            start_line(*rest)
+        elif op == "L":
+            line_step(*rest)
+        elif op == "N":
+            if rest[0]:
+                core_wait(0, *rest)
+            else:
+                ins[0].wait()
+            blocks_of(*rest, norm_block)
+        elif op == "P":
+            parameters()
+        elif op == "T":
+            tables()
+        elif op == "Q":
+            project()
+        elif op == "A":
+            attend(*rest)
+            if rest[0] == 3:
+                give(7).start()
+        elif op == "F":
+            feed(*rest)
+            if rest[0] == 3:
+                give(4).start()
+        elif op == "B":
+            if rest[0]:
+                core_wait(1, *rest)
+            else:
+                ins[1].wait()
+            blocks_of(*rest, back_attend)
+        elif op == "D":
+            blocks_of(*rest, back_feed)
+        elif op == "E":
+            close()
+
     key_grad[...] = jnp.zeros_like(key_grad)
     value_grad[...] = jnp.zeros_like(value_grad)
-    ins[0].wait()
-    norm_block(c)
-    line_step(0, 1)
-    start_z(1)
-    core_wait(0, 1)
-    blocks_of(1, norm_block)
-    spread(0)
-    line_step(0, 2)
-    start_z(3)
-    pass_on(0)
-    core_wait(0, 2)
-    blocks_of(2, norm_block)
-    line_step(0, 3)
-    start_line(1)
-    core_wait(0, 3)
-    blocks_of(3, norm_block)
-    finish(0)
-    give(0).start()
-    project()
-    spread(1)
-    start_z(2)
-    for i in range(4):
-        attend(i)
-        if i == 1:
-            pass_on(1)
-    give(7).start()
-    finish(1)
-    give(1).start()
-    line_step(1, 1)
-    for i in range(4):
-        feed(i)
-        if i == 0:
-            spread(3)
-        if i == 2:
-            spread(2)
-            line_step(1, 2)
-            pass_on(3)
-    give(4).start()
-    pass_on(2)
-    line_step(1, 3)
-    finish(2)
-    give(2).start()
-    ins[1].wait()
-    give_block(1, c).start()
-    back_attend(c)
-    core_wait(1, 1)
-    blocks_of(1, back_attend)
-    finish(3)
-    give(3).start()
-    back_feed(c)
-    blocks_of(1, back_feed)
-    core_wait(1, 2)
-
-    def both(origin):
-        back_attend(origin)
-        back_feed(origin)
-
-    blocks_of(2, both)
-    core_wait(1, 3)
-    blocks_of(3, both)
-
-    @pl.loop(0, length // tile)
-    def _(i):
-        at = span(i, tile)
-        dqkv[at, width : 2 * width] = turned(key_grad[at, :] * scale, at, -1.0).astype(BF16)
-        dqkv[at, 2 * width : 3 * width] = value_grad[at, :].astype(BF16)
-
-    give(5).start()
-    give(6).start()
-    for t in (1, 2, 3):
+    for step in FRONT_PLAN:
+        run(step)
+    for t in (0, 1, 2, 3):
         blocks_of(t, lambda origin: give_block(1, origin).start())
     for a in (0, 1):
         for side in (0, 1):
@@ -683,51 +716,64 @@
         give(i).wait()
 
 
-def gather_all(tokens, cotangent, w_qkv, w_up, w_out, w_down, rows, bias, turn, starts):
+def gather_all(tokens, cotangent, w_qkv, w_up, w_out, w_down, gain_a, off_a, gain_b, off_b, b_qkv, b_up, docs):
     count, model = tokens.shape
     length = 4 * count
     width, units = w_out.shape[0] // 4, w_down.shape[0] // 4
+    frequency = 10000.0 ** (-np.arange(0, ROT, 2, dtype=np.float32) / np.float32(ROT))
+    rate = jnp.asarray(np.tile(frequency.astype(np.float32), (8, 4)))
     dma = pltpu.SemaphoreType.DMA
     weights = [(3, model, width), (model, units), (width, model), (units, model)]
     wide, narrow = (length, model), (length, width)
     results = [wide, wide, (length, units), (length, units), (length, 3 * width), narrow] + weights
-    scratch = [dma((4, 3))] * 10 + [dma((2, 2, 3))] * 4 + [dma((6,)), dma((8,)), dma((2,))]
+    scratch = [dma((4, 3))] * 10 + [dma((2, 2, 3))] * 4 + [dma((6,)), dma((8,)), dma((2,)), dma((7,))]
     scratch += [
         pltpu.VMEM(v, BF16)
         for v in [wide, wide] + weights + [wide] * 3 + [narrow] * 3
         + [(length, units)] * 2 + [(length, 3 * width), narrow]
     ]
     scratch += [pltpu.VMEM(v, F32) for v in ((length, units), narrow, (length, 1), narrow, narrow)]
+    scratch += [pltpu.VMEM((3, length, rate.shape[1]), F32), pltpu.VMEM((length, 1), jnp.int32)]
+    scratch += [pltpu.VMEM((model,), BF16)] * 4 + [pltpu.VMEM(b_qkv.shape, BF16), pltpu.VMEM(b_up.shape, BF16)]
+    scratch += [pltpu.VMEM(v, F32) for v in (rate.shape, (8, model), (8, units))]
     any_space = pl.BlockSpec(memory_space=pl.ANY)
-    vmem_space = pl.BlockSpec(memory_space=pltpu.VMEM)
     return pl.pallas_call(
         gather_body,
         out_shape=[jax.ShapeDtypeStruct(v, BF16) for v in results],
-        in_specs=[any_space] * 6 + [vmem_space] * 4,
+        in_specs=[any_space] * 13 + [pl.BlockSpec(memory_space=pltpu.SMEM)],
         out_specs=[any_space] * 10,
         scratch_shapes=scratch,
         compiler_params=pltpu.CompilerParams(
             collective_id=0, has_side_effects=True, vmem_limit_bytes=63 << 20
         ),
         name="gather",
-    )(tokens, cotangent, w_qkv, w_up, w_out, w_down, rows, bias, turn, starts)
-
-
-LEADS = (12, 4, 1, 1)
-
+    )(
+        tokens, cotangent, w_qkv, w_up, w_out, w_down, gain_a, off_a, gain_b, off_b, b_qkv, b_up, rate, docs
+    )
+
+
+LEADS = (4, 4, 4, 4, 1, 1)
+BACK_PLAN = (
+    "D", "15", "P", "U", "13", "Q", "10", "11", "12", "O", "14", "B0", "B1", "25", "R0", "I0", "I1", "a", "23", "20", "21", "22", "b", "Z5", "24", "S0", "c", "Z3", "Z0", "Z1", "Z2", "Z4",
+    "R1", "X5", "d", "N5", "X3", "e", "N3", "X0", "X1", "X2", "N0", "N1", "N2", "X4", "N4", "S1",
+)
 def settle_body(
-    act_in, up_in, unit_in, dh_in, dqkv_in, mixed_in, wq_in, wu_in, wo_in, wd_in, cols_ref, rows_ref,
+    act_in, up_in, unit_in, dh_in, dqkv_in, mixed_in, wq_in, wu_in, wo_in, wd_in,
+    gain_a_ref, off_a_ref, gain_b_ref, off_b_ref,
     joint, inward, o0, o1, o2, o3, small_out,
     s1x_send, s1x_recv, s1y_send, s1y_recv, s2x_send, s2x_recv, s2y_send, s2y_recv,
     x_send, x_recv, y_send, y_recv, fx_send, fx_recv, fy_send, fy_recv,
     z_send, z_recv, keep_sem, load_sem, weight_sem,
     core_send, core_recv, row_send, row_recv, back_send, back_recv, back_sem,
-    sum_send, sum_recv, sum_sem,
-    act, up, unit, dh, dqkv, mixed, w_wide, w_out, w_qkv,
-    gb0, gb1, gb2, gb3, fa0, fb0, fa1, fb1, fa2, fb2, fa3, fb3, ga0, hb0, ga1, hb1, ga2, hb2, ga3, hb3,
-    own_half, core_half, send_half, row_parts, done_half,
-    sums, sums_core, slots, total_own, total_x, total_y,
+    sum_send, sum_recv, sum_sem, small_sem,
+    act, up, unit, dh, dqkv, mixed, w_wide, w_out, w_qkv, *rest,
 ):
+    grads, first, second = rest[0:6], (rest[6:18:2], rest[7:18:2]), (rest[18:30:2], rest[19:30:2])
+    (
+        own_half, core_half, send_half, row_parts, done_half,
+        sums, sums_core, slots, total_own, total_x, total_y,
+        gain_a, off_a, gain_b, off_b, rows_ref, low_ref,
+    ) = rest[30:]
     s, c, h = places()
     x_at, y_at = lax.rem(s, 2), lax.div(s, 2)
     x_off, y_off = 1 - x_at, 1 - y_at
@@ -736,9 +782,8 @@
     core_peer = (s, c, 1 - h)
     near = (1, 3, 2)
     greet([*across, core_peer, *[(s, lax.rem(c + k, 4), h) for k in near]])
-    grads, outs = (gb0, gb1, gb2, gb3), (o0, o1, o2, o3)
-    first = ((fa0, fb0), (fa1, fb1), (fa2, fb2), (fa3, fb3))
-    second = ((ga0, hb0), (ga1, hb1), (ga2, hb2), (ga3, hb3))
+    outs = (o0, o1, o2, o3)
+    first, second = list(zip(*first)), list(zip(*second))
     slab = o2.shape[-1]
     length, model = up.shape
     units, width = act.shape[1], mixed.shape[1]
@@ -759,6 +804,15 @@
     ]
     for load in loads:
         load.start()
+
+    smalls = [
+        pltpu.make_async_copy(a, b, small_sem.at[i])
+        for i, (a, b) in enumerate(
+            ((gain_a_ref, gain_a), (off_a_ref, off_a), (gain_b_ref, gain_b), (off_b_ref, off_b))
+        )
+    ]
+    for copy in smalls:
+        copy.start()
 
     def side(which):
         return 1 - h if which == 0 else h
@@ -813,18 +867,14 @@
 
     def share_of(m, half, to):
         ref = second[m][half]
-        if m == 0:
-            return ref.reshape(3, 4, *ref.shape[1:]).at[:, to]
-        if m == 1:
-            return ref.at[to]
-        return ref.at[0, :, span(to, slab)]
+        return ref.at[to] if m < 4 else ref.at[0, :, span(to, slab)]
 
     def home(m, half):
-        if m == 0:
-            return outs[0].at[:, s, half, :, span(c, width)]
-        if m == 1:
+        if m < 3:
+            return outs[0].at[m, s, half, :, span(c, width)]
+        if m == 3:
             return outs[1].at[s, half, :, span(c, units)]
-        return outs[m].at[c, s, half]
+        return outs[m - 2].at[c, s, half]
 
     def z_copy(m, half, k):
         to = lax.rem(c + 4 - k, 4)
@@ -835,9 +885,12 @@
         return pltpu.make_async_copy(share_of(m, half, c), home(m, half), keep_sem.at[m, half])
 
     def quarter(m, q, half=None):
-        if half is None:
-            return outs[m].at[q] if m == 1 else outs[m].at[:, q]
-        return outs[m].at[q, half] if m == 1 else outs[m].at[:, q, half]
+        at = (q,) if half is None else (q, half)
+        if m < 3:
+            return outs[0].at[(m, *at)]
+        if m == 3:
+            return outs[1].at[at]
+        return outs[m - 2].at[(slice(None), *at)]
 
     def direct(m, axis):
         send, recv = (x_send, x_recv) if axis == 0 else (y_send, y_recv)
@@ -908,7 +961,7 @@
             for j in range(model // 512):
                 part = dot(left, up[:, j * 512 : (j + 1) * 512], (0, 0)).astype(BF16)
                 for half in (0, 1):
-                    gb3[0, lax.div(q, 2), lax.rem(q, 2), half, :, j * 512 : (j + 1) * 512] = part[
+                    grads[5][0, lax.div(q, 2), lax.rem(q, 2), half, :, j * 512 : (j + 1) * 512] = part[
                         half * rows : (half + 1) * rows
                     ]
 
@@ -917,11 +970,16 @@
         for j in range(model // 512):
             part = dot(mixed[...], up[:, j * 512 : (j + 1) * 512], (0, 0)).astype(BF16)
             for i in range(8):
-                gb2[0, i // 4, (i // 2) % 2, i % 2, :, j * 512 : (j + 1) * 512] = part[i * rows : (i + 1) * rows]
-
-    def scaled(part, t, at, column_sum):
-        rows = span(t, tile)
-        return (part * cols_ref[rows, at : at + 1] + cols_ref[rows, at + 1 : at + 2] * column_sum).astype(BF16)
+                grads[4][0, i // 4, (i // 2) % 2, i % 2, :, j * 512 : (j + 1) * 512] = part[i * rows : (i + 1) * rows]
+
+    same = lax.broadcasted_iota(jnp.int32, (tile, tile), 0) == lax.broadcasted_iota(jnp.int32, (tile, tile), 1)
+    eye = jnp.where(same, 1.0, 0.0).astype(BF16)
+
+    def columns(t):
+        return dot(eye, low_ref[:, span(t, tile)], (1, 1))
+
+    def scaled(part, column, at, column_sum):
+        return (part * column[:, at : at + 1] + column[:, at + 1 : at + 2] * column_sum).astype(BF16)
 
     def column_sum(ref, cols):
         total = jnp.zeros((1, cols.stop - cols.start), F32)
@@ -934,25 +992,25 @@
 
         @pl.loop(0, model // tile)
         def _(t):
-            left = unit[:, span(t, tile)]
+            left, column = unit[:, span(t, tile)], columns(t)
             for j in range(units // 512):
                 cols = slice(j * 512, (j + 1) * 512)
                 near_sum = sums[5:6, 3 * width + j * 512 : 3 * width + (j + 1) * 512]
-                part = scaled(dot(left, dh[:, cols], (0, 0)), t, 2, near_sum)
+                part = scaled(dot(left, dh[:, cols], (0, 0)), column, 2, near_sum)
                 for i in range(4):
-                    gb1[lax.div(t, 2), lax.rem(t, 2), i // 2, i % 2, :, cols] = part[i * rows : (i + 1) * rows]
+                    grads[3][lax.div(t, 2), lax.rem(t, 2), i // 2, i % 2, :, cols] = part[i * rows : (i + 1) * rows]
 
     def qkv_grad():
         rows = tile // 4
 
         @pl.loop(0, model // tile)
         def _(t):
-            left = unit[:, span(t, tile)]
+            left, column = unit[:, span(t, tile)], columns(t)
             for p in range(3):
                 cols = slice(p * width, (p + 1) * width)
-                part = scaled(dot(left, dqkv[:, cols], (0, 0)), t, 0, sums[5:6, cols])
+                part = scaled(dot(left, dqkv[:, cols], (0, 0)), column, 0, sums[5:6, cols])
                 for i in range(4):
-                    gb0[p * 4 + lax.div(t, 2), lax.rem(t, 2), i // 2, i % 2] = part[i * rows : (i + 1) * rows]
+                    grads[p][lax.div(t, 2), lax.rem(t, 2), i // 2, i % 2] = part[i * rows : (i + 1) * rows]
 
     def branches(which):
         into = send_half if which == 0 else own_half.at[0]
@@ -1013,40 +1071,29 @@
     def sum_y():
         return remote(total_own, total_y, sum_send.at[5], sum_recv.at[5], across[1])
 
-    order = (3, 1, 0, 2)
-    loads[0].wait()
-    loads[1].wait()
-    down_grad()
-    one(3, 0).start()
-    one(3, 1).start()
-    sums[4:5, :] = jnp.sum(up[span(c, count), :].astype(F32), axis=0, keepdims=True) * 0.5
-    sums[5:8, :] = jnp.zeros((3, model), F32)
-    loads[2].wait()
-    loads[3].wait()
-    for j in range(units // 512):
-        sums[5:6, 3 * width + j * 512 : 3 * width + (j + 1) * 512] = column_sum(dh, slice(j * 512, (j + 1) * 512))
-    up_grad()
-    one(1, 0).start()
-    one(1, 1).start()
-    loads[4].wait()
-    for p in range(3):
-        sums[5:6, p * width : (p + 1) * width] = column_sum(dqkv, slice(p * width, (p + 1) * width))
-    qkv_grad()
-    one(0, 0).start()
-    one(0, 1).start()
-    loads[5].wait()
-    out_grad()
-    one(2, 0).start()
-    one(2, 1).start()
-    weight_load(0).wait()
-    weight_load(4).wait()
-    branches(0)
-    core_copy(0).start()
-    weight_load(2).start()
-    weight_load(1).wait()
-    weight_load(5).wait()
-    branches(1)
-    weight_load(3).start()
+    kinds = range(6)
+    loaded = set()
+
+    def need(*which):
+        for i in which:
+            if i not in loaded:
+                loads[i].wait()
+                loaded.add(i)
+
+    def parameters():
+        for copy in smalls:
+            copy.wait()
+        rows_ref[...] = jnp.zeros_like(rows_ref)
+        for i, ref in enumerate((gain_a, off_a, gain_b, off_b)):
+            rows_ref[i : i + 1, :] = ref[...].astype(F32).reshape(1, model)
+        low_ref[...] = rows_ref[...].astype(BF16)
+
+    def compute_sums():
+        sums[4:5, :] = jnp.sum(up[span(c, count), :].astype(F32), axis=0, keepdims=True) * 0.5
+        sums[5:8, :] = jnp.zeros((3, model), F32)
+
+    def small_copy():
+        return pltpu.make_async_copy(total_own, small_out, sum_sem.at[0])
 
     def stage_two(m):
         for half in (0, 1):
@@ -1076,65 +1123,99 @@
         direct(m, 1).wait_recv()
         onward(m, 0).start()
 
-    stage_two(3)
-    line_start(0)
-    core_copy(0).wait_send()
-    weight_load(2).wait()
-    weight_load(6).wait()
-    inwards(0)
-    core_copy(1).start()
-    weight_load(3).wait()
-    weight_load(7).wait()
-    inwards(1)
-    sum_core().start()
-    stage_two(1)
-    stage_two(0)
-    sum_core().wait()
-    sums[0:5, :] = sums[0:5, :] + sums_core[0:5, :]
-    for k in near:
-        sum_line(k).start()
-    slots[c] = sums[...]
-    stage_z(3)
-    stage_two(2)
-    line_sum(0)
-    for k in near:
-        sum_line(k).wait()
-    total_own[0:8, :] = slots[0] + slots[1] + slots[2] + slots[3]
-    for i in range(4):
-        total_own[8 + i : 9 + i, :] = slots[i, 5:6, :]
-    total_own[12:16, :] = jnp.zeros((4, model), F32)
-    sum_x().start()
-    stage_z(1)
-    stage_z(0)
-    stage_z(2)
-    line_start(1)
-    stage_out(3)
-    sum_x().wait()
-    total_own[...] = total_own[...] + total_x[...]
-    sum_y().start()
-    stage_on(3)
-    stage_out(1)
-    sum_y().wait()
-    total_own[...] = total_own[...] + total_y[...]
-    small_copy = pltpu.make_async_copy(total_own, small_out, sum_sem.at[0])
-    small_copy.start()
-    stage_on(1)
-    stage_out(0)
-    stage_on(0)
-    stage_out(2)
-    stage_on(2)
-    line_sum(1)
-    for m in order:
+    def run(step):
+        op, m = step[0], int(step[1]) if len(step) > 1 else None
+        if op == "D":
+            need(0, 1)
+            down_grad()
+        elif op == "P":
+            parameters()
+        elif op == "U":
+            need(1, 2, 3)
+            compute_sums()
+            for j in range(units // 512):
+                cols = slice(j * 512, (j + 1) * 512)
+                sums[5:6, 3 * width + cols.start : 3 * width + cols.stop] = column_sum(dh, cols)
+            up_grad()
+        elif op == "Q":
+            need(3, 4)
+            for p in range(3):
+                cols = slice(p * width, (p + 1) * width)
+                sums[5:6, cols] = column_sum(dqkv, cols)
+            qkv_grad()
+        elif op == "O":
+            need(1, 5)
+            out_grad()
+        elif op == "1":
+            one(m, 0).start()
+            one(m, 1).start()
+        elif op == "B":
+            need(0, 5)
+            weight_load(m).wait()
+            weight_load(4 + m).wait()
+            branches(m)
+            weight_load(2 + m).start()
+            if m == 0:
+                core_copy(0).start()
+        elif op == "I":
+            need(2, 3, 4)
+            if m == 0:
+                core_copy(0).wait_send()
+            weight_load(2 + m).wait()
+            weight_load(6 + m).wait()
+            inwards(m)
+            if m == 0:
+                core_copy(1).start()
+        elif op == "2":
+            stage_two(m)
+        elif op == "Z":
+            stage_z(m)
+        elif op == "X":
+            stage_out(m)
+        elif op == "N":
+            stage_on(m)
+        elif op == "R":
+            line_start(m)
+        elif op == "S":
+            line_sum(m)
+        elif op == "a":
+            sum_core().start()
+        elif op == "b":
+            sum_core().wait()
+            sums[0:5, :] = sums[0:5, :] + sums_core[0:5, :]
+            for k in near:
+                sum_line(k).start()
+            slots[c] = sums[...]
+        elif op == "c":
+            for k in near:
+                sum_line(k).wait()
+            total_own[0:8, :] = slots[0] + slots[1] + slots[2] + slots[3]
+            for i in range(4):
+                total_own[8 + i : 9 + i, :] = slots[i, 5:6, :]
+            total_own[12:16, :] = jnp.zeros((4, model), F32)
+            sum_x().start()
+        elif op == "d":
+            sum_x().wait()
+            total_own[...] = total_own[...] + total_x[...]
+            sum_y().start()
+        elif op == "e":
+            sum_y().wait()
+            total_own[...] = total_own[...] + total_y[...]
+            small_copy().start()
+
+    for step in BACK_PLAN:
+        run(step)
+    for m in kinds:
         for axis in (0, 1):
             onward(m, axis).wait_recv()
-    small_copy.wait()
+    small_copy().wait()
     for a in (0, 1):
         back_copy(a).wait()
         back_keep(a).wait()
         for k in near:
             row_copy(a, k).wait_send()
     core_copy(1).wait_send()
-    for m in order:
+    for m in kinds:
         for half in (0, 1):
             one(m, half).wait_send()
             two(m, half).wait_send()
@@ -1145,21 +1226,21 @@
             onward(m, axis).wait_send()
 
 
-def settle_all(act, up, unit, dh, dqkv, mixed, w_qkv, w_up, w_out, w_down, cols, rows):
+def settle_all(act, up, unit, dh, dqkv, mixed, w_qkv, w_up, w_out, w_down, gain_a, off_a, gain_b, off_b):
     length, model = up.shape
     units, width = act.shape[1], mixed.shape[1]
     slab, count, half = model // 4, length // 4, model // 2
     dma = pltpu.SemaphoreType.DMA
-    heights = (slab // 8, slab // 8, width // 8, units // 8)
-    widths = (width, units, model, model)
+    heights = (*[slab // 8] * 4, width // 8, units // 8)
+    widths = (width, width, width, units, model, model)
     out_shapes = [
         (count, model), (count, model),
-        (3, 4, 2, heights[0], 4 * width), (4, 2, heights[1], 4 * units),
-        (4, 4, 2, heights[2], slab), (4, 4, 2, heights[3], slab),
+        (3, 4, 2, heights[0], 4 * width), (4, 2, heights[3], 4 * units),
+        (4, 4, 2, heights[4], slab), (4, 4, 2, heights[5], slab),
     ]
-    scratch = [dma((4,))] * 16 + [dma((24,))] * 2 + [dma((4, 2)), dma((6,)), dma((8,))]
+    scratch = [dma((6,))] * 16 + [dma((36,))] * 2 + [dma((6, 2)), dma((6,)), dma((8,))]
     scratch += [dma((2,)), dma((2,)), dma((2, 3)), dma((2, 3)), dma((2,)), dma((2,)), dma((2,))]
-    scratch += [dma((6,)), dma((6,)), dma((1,))]
+    scratch += [dma((6,)), dma((6,)), dma((1,)), dma((4,))]
     vmem = [(length, units), (length, model), (length, model), (length, units), (length, 3 * width), (length, width)]
     vmem += [(2, units, half), (2, width, half), (2, 3, half, width)]
     shapes = list(zip(LEADS, heights, widths))
@@ -1169,23 +1250,79 @@
     vmem += [(2, length, half), (2, length, half), (length, half), (2, 3, count, half), (2, count, half)]
     scratch += [pltpu.VMEM(v, BF16) for v in vmem]
     scratch += [pltpu.VMEM(v, F32) for v in ((8, model), (8, model), (4, 8, model), (16, model), (16, model), (16, model))]
+    scratch += [pltpu.VMEM((model,), BF16)] * 4 + [pltpu.VMEM((8, model), F32), pltpu.VMEM((8, model), BF16)]
     any_space = pl.BlockSpec(memory_space=pl.ANY)
-    vmem_space = pl.BlockSpec(memory_space=pltpu.VMEM)
     joint, inward, q, u, o, d, small = pl.pallas_call(
         settle_body,
         out_shape=[jax.ShapeDtypeStruct(v, BF16) for v in out_shapes] + [jax.ShapeDtypeStruct((16, model), F32)],
-        in_specs=[any_space] * 10 + [vmem_space] * 2,
+        in_specs=[any_space] * 14,
         out_specs=[any_space] * 7,
         scratch_shapes=scratch,
         compiler_params=pltpu.CompilerParams(
             collective_id=1, has_side_effects=True, vmem_limit_bytes=63 << 20
         ),
         name="settle",
-    )(act, up, unit, dh, dqkv, mixed, w_qkv, w_up, w_out, w_down, cols, rows)
+    )(act, up, unit, dh, dqkv, mixed, w_qkv, w_up, w_out, w_down, gain_a, off_a, gain_b, off_b)
     return (
         joint, inward, q.reshape(3, slab, 4 * width), u.reshape(slab, 4 * units),
         o.reshape(4 * width, slab), d.reshape(4 * units, slab), small,
     )
+
+
+def finish_body(
+    q_ref, u_ref, o_ref, d_ref, joint_ref, inward_ref, own_ref, up_ref,
+    small_ref, bias_a, bias_b,
+    q_out, u_out, o_out, d_out, y_out, g_out, v0, v1, v2, v3, v4, v5, qb_out, ub_out,
+):
+    q_out[...] = q_ref[...].astype(F32)
+    u_out[...] = u_ref[...].astype(F32)
+    o_out[...] = o_ref[...].astype(F32)
+    d_out[...] = d_ref[...].astype(F32)
+    wide = own_ref[...].astype(F32)
+    bias = (bias_a[...].astype(F32) + bias_b[...].astype(F32)).reshape(1, wide.shape[1])
+    y_out[...] = (wide + joint_ref[...].astype(F32) + bias).astype(BF16)
+    centred = wide - jnp.mean(wide, axis=-1, keepdims=True)
+    scale = lax.rsqrt(jnp.mean(centred * centred, axis=-1, keepdims=True) + 1e-05)
+    unit = centred * scale
+    inward = inward_ref[...].astype(F32)
+    inward = inward - jnp.mean(inward, axis=-1, keepdims=True) - unit * jnp.mean(inward * unit, axis=-1, keepdims=True)
+    g_out[...] = up_ref[...].astype(F32) + scale * inward
+
+    @pl.when(pl.program_id(0) == 0)
+    def _():
+        for i, out in zip((0, 1, 4, 2, 3, 4), (v0, v1, v2, v3, v4, v5)):
+            out[...] = small_ref[i : i + 1, :].reshape(out.shape)
+        width, units = qb_out.shape[1] // 4, ub_out.shape[0] // 4
+        for i in range(4):
+            row = small_ref[8 + i : 9 + i, :]
+            for p in range(3):
+                qb_out[p : p + 1, i * width : (i + 1) * width] = row[:, p * width : (p + 1) * width]
+            ub_out[i * units : (i + 1) * units] = row[:, 3 * width : 3 * width + units].reshape(units)
+
+
+def finish_all(q, u, o, d, joint, inward, own, upstream, small, bias_a, bias_b):
+    steps = 16
+    arrays = [q, u, o, d, joint, inward, own, upstream]
+
+    def spec(a):
+        return pl.BlockSpec((a.shape[0] // steps, a.shape[1]), lambda i: (i, 0))
+
+    results = [(a.shape, F32) for a in (q, u, o, d)] + [(own.shape, BF16), (own.shape, F32)]
+    smalls = [(own.shape[1:], F32)] * 6 + [((3, q.shape[1]), F32), (u.shape[1:], F32)]
+    results += smalls
+
+    def whole(shape):
+        return pl.BlockSpec(shape, lambda i: (0,) * len(shape))
+
+    return pl.pallas_call(
+        finish_body,
+        grid=(steps,),
+        out_shape=[jax.ShapeDtypeStruct(v, t) for v, t in results],
+        in_specs=[spec(a) for a in arrays] + [whole(v.shape) for v in (small, bias_a, bias_b)],
+        out_specs=[spec(a) for a in (q, u, o, d, own, own)] + [whole(v) for v, _ in smalls],
+        compiler_params=pltpu.CompilerParams(vmem_limit_bytes=63 << 20),
+        name="finish",
+    )(*arrays, small, bias_a, bias_b)
 
 
 def per_device(
@@ -1205,40 +1342,6 @@
     down_bias,
     cotangent,
 ):
-    f32, bf16 = jnp.float32, jnp.bfloat16
-    ctx_count = lax.axis_size("ctx")
-    c = lax.axis_index("ctx")
-    count, model = tokens.shape[1], tokens.shape[2]
-    length = count * ctx_count
-    width = qkv_weight.shape[2] // ctx_count
-    units = up_weight.shape[1] // ctx_count
-
-    gains = jnp.stack([ln1_gain, ln1_bias, ln2_gain, ln2_bias]).astype(f32)
-    gain_rows = jnp.pad(gains, ((0, 4), (0, 0)))
-    biases = jnp.stack(
-        [
-            jnp.pad(
-                lax.dynamic_slice_in_dim(qkv_bias, c * width, width, 1).reshape(-1),
-                (0, units - 3 * width),
-            ),
-            lax.dynamic_slice_in_dim(up_bias, c * units, units, 0),
-        ]
-    ).astype(f32)
-    biases = jnp.pad(biases, ((0, 6), (0, 0)))
-    positions, starts = token_places(doc_lengths[0], length)
-    half = ROT // 2
-    lane = jnp.arange(2 * ROT)
-    frequency = 10000.0 ** (-jnp.arange(0, ROT, 2, dtype=f32) / ROT)
-    angles = (positions - starts).astype(f32)[:, None] * frequency[None, :]
-    cosine, sine = jnp.tile(jnp.cos(angles), (1, 4)), jnp.tile(jnp.sin(angles), (1, 4))
-    turn = jnp.stack(
-        [
-            jnp.where(lane < ROT, cosine, 1.0),
-            jnp.where((lane >= half) & (lane < ROT), sine, 0.0),
-            jnp.where(lane < half, -sine, 0.0),
-        ]
-    )
-
     upstream, unit, activated, hidden_grad, projected_grad, mixed_low, w_qkv, w_up, w_out, w_down = (
         gather_all(
             tokens[0],
@@ -1247,10 +1350,13 @@
             up_weight,
             out_weight,
             down_weight,
-            gain_rows,
-            biases,
-            turn,
-            starts[:, None],
+            ln1_gain,
+            ln1_bias,
+            ln2_gain,
+            ln2_bias,
+            qkv_bias,
+            up_bias,
+            doc_lengths,
         )
     )
 
@@ -1265,42 +1371,39 @@
         w_up,
         w_out,
         w_down,
-        jnp.pad(gains.T, ((0, 0), (0, 124))),
-        gain_rows,
-    )
-    joint, inward = joint.astype(f32), inward.astype(f32)
-
-    own = tokens[0].astype(f32)
-    own_upstream = cotangent[0].astype(f32)
-    output = own + joint + out_bias.astype(f32) + down_bias.astype(f32)
-    own_centred = own - jnp.mean(own, axis=-1, keepdims=True)
-    own_scale = lax.rsqrt(jnp.mean(own_centred * own_centred, axis=-1, keepdims=True) + 1e-05)
-    own_unit = own_centred * own_scale
-    input_grad = own_upstream + own_scale * (
-        inward
-        - jnp.mean(inward, axis=-1, keepdims=True)
-        - own_unit * jnp.mean(inward * own_unit, axis=-1, keepdims=True)
-    )
-
-    qkv_bias_grad = (
-        small[8:12, : 3 * width].reshape(ctx_count, 3, width).transpose(1, 0, 2).reshape(3, -1)
-    )
-    up_bias_grad = small[8:12, 3 * width : 3 * width + units].reshape(-1)
+        ln1_gain,
+        ln1_bias,
+        ln2_gain,
+        ln2_bias,
+    )
+    q_grad, u_grad, o_grad, d_grad, output, input_grad, *rest = finish_all(
+        qkv_out.reshape(-1, qkv_out.shape[-1]),
+        up_out,
+        out_out,
+        down_out,
+        joint,
+        inward,
+        tokens[0],
+        cotangent[0],
+        small,
+        out_bias,
+        down_bias,
+    )
     return (
-        output.astype(bf16)[None],
+        output[None],
         input_grad[None],
-        small[0],
-        small[1],
-        qkv_out.astype(f32),
-        qkv_bias_grad,
-        out_out.astype(f32),
-        small[4],
-        small[2],
-        small[3],
-        up_out.astype(f32),
-        up_bias_grad,
-        down_out.astype(f32),
-        small[4],
+        rest[0],
+        rest[1],
+        q_grad.reshape(qkv_out.shape),
+        rest[6],
+        o_grad,
+        rest[2],
+        rest[3],
+        rest[4],
+        u_grad,
+        rest[7],
+        d_grad,
+        rest[5],
     )
 
 

time: 448 us -> 408 us (0.911)
  other arithmetic: 24.7 us -> 0 us
  Pallas kernels: 413 us -> 402 us
  local copies, waits for them, and re-layouts: 8.06 us -> 0 us
    pallas_call x1, Pallas kernels: 181 us -> 158 us  [gather_all(): pl.pallas_call(gather_body, out_shape=[jax.ShapeDtypeStruct(v, BF16) for...]
    pallas_call x0 -> x1, Pallas kernels: none -> 20.7 us  [finish_all(): pl.pallas_call(finish_body, grid=(steps,), out_shape=[jax.ShapeDtypeStruc...]
    convert_element_type x7 -> x0, other arithmetic: 17 us -> none  [the longest x1 6.94 us: per_device(): down_out.astype(f32)]
    pallas_call x1, Pallas kernels: 232 us -> 223 us  [settle_all(): pl.pallas_call(settle_body, out_shape=[jax.ShapeDtypeStruct(v, BF16) for...]
where the time goes in v5:
time: 408 us; the launch traced here: 403 us
  Pallas kernels  402 us (99%)
    pallas_call x1, Pallas kernels, settle_all(): pl.pallas_call(settle_body, out_shape=[jax.ShapeDtypeStruct(v, BF16) for...  223 us
    pallas_call x1, Pallas kernels, gather_all(): pl.pallas_call(gather_body, out_shape=[jax.ShapeDtypeStruct(v, BF16) for...  158 us
    pallas_call x1, Pallas kernels, finish_all(): pl.pallas_call(finish_body, grid=(steps,), out_shape=[jax.ShapeDtypeStruc...  20.7 us

profile of v5, /device:TPU:0, one launch (start us, length us, event | category | flops | bytes accessed | tf_op | source)
XLA Modules:
  0.0 402.8 jit_solution(16549511679249772378)
XLA Ops:
  0.6 157.9 %gather.1 = (bf16[1024,2048]{1,0:T(8,128)(2,1)}, bf16[1024,2048]{1,0:T(8,128)(2,1)}, bf16[1024,1024]{1,0:T(8,128)(2,1)}, bf16[1024,1024]{1,0:T(8,128)(2,1)}, bf1...) custom-call(bf16[256,2048]{1,0:T(8,128)(2,1)} %bitcast.11, ...), custom_call_target="tpu_custom_call" | custom-call | tf_op jit(solution)/shard_map/gather/pallas_call | solution.py:740
  158.6 223.3 %settle.1 = (bf16[256,2048]{1,0:T(8,128)(2,1)}, bf16[256,2048]{1,0:T(8,128)(2,1)}, bf16[3,4,2,64,1024]{4,3,2,1,0:T(8,128)(2,1)}, bf16[4,2,64,4096]{3,2,1,0:T(8,1...) custom-call(bf16[1024,1024]{1,0:T(8,128)(2,1)} %get-tuple-element.45.act_in,, ...), custom_call_target="tpu_custom_call" | custom-call | tf_op jit(solution)/shard_map/settle/pallas_call | solution.py:1255
  381.9 20.7 %finish.1 = (f32[1536,1024]{1,0:T(8,128)}, f32[512,4096]{1,0:T(8,128)}, f32[1024,512]{1,0:T(8,128)}, f32[4096,512]{1,0:T(8,128)}, bf16[256,2048]{1,0:T(8,128)(2,...) custom-call(bf16[1536,1024]{1,0:T(8,128)(2,1)} %bitcast.15, ...), custom_call_target="tpu_custom_call" | custom-call | tf_op jit(solution)/shard_map/finish/pallas_call | solution.py:1317

commit v6 on v5

--- a/solution.py
+++ b/solution.py
@@ -285,8 +285,8 @@
 
 MESH = pl.DeviceIdType.MESH
 FRONT_PLAN = (
-    "z0", "z1", "l0", "P", "T", "N0", "s0", "z3", "s1", "p0", "L01", "z2", "p1", "N1", "L02", "l1", "s3", "N2", "L03", "p3", "s2", "N3", "f0", "Q", "L11", "p2", "A0", "A1", "A2",
-    "A3", "L12", "f1", "F0", "F1", "F2", "F3", "L13", "f2", "B0", "B1", "f3", "D0", "D1", "B2", "D2", "B3", "D3", "E",
+    "z0", "l0", "z1", "P", "T", "N0", "s0", "L01", "z2", "l1", "z3", "p0", "N1", "f0", "Q0", "Q1", "s1", "L02", "s2", "p1", "L11", "p2", "N2", "Q2", "f1", "F0", "F1", "F2", "s3",
+    "L03", "L12", "N3", "Q3", "p3", "F3", "A0", "A1", "A2", "A3", "f2", "B0", "B1", "L13", "f3", "D0", "D1", "B2", "D2", "B3", "D3", "E",
 )
 F32, BF16 = jnp.float32, jnp.bfloat16
 
@@ -327,7 +327,6 @@
     across = ((x_peer, c, h), (y_peer, c, h))
     core_peer = (s, c, 1 - h)
     ring = [(s, lax.rem(c + k, 4), h) for k in (1, 2, 3)]
-    greet([*across, core_peer, *ring])
 
     count = x_ref.shape[0]
     slab, width, units = up_ref.shape[0], out_ref.shape[0] // 4, down_ref.shape[0] // 4
@@ -572,13 +571,11 @@
         moved = pltpu.roll(near_part, span_rot, 1) * turn_ref[1, at, :] + pltpu.roll(near_part, rot - span_rot, 1) * turn_ref[2, at, :]
         return jnp.concatenate([near_part * turn_ref[0, at, :] + sign * moved, v[:, rot:]], axis=1)
 
-    def project():
-        @pl.loop(0, length // tile)
-        def _(i):
-            at = span(i, tile)
-            for p, into in enumerate((query, keys, values)):
-                part = dot(low_one[at, :], qkv_all[p], (1, 0)) + bias_ref[0:1, p * width : (p + 1) * width]
-                into[at, :] = (turned(part, at, 1.0) if p < 2 else part).astype(BF16)
+    def project(i):
+        at = span(i, tile)
+        for p, into in enumerate((query, keys, values)):
+            part = dot(low_one[at, :], qkv_all[p], (1, 0)) + bias_ref[0:1, p * width : (p + 1) * width]
+            into[at, :] = (turned(part, at, 1.0) if p < 2 else part).astype(BF16)
 
     def allowed_of(i, wide):
         first = lax.broadcasted_iota(jnp.int32, (tile, wide), 1)
@@ -670,13 +667,13 @@
         elif op == "T":
             tables()
         elif op == "Q":
-            project()
+            blocks_of(*rest, project)
         elif op == "A":
             attend(*rest)
             if rest[0] == 3:
                 give(7).start()
         elif op == "F":
-            feed(*rest)
+            blocks_of(*rest, feed)
             if rest[0] == 3:
                 give(4).start()
         elif op == "B":
@@ -690,6 +687,7 @@
         elif op == "E":
             close()
 
+    greet([*across, core_peer, *ring])
     key_grad[...] = jnp.zeros_like(key_grad)
     value_grad[...] = jnp.zeros_like(value_grad)
     for step in FRONT_PLAN:
@@ -754,8 +752,8 @@
 
 LEADS = (4, 4, 4, 4, 1, 1)
 BACK_PLAN = (
-    "D", "15", "P", "U", "13", "Q", "10", "11", "12", "O", "14", "B0", "B1", "25", "R0", "I0", "I1", "a", "23", "20", "21", "22", "b", "Z5", "24", "S0", "c", "Z3", "Z0", "Z1", "Z2", "Z4",
-    "R1", "X5", "d", "N5", "X3", "e", "N3", "X0", "X1", "X2", "N0", "N1", "N2", "X4", "N4", "S1",
+    "O", "14", "D", "B0", "24", "B1", "R0", "P", "Q", "12", "25", "Z4", "I0", "22", "11", "U", "13", "10", "I1", "Z5", "X4", "20", "23", "21", "a", "Z0", "Z2", "b", "X5", "X0", "S0", "N4",
+    "Z3", "Z1", "N5", "X3", "X2", "c", "R1", "X1", "N3", "N1", "d", "N0", "N2", "e", "S1",
 )
 def settle_body(
     act_in, up_in, unit_in, dh_in, dqkv_in, mixed_in, wq_in, wu_in, wo_in, wd_in,
@@ -781,7 +779,6 @@
     across = ((x_peer, c, h), (y_peer, c, h))
     core_peer = (s, c, 1 - h)
     near = (1, 3, 2)
-    greet([*across, core_peer, *[(s, lax.rem(c + k, 4), h) for k in near]])
     outs = (o0, o1, o2, o3)
     first, second = list(zip(*first)), list(zip(*second))
     slab = o2.shape[-1]
@@ -802,8 +799,9 @@
             ((act_in, act), (up_in, up), (dh_in, dh), (unit_in, unit), (dqkv_in, dqkv), (mixed_in, mixed))
         )
     ]
-    for load in loads:
+    for load in loads[:2]:
         load.start()
+    greet([*across, core_peer, *[(s, lax.rem(c + k, 4), h) for k in near]])
 
     smalls = [
         pltpu.make_async_copy(a, b, small_sem.at[i])
@@ -827,6 +825,8 @@
             return pltpu.make_async_copy(wo_in.at[:, at], w_out.at[i % 2], weight_sem.at[i])
         return pltpu.make_async_copy(wq_in.at[:, at, :], w_qkv.at[i % 2], weight_sem.at[i])
 
+    for load in loads[2:]:
+        load.start()
     for i in (0, 4, 1, 5, 6, 7):
         weight_load(i).start()
 
@@ -955,15 +955,20 @@
     def down_grad():
         rows = units // 8
 
-        @pl.loop(0, 4)
-        def _(q):
-            left = act[:, span(q, 2 * rows)]
+        def part_of(y, x):
+            left = act[:, span(2 * y + x, 2 * rows)]
             for j in range(model // 512):
-                part = dot(left, up[:, j * 512 : (j + 1) * 512], (0, 0)).astype(BF16)
+                cols = slice(j * 512, (j + 1) * 512)
+                part = dot(left, up[:, cols], (0, 0)).astype(BF16)
                 for half in (0, 1):
-                    grads[5][0, lax.div(q, 2), lax.rem(q, 2), half, :, j * 512 : (j + 1) * 512] = part[
-                        half * rows : (half + 1) * rows
-                    ]
+                    grads[5][0, y, x, half, :, cols] = part[half * rows : (half + 1) * rows]
+
+        part_of(y_off, x_off)
+        part_of(y_at, x_off)
+        one(5, 0).start()
+        part_of(y_off, x_at)
+        one(5, 1).start()
+        part_of(y_at, x_at)
 
     def out_grad():
         rows = width // 8
@@ -1129,10 +1134,11 @@
             need(0, 1)
             down_grad()
         elif op == "P":
+            need(1)
             parameters()
+            compute_sums()
         elif op == "U":
             need(1, 2, 3)
-            compute_sums()
             for j in range(units // 512):
                 cols = slice(j * 512, (j + 1) * 512)
                 sums[5:6, 3 * width + cols.start : 3 * width + cols.stop] = column_sum(dh, cols)
@@ -1301,7 +1307,7 @@
 
 
 def finish_all(q, u, o, d, joint, inward, own, upstream, small, bias_a, bias_b):
-    steps = 16
+    steps = 8
     arrays = [q, u, o, d, joint, inward, own, upstream]
 
     def spec(a):

time: 408 us -> 381 us (0.934); the launches traced: 403 us -> 381 us
  Pallas kernels: 402 us -> 380 us
    pallas_call x1, Pallas kernels: 158 us -> 145 us  [gather_all(): pl.pallas_call(gather_body, out_shape=[jax.ShapeDtypeStruct(v, BF16) for...]
    pallas_call x1, Pallas kernels: 223 us -> 218 us  [settle_all(): pl.pallas_call(settle_body, out_shape=[jax.ShapeDtypeStruct(v, BF16) for...]
where the time goes in v6:
time: 381 us
  Pallas kernels  380 us (100%)
    pallas_call x1, Pallas kernels, settle_all(): pl.pallas_call(settle_body, out_shape=[jax.ShapeDtypeStruct(v, BF16) for...  218 us
    pallas_call x1, Pallas kernels, gather_all(): pl.pallas_call(gather_body, out_shape=[jax.ShapeDtypeStruct(v, BF16) for...  145 us
    pallas_call x1, Pallas kernels, finish_all(): pl.pallas_call(finish_body, grid=(steps,), out_shape=[jax.ShapeDtypeStruc...  17.2 us

profile of v6, /device:TPU:0, one launch (start us, length us, event | category | flops | bytes accessed | tf_op | source)
XLA Modules:
  0.0 381.0 jit_solution(17541182516949873981)
XLA Ops:
  0.6 144.9 %gather.1 = (bf16[1024,2048]{1,0:T(8,128)(2,1)}, bf16[1024,2048]{1,0:T(8,128)(2,1)}, bf16[1024,1024]{1,0:T(8,128)(2,1)}, bf16[1024,1024]{1,0:T(8,128)(2,1)}, bf1...) custom-call(bf16[256,2048]{1,0:T(8,128)(2,1)} %bitcast.11, ...), custom_call_target="tpu_custom_call" | custom-call | tf_op jit(solution)/shard_map/gather/pallas_call | solution.py:738
  145.6 218.1 %settle.1 = (bf16[256,2048]{1,0:T(8,128)(2,1)}, bf16[256,2048]{1,0:T(8,128)(2,1)}, bf16[3,4,2,64,1024]{4,3,2,1,0:T(8,128)(2,1)}, bf16[4,2,64,4096]{3,2,1,0:T(8,1...) custom-call(bf16[1024,1024]{1,0:T(8,128)(2,1)} %get-tuple-element.45.act_in,, ...), custom_call_target="tpu_custom_call" | custom-call | tf_op jit(solution)/shard_map/settle/pallas_call | solution.py:1261
  363.7 17.2 %finish.1 = (f32[1536,1024]{1,0:T(8,128)}, f32[512,4096]{1,0:T(8,128)}, f32[1024,512]{1,0:T(8,128)}, f32[4096,512]{1,0:T(8,128)}, bf16[256,2048]{1,0:T(8,128)(2,...) custom-call(bf16[1536,1024]{1,0:T(8,128)(2,1)} %bitcast.15, ...), custom_call_target="tpu_custom_call" | custom-call | tf_op jit(solution)/shard_map/finish/pallas_call | solution.py:1323

commit v7 on v6

--- a/solution.py
+++ b/solution.py
@@ -632,13 +632,14 @@
                 line_copy(a, 0, side).start()
 
     def close():
+        give(5).start()
+
         @pl.loop(0, length // tile)
         def _(i):
             at = span(i, tile)
             dqkv[at, width : 2 * width] = turned(key_grad[at, :] * scale, at, -1.0).astype(BF16)
             dqkv[at, 2 * width : 3 * width] = value_grad[at, :].astype(BF16)
 
-        give(5).start()
         give(6).start()
 
     def run(step):
@@ -752,8 +753,8 @@
 
 LEADS = (4, 4, 4, 4, 1, 1)
 BACK_PLAN = (
-    "O", "14", "D", "B0", "24", "B1", "R0", "P", "Q", "12", "25", "Z4", "I0", "22", "11", "U", "13", "10", "I1", "Z5", "X4", "20", "23", "21", "a", "Z0", "Z2", "b", "X5", "X0", "S0", "N4",
-    "Z3", "Z1", "N5", "X3", "X2", "c", "R1", "X1", "N3", "N1", "d", "N0", "N2", "e", "S1",
+    "O", "14", "D", "B0", "24", "B1", "R0", "P", "Q", "11", "12", "25", "Z4", "22", "U", "13", "10", "I0", "I1", "Z5", "X4", "20", "23", "21", "a", "Z0", "Z2", "b", "X5", "X0", "S0", "N4",
+    "Z3", "Z1", "N5", "X3", "c", "X2", "R1", "X1", "N3", "N1", "d", "N0", "N2", "e", "S1",
 )
 def settle_body(
     act_in, up_in, unit_in, dh_in, dqkv_in, mixed_in, wq_in, wu_in, wo_in, wd_in,
@@ -1276,59 +1277,121 @@
 
 
 def finish_body(
-    q_ref, u_ref, o_ref, d_ref, joint_ref, inward_ref, own_ref, up_ref,
-    small_ref, bias_a, bias_b,
+    q_ref, u_ref, o_ref, d_ref, joint_ref, inward_ref, own_ref, up_ref, small_ref, bias_a_ref, bias_b_ref,
     q_out, u_out, o_out, d_out, y_out, g_out, v0, v1, v2, v3, v4, v5, qb_out, ub_out,
+    q_low, u_low, o_low, d_low, q_wide, u_wide, o_wide, d_wide,
+    joint, inward, own, up, small, bias_a, bias_b, y, g, w0, w1, w2, w3, w4, qb, ub,
+    read_sem, write_sem, in_sem, out_sem,
 ):
-    q_out[...] = q_ref[...].astype(F32)
-    u_out[...] = u_ref[...].astype(F32)
-    o_out[...] = o_ref[...].astype(F32)
-    d_out[...] = d_ref[...].astype(F32)
-    wide = own_ref[...].astype(F32)
-    bias = (bias_a[...].astype(F32) + bias_b[...].astype(F32)).reshape(1, wide.shape[1])
-    y_out[...] = (wide + joint_ref[...].astype(F32) + bias).astype(BF16)
-    centred = wide - jnp.mean(wide, axis=-1, keepdims=True)
-    scale = lax.rsqrt(jnp.mean(centred * centred, axis=-1, keepdims=True) + 1e-05)
-    unit = centred * scale
-    inward = inward_ref[...].astype(F32)
-    inward = inward - jnp.mean(inward, axis=-1, keepdims=True) - unit * jnp.mean(inward * unit, axis=-1, keepdims=True)
-    g_out[...] = up_ref[...].astype(F32) + scale * inward
-
-    @pl.when(pl.program_id(0) == 0)
-    def _():
-        for i, out in zip((0, 1, 4, 2, 3, 4), (v0, v1, v2, v3, v4, v5)):
-            out[...] = small_ref[i : i + 1, :].reshape(out.shape)
-        width, units = qb_out.shape[1] // 4, ub_out.shape[0] // 4
+    sources, results = (q_ref, u_ref, o_ref, d_ref), (q_out, u_out, o_out, d_out)
+    lows, wides = (q_low, u_low, o_low, d_low), (q_wide, u_wide, o_wide, d_wide)
+    counts = [src.shape[0] // low.shape[1] for src, low in zip(sources, lows)]
+    order = [(a, n) for n in range(max(counts)) for a in (3, 1, 0, 2) if n < counts[a]]
+
+    def rows(a, n):
+        size = lows[a].shape[1]
+        return slice(n * size, (n + 1) * size)
+
+    def read(a, n):
+        return pltpu.make_async_copy(sources[a].at[rows(a, n), :], lows[a].at[n % 2], read_sem.at[a, n % 2])
+
+    def write(a, n):
+        return pltpu.make_async_copy(wides[a].at[n % 2], results[a].at[rows(a, n), :], write_sem.at[a, n % 2])
+
+    loads = [
+        pltpu.make_async_copy(a, b, in_sem.at[i])
+        for i, (a, b) in enumerate(
+            (
+                (joint_ref, joint), (inward_ref, inward), (own_ref, own), (up_ref, up),
+                (small_ref, small), (bias_a_ref, bias_a), (bias_b_ref, bias_b),
+            )
+        )
+    ]
+    stores = [
+        pltpu.make_async_copy(a, b, out_sem.at[i])
+        for i, (a, b) in enumerate(
+            (
+                (y, y_out), (g, g_out), (w0, v0), (w1, v1), (w4, v2), (w2, v3), (w3, v4), (w4, v5),
+                (qb, qb_out), (ub, ub_out),
+            )
+        )
+    ]
+    for a, n in order:
+        if n < 2:
+            read(a, n).start()
+    for load in loads:
+        load.start()
+
+    def rest():
+        for load in loads:
+            load.wait()
+        for i, out in enumerate((w0, w1, w2, w3, w4)):
+            out[...] = small[i : i + 1, :].reshape(out.shape)
+        width, units = qb.shape[1] // 4, ub.shape[0] // 4
         for i in range(4):
-            row = small_ref[8 + i : 9 + i, :]
+            row = small[8 + i : 9 + i, :]
             for p in range(3):
-                qb_out[p : p + 1, i * width : (i + 1) * width] = row[:, p * width : (p + 1) * width]
-            ub_out[i * units : (i + 1) * units] = row[:, 3 * width : 3 * width + units].reshape(units)
+                qb[p : p + 1, i * width : (i + 1) * width] = row[:, p * width : (p + 1) * width]
+            ub[i * units : (i + 1) * units] = row[:, 3 * width : 3 * width + units].reshape(units)
+        bias = (bias_a[...].astype(F32) + bias_b[...].astype(F32)).reshape(1, own.shape[1])
+        tall = 32
+
+        @pl.loop(0, own.shape[0] // tall)
+        def _(i):
+            at = span(i, tall)
+            wide = own[at, :].astype(F32)
+            y[at, :] = (wide + joint[at, :].astype(F32) + bias).astype(BF16)
+            centred = wide - jnp.mean(wide, axis=-1, keepdims=True)
+            scale = lax.rsqrt(jnp.mean(centred * centred, axis=-1, keepdims=True) + 1e-05)
+            unit = centred * scale
+            back = inward[at, :].astype(F32)
+            back = back - jnp.mean(back, axis=-1, keepdims=True) - unit * jnp.mean(back * unit, axis=-1, keepdims=True)
+            g[at, :] = up[at, :].astype(F32) + scale * back
+
+        for store in stores:
+            store.start()
+
+    for i, (a, n) in enumerate(order):
+        read(a, n).wait()
+        if n >= 2:
+            write(a, n - 2).wait()
+        wides[a][n % 2] = lows[a][n % 2].astype(F32)
+        write(a, n).start()
+        if n + 2 < counts[a]:
+            read(a, n + 2).start()
+        if i == len(order) // 2:
+            rest()
+    for a in range(4):
+        for n in range(max(0, counts[a] - 2), counts[a]):
+            write(a, n).wait()
+    for store in stores:
+        store.wait()
 
 
 def finish_all(q, u, o, d, joint, inward, own, upstream, small, bias_a, bias_b):
-    steps = 8
-    arrays = [q, u, o, d, joint, inward, own, upstream]
-
-    def spec(a):
-        return pl.BlockSpec((a.shape[0] // steps, a.shape[1]), lambda i: (i, 0))
-
-    results = [(a.shape, F32) for a in (q, u, o, d)] + [(own.shape, BF16), (own.shape, F32)]
-    smalls = [(own.shape[1:], F32)] * 6 + [((3, q.shape[1]), F32), (u.shape[1:], F32)]
-    results += smalls
-
-    def whole(shape):
-        return pl.BlockSpec(shape, lambda i: (0,) * len(shape))
-
+    arrays = [q, u, o, d, joint, inward, own, upstream, small, bias_a, bias_b]
+    grads = (q, u, o, d)
+    tall = (q.shape[0] // 6, u.shape[0] // 8, o.shape[0] // 2, d.shape[0] // 8)
+    vector, qb, ub = own.shape[1:], (3, q.shape[1]), u.shape[1:]
+    results = [(a.shape, F32) for a in grads] + [(own.shape, BF16), (own.shape, F32)]
+    results += [(vector, F32)] * 6 + [(qb, F32), (ub, F32)]
+    scratch = [pltpu.VMEM((2, t, a.shape[1]), k) for k in (BF16, F32) for t, a in zip(tall, grads)]
+    scratch += [pltpu.VMEM(own.shape, BF16)] * 4
+    scratch += [pltpu.VMEM(small.shape, F32), pltpu.VMEM(vector, BF16), pltpu.VMEM(vector, BF16)]
+    scratch += [pltpu.VMEM(own.shape, BF16), pltpu.VMEM(own.shape, F32)]
+    scratch += [pltpu.VMEM(v, F32) for v in [vector] * 5 + [qb, ub]]
+    dma = pltpu.SemaphoreType.DMA
+    scratch += [dma((4, 2)), dma((4, 2)), dma((7,)), dma((10,))]
+    any_space = pl.BlockSpec(memory_space=pl.ANY)
     return pl.pallas_call(
         finish_body,
-        grid=(steps,),
         out_shape=[jax.ShapeDtypeStruct(v, t) for v, t in results],
-        in_specs=[spec(a) for a in arrays] + [whole(v.shape) for v in (small, bias_a, bias_b)],
-        out_specs=[spec(a) for a in (q, u, o, d, own, own)] + [whole(v) for v, _ in smalls],
+        in_specs=[any_space] * len(arrays),
+        out_specs=[any_space] * len(results),
+        scratch_shapes=scratch,
         compiler_params=pltpu.CompilerParams(vmem_limit_bytes=63 << 20),
         name="finish",
-    )(*arrays, small, bias_a, bias_b)
+    )(*arrays)
 
 
 def per_device(

time: 381 us -> 387 us (1.016); the launches traced: 381 us -> 380 us
  no operation moved by 1% of the time
where the time goes in v7:
time: 387 us; the launch traced here: 380 us
  Pallas kernels  378 us (98%)
    pallas_call x1, Pallas kernels, settle_all(): pl.pallas_call(settle_body, out_shape=[jax.ShapeDtypeStruct(v, BF16) for...  218 us
    pallas_call x1, Pallas kernels, gather_all(): pl.pallas_call(gather_body, out_shape=[jax.ShapeDtypeStruct(v, BF16) for...  144 us
    pallas_call x1, Pallas kernels, finish_all(): pl.pallas_call(finish_body, out_shape=[jax.ShapeDtypeStruct(v, t) for v,...  15.9 us

profile of v7, /device:TPU:0, one launch (start us, length us, event | category | flops | bytes accessed | tf_op | source)
XLA Modules:
  0.0 379.5 jit_solution(1125116378777263077)
XLA Ops:
  0.6 144.4 %gather.1 = (bf16[1024,2048]{1,0:T(8,128)(2,1)}, bf16[1024,2048]{1,0:T(8,128)(2,1)}, bf16[1024,1024]{1,0:T(8,128)(2,1)}, bf16[1024,1024]{1,0:T(8,128)(2,1)}, bf1...) custom-call(bf16[256,2048]{1,0:T(8,128)(2,1)} %bitcast.11, ...), custom_call_target="tpu_custom_call" | custom-call | tf_op jit(solution)/shard_map/gather/pallas_call | solution.py:739
  145.1 218.1 %settle.1 = (bf16[256,2048]{1,0:T(8,128)(2,1)}, bf16[256,2048]{1,0:T(8,128)(2,1)}, bf16[3,4,2,64,1024]{4,3,2,1,0:T(8,128)(2,1)}, bf16[4,2,64,4096]{3,2,1,0:T(8,1...) custom-call(bf16[1024,1024]{1,0:T(8,128)(2,1)} %get-tuple-element.45.act_in,, ...), custom_call_target="tpu_custom_call" | custom-call | tf_op jit(solution)/shard_map/settle/pallas_call | solution.py:1262
  363.2 15.9 %finish.1 = (f32[1536,1024]{1,0:T(8,128)}, f32[512,4096]{1,0:T(8,128)}, f32[1024,512]{1,0:T(8,128)}, f32[4096,512]{1,0:T(8,128)}, bf16[256,2048]{1,0:T(8,128)(2,...) custom-call(bf16[1536,1024]{1,0:T(8,128)(2,1)} %bitcast.15, ...), custom_call_target="tpu_custom_call" | custom-call | tf_op jit(solution)/shard_map/finish/pallas_call | solution.py:1386

commit v8 on v6

--- a/solution.py
+++ b/solution.py
@@ -632,13 +632,14 @@
                 line_copy(a, 0, side).start()
 
     def close():
+        give(5).start()
+
         @pl.loop(0, length // tile)
         def _(i):
             at = span(i, tile)
             dqkv[at, width : 2 * width] = turned(key_grad[at, :] * scale, at, -1.0).astype(BF16)
             dqkv[at, 2 * width : 3 * width] = value_grad[at, :].astype(BF16)
 
-        give(5).start()
         give(6).start()
 
     def run(step):
@@ -752,8 +753,8 @@
 
 LEADS = (4, 4, 4, 4, 1, 1)
 BACK_PLAN = (
-    "O", "14", "D", "B0", "24", "B1", "R0", "P", "Q", "12", "25", "Z4", "I0", "22", "11", "U", "13", "10", "I1", "Z5", "X4", "20", "23", "21", "a", "Z0", "Z2", "b", "X5", "X0", "S0", "N4",
-    "Z3", "Z1", "N5", "X3", "X2", "c", "R1", "X1", "N3", "N1", "d", "N0", "N2", "e", "S1",
+    "O", "14", "D", "B0", "24", "B1", "R0", "P", "Q", "11", "12", "25", "Z4", "22", "U", "13", "10", "I0", "I1", "Z5", "X4", "20", "23", "21", "a", "Z0", "Z2", "b", "X5", "X0", "S0", "N4",
+    "Z3", "Z1", "N5", "X3", "c", "X2", "R1", "X1", "N3", "N1", "d", "N0", "N2", "e", "S1",
 )
 def settle_body(
     act_in, up_in, unit_in, dh_in, dqkv_in, mixed_in, wq_in, wu_in, wo_in, wd_in,

time: 381 us -> 381 us (level)
  no operation moved by 1% of the time
where the time goes in v8:
time: 381 us
  Pallas kernels  380 us (100%)
    pallas_call x1, Pallas kernels, settle_all(): pl.pallas_call(settle_body, out_shape=[jax.ShapeDtypeStruct(v, BF16) for...  218 us
    pallas_call x1, Pallas kernels, gather_all(): pl.pallas_call(gather_body, out_shape=[jax.ShapeDtypeStruct(v, BF16) for...  144 us
    pallas_call x1, Pallas kernels, finish_all(): pl.pallas_call(finish_body, grid=(steps,), out_shape=[jax.ShapeDtypeStruc...  17.2 us

profile of v8, /device:TPU:0, one launch (start us, length us, event | category | flops | bytes accessed | tf_op | source)
XLA Modules:
  0.0 380.5 jit_solution(7716491478046767733)
XLA Ops:
  0.6 144.4 %gather.1 = (bf16[1024,2048]{1,0:T(8,128)(2,1)}, bf16[1024,2048]{1,0:T(8,128)(2,1)}, bf16[1024,1024]{1,0:T(8,128)(2,1)}, bf16[1024,1024]{1,0:T(8,128)(2,1)}, bf1...) custom-call(bf16[256,2048]{1,0:T(8,128)(2,1)} %bitcast.11, ...), custom_call_target="tpu_custom_call" | custom-call | tf_op jit(solution)/shard_map/gather/pallas_call | solution.py:739
  145.1 218.1 %settle.1 = (bf16[256,2048]{1,0:T(8,128)(2,1)}, bf16[256,2048]{1,0:T(8,128)(2,1)}, bf16[3,4,2,64,1024]{4,3,2,1,0:T(8,128)(2,1)}, bf16[4,2,64,4096]{3,2,1,0:T(8,1...) custom-call(bf16[1024,1024]{1,0:T(8,128)(2,1)} %get-tuple-element.45.act_in,, ...), custom_call_target="tpu_custom_call" | custom-call | tf_op jit(solution)/shard_map/settle/pallas_call | solution.py:1262
  363.2 17.2 %finish.1 = (f32[1536,1024]{1,0:T(8,128)}, f32[512,4096]{1,0:T(8,128)}, f32[1024,512]{1,0:T(8,128)}, f32[4096,512]{1,0:T(8,128)}, bf16[256,2048]{1,0:T(8,128)(2,...) custom-call(bf16[1536,1024]{1,0:T(8,128)(2,1)} %bitcast.15, ...), custom_call_target="tpu_custom_call" | custom-call | tf_op jit(solution)/shard_map/finish/pallas_call | solution.py:1324
